TPU v7x, 128 devices: a whole 4x4x4 slice. The times are simulated.
128 devices in a mesh: outer: 16 (over x, z_hi, core), inner: 8 (over y, z_lo).
Axes of the slice: x: 4, y: 4, z: 4 (z_hi: 2, z_lo: 2; z = z_hi * 2 + z_lo), core: 2. Of those that a mesh axis runs over, the one named last changes fastest.
Arguments:
- tokens: bfloat16 [32768, 2048], P(('outer', 'inner')), may hold values from -16 to 16
- qkv_weight: bfloat16 [2048, 6144], P(None, 'inner'), may hold values from -1 to 1, as said below
- offsets: int32 [16], replicated, may hold values from 0 to 127
Outputs:
- attended: bfloat16 [32768, 2048], P(('outer', 'inner'))
Inputs may be any that keep to these rules, and one draw needn't show every extreme that they name: `qkv_weight`: projection entries scaled by the inverse square root of 2048.
All inputs are finite; a program needn't handle non-finite values.
Results may differ from a plain program's by a relative error of at most 0.0067.
Values may be sent and summed in bfloat16 or wider, within the bound.
No kernel may reach another device: no remote copies, remote signals or barrier semaphores. Data moves between devices by JAX's collectives and lax.ppermute only.
A program may use at most 128 MiB of HBM per device.

v0:
```python
import math

import jax
import jax.numpy as jnp
from jax import lax
from jax.sharding import PartitionSpec as P

HEADS = 16
DH = 128


def swapped(value, axis, stride):
    return lax.ppermute(value, axis, [(i, i ^ 1 << stride) for i in range(lax.axis_size(axis))])


def select_half(source, parity):
    row_count = source.shape[0]
    paired = source.reshape((row_count // 2, 2) + source.shape[1:])
    view_shape = (1, source.shape[1]) + (1,) * (source.ndim - 2)
    chooser = parity.reshape(view_shape) == 0
    return jnp.where(chooser, paired[:, 0], paired[:, 1])


def attend(queries, keys_values, inv_root):
    head_size = queries.shape[2]
    key_part = keys_values[:, :, :head_size]
    value_part = keys_values[:, :, head_size:]
    raw_scores = jnp.einsum("qhd,khd->hqk", queries, key_part, preferred_element_type=jnp.float32)
    scores = raw_scores * inv_root
    row_top = jnp.max(scores, axis=2)
    exponent = jnp.exp(scores - row_top[:, :, None])
    row_total = jnp.sum(exponent, axis=2)
    row_mixed = jnp.einsum(
        "hqk,khd->hqd",
        exponent.astype(jnp.bfloat16),
        value_part,
        preferred_element_type=jnp.float32,
    )
    return (row_top, row_total, row_mixed)


def fold_level(finer, coarser, parity):
    fine_top, fine_total, fine_mixed = finer
    coarse_top, coarse_total, coarse_mixed = coarser
    head_count, row_count = fine_top.shape
    chosen = jnp.arange(2, dtype=jnp.int32)[None, None, :] == parity[:, None, None]
    pair_top = fine_top.reshape(head_count, row_count // 2, 2)
    pair_total = fine_total.reshape(head_count, row_count // 2, 2)
    pair_mixed = fine_mixed.reshape(head_count, row_count // 2, 2, -1)
    merged_top = jnp.where(chosen, jnp.maximum(pair_top, coarse_top[:, :, None]), pair_top)
    fine_scale = jnp.exp(pair_top - merged_top)
    coarse_scale = jnp.where(chosen, jnp.exp(coarse_top[:, :, None] - merged_top), 0.0)
    new_total = pair_total * fine_scale + coarse_total[:, :, None] * coarse_scale
    new_mixed = (
        pair_mixed * fine_scale[:, :, :, None]
        + coarse_mixed[:, :, None, :] * coarse_scale[:, :, :, None]
    )
    return (
        merged_top.reshape(head_count, row_count),
        new_total.reshape(head_count, row_count),
        new_mixed.reshape(head_count, row_count, -1),
    )


def shards(tokens, qkv_weight, offsets):
    tok_rows = tokens.shape[0]
    projected = jnp.dot(
        tokens,
        lax.all_gather(qkv_weight, "inner", axis=1, tiled=True),
        preferred_element_type=jnp.float32,
    ).astype(jnp.bfloat16)
    sections = projected.reshape(tok_rows, HEADS, 3, DH)
    queries = sections[:, :, 0]
    buffer = sections[:, :, 1:].reshape(tok_rows, HEADS, 2 * DH)
    inv_root = 1.0 / math.sqrt(DH)
    states = [attend(queries, buffer, inv_root)]
    inner_bits = lax.axis_size("inner").bit_length() - 1
    levels = inner_bits + lax.axis_size("outer").bit_length() - 1
    for level_index in range(levels):
        parity = offsets // 2**level_index % 2
        queries = select_half(queries, parity)
        kept_rows = select_half(buffer, parity)
        if level_index < inner_bits:
            partner = swapped(kept_rows, "inner", level_index)
        else:
            partner = swapped(kept_rows, "outer", level_index - inner_bits)
        buffer = jnp.concatenate([kept_rows, partner], axis=0)
        states.append(attend(queries, buffer, inv_root))
    combined = states[levels]
    for level_index in reversed(range(levels)):
        parity = offsets // 2**level_index % 2
        combined = fold_level(states[level_index], combined, parity)
    final_top, final_total, final_mixed = combined
    result = (final_mixed / final_total[:, :, None]).astype(jnp.bfloat16)
    return jnp.transpose(result, (1, 0, 2)).reshape(tok_rows, HEADS * DH)


def solution(mesh):
    placed = (P(("outer", "inner"), None), P(None, "inner"), P())
    return jax.shard_map(
        shards, mesh=mesh, in_specs=placed, out_specs=P(("outer", "inner"), None), check_vma=False
    )
```

profile of v0, /device:TPU:0, one launch (start us, length us, event | category | flops | bytes accessed | tf_op | source)
XLA Modules:
  0.0 814.9 jit_solution(15751359835600641045)
XLA Ops:
  10.6 483.9 %all-gather.2.cloned.1.call-done = bf16[2048,6144]{1,0:T(8,128)(2,1)} async-done(((bf16[2048,768]{1,0:T(8,128)(2,1)}), bf16[2048,6144]{1,0:T(8,128)(2,1)}) %all-gather.2.cloned.1.call-update) | async-done | bytes 25165840 | tf_op jit(solution)/shard_map/all_gather | solution.py:69
  494.5 12.8 %convolution_convert_fusion = bf16[256,6144]{1,0:T(8,128)(2,1)} fusion(bf16[256,2048]{1,0:T(8,128)(2,1)S(1)} %copy-done, bf16[2048,6144]{1,0:T(8,128)(2,1)} %all-gather.2.cloned.1.call-done), kind=kOutput, calls=%fused_computation | convolution fusion | flops 6444023808 | bytes 29360128 | tf_op jit(solution)/shard_map/dot_general | solution.py:67
  507.4 4.6 copy.94
  513.7 4.4 copy.101
  518.1 4.4 reshape_reshape.3
  536.1 14.2 %collective-permute-done = bf16[128,16,256]{2,0,1:T(8,128)(2,1)S(1)} collective-permute-done((bf16[128,16,256]{2,0,1:T(8,128)(2,1)S(1)}, bf16[128,16,256]{2,0,1:T(8,128)(2,1)S(1)}, u32[]{:S(2)}, u32[]{:S(2)}) %collective-permute-start) | collective-permute-done | bytes 1048608 | tf_op jit(solution)/shard_map/ppermute | solution.py:13
  552.9 2.7 reshape.873
  555.7 3.0 fusion.126
  561.9 21.5 %collective-permute-done.1 = bf16[128,16,256]{2,0,1:T(8,128)(2,1)S(1)} collective-permute-done((bf16[128,16,256]{2,0,1:T(8,128)(2,1)S(1)}, bf16[128,16,256]{2,0,1:T(8,128)(2,1)S(1)}, u32[]{:S(2)}, u32[]{:S(2)}) %collective-permute-start.1) | collective-permute-done | bytes 1048608 | tf_op jit(solution)/shard_map/ppermute | solution.py:13
  588.8 3.0 fusion.125
  592.1 3.3 collective-permute-start.2
  596.8 20.3 %collective-permute-done.2 = bf16[128,16,256]{2,0,1:T(8,128)(2,1)S(1)} collective-permute-done((bf16[128,16,256]{2,0,1:T(8,128)(2,1)S(1)}, bf16[128,16,256]{2,0,1:T(8,128)(2,1)S(1)}, u32[]{:S(2)}, u32[]{:S(2)}) %collective-permute-start.2) | collective-permute-done | bytes 1048608 | tf_op jit(solution)/shard_map/ppermute | solution.py:13
  622.4 3.0 fusion.124
  635.7 3.0 fusion.123
  639.0 2.9 collective-permute-start.4
  646.8 19.1 %collective-permute-done.4 = bf16[128,16,256]{2,0,1:T(8,128)(2,1)S(1)} collective-permute-done((bf16[128,16,256]{2,0,1:T(8,128)(2,1)S(1)}, bf16[128,16,256]{2,0,1:T(8,128)(2,1)S(1)}, u32[]{:S(2)}, u32[]{:S(2)}) %collective-permute-start.4) | collective-permute-done | bytes 1048608 | tf_op jit(solution)/shard_map/ppermute | solution.py:13
  671.1 3.0 fusion.122
  682.1 17.0 %collective-permute-done.5 = bf16[128,16,256]{2,0,1:T(8,128)(2,1)S(1)} collective-permute-done((bf16[128,16,256]{2,0,1:T(8,128)(2,1)S(1)}, bf16[128,16,256]{2,0,1:T(8,128)(2,1)S(1)}, u32[]{:S(2)}, u32[]{:S(2)}) %collective-permute-start.5) | collective-permute-done | bytes 1048608 | tf_op jit(solution)/shard_map/ppermute | solution.py:13
  701.7 4.1 reshape.878
  705.8 5.7 fusion.121
  711.8 3.1 collective-permute-start.6
  720.1 16.8 %collective-permute-done.6 = bf16[128,16,256]{2,0,1:T(8,128)(2,1)S(1)} collective-permute-done((bf16[128,16,256]{2,0,1:T(8,128)(2,1)S(1)}, bf16[128,16,256]{2,0,1:T(8,128)(2,1)S(1)}, u32[]{:S(2)}, u32[]{:S(2)}) %collective-permute-start.6) | collective-permute-done | bytes 1048608 | tf_op jit(solution)/shard_map/ppermute | solution.py:13
  797.1 3.1 copy.165
  800.8 5.0 divide_convert_fusion
  (348 shorter events, 136.4 us)
Async XLA Ops:
  6.5 488.0 %copy-start = (bf16[256,2048]{1,0:T(8,128)(2,1)S(1)}, bf16[256,2048]{1,0:T(8,128)(2,1)}, u32[]{:S(2)}) copy-start(bf16[256,2048]{1,0:T(8,128)(2,1)} %param.3) | copy-start | bytes 3145732
  6.5 488.0 %all-gather.2.cloned.1.call-start = ((), (), s32[]{:S(2)}) async-start(), calls=%async_computation | async-start | bytes 28311552 | tf_op jit(solution)/shard_map/all_gather | solution.py:69
  7.8 553.3 %copy-start.93 = (pred[16]{0:T(512)(128)(4,1)}, pred[16]{0:T(512)(128)(4,1)S(1)}, u32[]{:S(2)}) copy-start(pred[16]{0:T(512)(128)(4,1)S(1)} %get-tuple-element.81) | copy-start | bytes 52
  7.8 584.0 %copy-start.90 = (pred[16]{0:T(512)(128)(4,1)}, pred[16]{0:T(512)(128)(4,1)S(1)}, u32[]{:S(2)}) copy-start(pred[16]{0:T(512)(128)(4,1)S(1)} %get-tuple-element.75) | copy-start | bytes 52
  7.8 587.7 %copy-start.87 = (pred[16]{0:T(512)(128)(4,1)}, pred[16]{0:T(512)(128)(4,1)S(1)}, u32[]{:S(2)}) copy-start(pred[16]{0:T(512)(128)(4,1)S(1)} %get-tuple-element.83) | copy-start | bytes 52
  7.8 617.6 %copy-start.92 = (pred[16]{0:T(512)(128)(4,1)}, pred[16]{0:T(512)(128)(4,1)S(1)}, u32[]{:S(2)}) copy-start(pred[16]{0:T(512)(128)(4,1)S(1)} %get-tuple-element.77) | copy-start | bytes 52
  7.8 618.0 %copy-start.85 = (pred[16]{0:T(512)(128)(4,1)}, pred[16]{0:T(512)(128)(4,1)S(1)}, u32[]{:S(2)}) copy-start(pred[16]{0:T(512)(128)(4,1)S(1)} %get-tuple-element.79) | copy-start | bytes 52
  525.4 25.0 %collective-permute-start = (bf16[128,16,256]{2,0,1:T(8,128)(2,1)S(1)}, bf16[128,16,256]{2,0,1:T(8,128)(2,1)S(1)}, u32[]{:S(2)}, u32[]{:S(2)}) collective-permute-start(bf16[128,16,256]{2,0,1:T(8,128)(2,1)S(1)} %fusion.56), channel_id=1, source_target_pairs={{0,1},{1,0},{2,3},{3,2},{4,5},{5,4},{6,7},{7,6},{8,9},{9,8},{10,11... | collective-permute-start | bytes 3145736 | tf_op jit(solution)/shard_map/ppermute | solution.py:13
  559.0 24.5 %copy-start.3 = (bf16[128,16,256]{2,0,1:T(8,128)(2,1)}, bf16[128,16,256]{2,0,1:T(8,128)(2,1)S(1)}, u32[]{:S(2)}) copy-start(bf16[128,16,256]{2,0,1:T(8,128)(2,1)S(1)} %fusion.55) | copy-start | bytes 3145732
  559.0 24.5 %collective-permute-start.1 = (bf16[128,16,256]{2,0,1:T(8,128)(2,1)S(1)}, bf16[128,16,256]{2,0,1:T(8,128)(2,1)S(1)}, u32[]{:S(2)}, u32[]{:S(2)}) collective-permute-start(bf16[128,16,256]{2,0,1:T(8,128)(2,1)S(1)} %fusion.55), channel_id=1, source_target_pairs={{0,2},{1,3},{2,0},{3,1},{4,6},{5,7},{6,4},{7,5},{8,10},{9,11},{10,... | collective-permute-start | bytes 3145736 | tf_op jit(solution)/shard_map/ppermute | solution.py:13
  592.1 25.0 %copy-start.20 = (bf16[128,16,256]{2,0,1:T(8,128)(2,1)}, bf16[128,16,256]{2,0,1:T(8,128)(2,1)S(1)}, u32[]{:S(2)}) copy-start(bf16[128,16,256]{2,0,1:T(8,128)(2,1)S(1)} %fusion.54) | copy-start | bytes 3145732
  592.1 25.0 %collective-permute-start.2 = (bf16[128,16,256]{2,0,1:T(8,128)(2,1)S(1)}, bf16[128,16,256]{2,0,1:T(8,128)(2,1)S(1)}, u32[]{:S(2)}, u32[]{:S(2)}) collective-permute-start(bf16[128,16,256]{2,0,1:T(8,128)(2,1)S(1)} %fusion.54), channel_id=1, source_target_pairs={{0,4},{1,5},{2,6},{3,7},{4,0},{5,1},{6,2},{7,3},{8,12},{9,13},{10,... | collective-permute-start | bytes 3145736 | tf_op jit(solution)/shard_map/ppermute | solution.py:13
  625.7 4.6 collective-permute-start.3
  639.0 26.8 %copy-start.26 = (bf16[128,16,256]{2,0,1:T(8,128)(2,1)}, bf16[128,16,256]{2,0,1:T(8,128)(2,1)S(1)}, u32[]{:S(2)}) copy-start(bf16[128,16,256]{2,0,1:T(8,128)(2,1)S(1)} %fusion.52) | copy-start | bytes 3145732
  639.0 26.8 %collective-permute-start.4 = (bf16[128,16,256]{2,0,1:T(8,128)(2,1)S(1)}, bf16[128,16,256]{2,0,1:T(8,128)(2,1)S(1)}, u32[]{:S(2)}, u32[]{:S(2)}) collective-permute-start(bf16[128,16,256]{2,0,1:T(8,128)(2,1)S(1)} %fusion.52), channel_id=1, source_target_pairs={{0,16},{8,24},{16,0},{24,8},{32,48},{40,56},{48,32},{56,40},{64,80... | collective-permute-start | bytes 3145736 | tf_op jit(solution)/shard_map/ppermute | solution.py:13
  674.4 24.7 %copy-start.29 = (bf16[128,16,256]{2,0,1:T(8,128)(2,1)}, bf16[128,16,256]{2,0,1:T(8,128)(2,1)S(1)}, u32[]{:S(2)}) copy-start(bf16[128,16,256]{2,0,1:T(8,128)(2,1)S(1)} %fusion.51) | copy-start | bytes 3145732
  674.4 24.7 %collective-permute-start.5 = (bf16[128,16,256]{2,0,1:T(8,128)(2,1)S(1)}, bf16[128,16,256]{2,0,1:T(8,128)(2,1)S(1)}, u32[]{:S(2)}, u32[]{:S(2)}) collective-permute-start(bf16[128,16,256]{2,0,1:T(8,128)(2,1)S(1)} %fusion.51), channel_id=1, source_target_pairs={{0,32},{8,40},{16,48},{24,56},{32,0},{40,8},{48,16},{56,24},{64,96... | collective-permute-start | bytes 3145736 | tf_op jit(solution)/shard_map/ppermute | solution.py:13
  711.8 25.1 %copy-start.19 = (bf16[128,16,256]{2,0,1:T(8,128)(2,1)}, bf16[128,16,256]{2,0,1:T(8,128)(2,1)S(1)}, u32[]{:S(2)}) copy-start(bf16[128,16,256]{2,0,1:T(8,128)(2,1)S(1)} %fusion.50) | copy-start | bytes 3145732
  711.8 5.2 copy-start.27
  711.8 25.1 %collective-permute-start.6 = (bf16[128,16,256]{2,0,1:T(8,128)(2,1)S(1)}, bf16[128,16,256]{2,0,1:T(8,128)(2,1)S(1)}, u32[]{:S(2)}, u32[]{:S(2)}) collective-permute-start(bf16[128,16,256]{2,0,1:T(8,128)(2,1)S(1)} %fusion.50), channel_id=1, source_target_pairs={{0,64},{8,72},{16,80},{24,88},{32,96},{40,104},{48,112},{56,120},{... | collective-permute-start | bytes 3145736 | tf_op jit(solution)/shard_map/ppermute | solution.py:13
  717.1 19.9 %copy-start.84 = (bf16[2,16,128]{2,1,0:T(8,128)(2,1)S(1)}, bf16[2,16,128]{2,1,0:T(8,128)(2,1)}, u32[]{:S(2)}) copy-start(bf16[2,16,128]{2,1,0:T(8,128)(2,1)} %fusion.94) | copy-start | bytes 24580
  717.5 19.9 %copy-start.54 = (f32[16,8,256]{2,1,0:T(8,128)}, f32[16,8,256]{2,1,0:T(8,128)S(1)}, u32[]{:S(2)}) copy-start(f32[16,8,256]{2,1,0:T(8,128)S(1)} %get-tuple-element.92) | copy-start | bytes 393220
  719.4 56.0 %copy-start.59 = (f32[16,4,256]{2,1,0:T(4,128)}, f32[16,4,256]{2,1,0:T(4,128)S(1)}, u32[]{:S(2)}) copy-start(f32[16,4,256]{2,1,0:T(4,128)S(1)} %get-tuple-element.90) | copy-start | bytes 196612
  800.8 7.3 copy-start.1
  (81 other events, 190.8 us)
Sparse Core Ops, SparseCore 0:
  9.0 485.4 all-gather.1
where the time goes:
time: 817 us; the launch traced here: 815 us
  waiting for transfers between devices  594 us (73%)
  local copies, waits for them, and re-layouts  127 us (16%)
  other arithmetic  36.9 us (5%)
  matrix products  29.5 us (4%)
  between operations  14.5 us (2%)
  starting transfers between devices  13.5 us (2%)
    all_gather x1, waiting for transfers between devices, shards(): lax.all_gather(qkv_weight, 'inner', axis=1, tiled=True)  484 us
    ppermute x7, waiting for transfers between devices, swapped(): lax.ppermute(value, axis, [(i, i ^ 1 << stride) for i in range(lax.axis_s...  109 us
    slice x13, local copies, waits for them, and re-layouts, select_half(): return jnp.where(chooser, paired[:, 0], paired[:, 1])  24.9 us
    reshape x6, local copies, waits for them, and re-layouts, select_half(): paired = source.reshape((row_count // 2, 2) + source.shape[1:])  17.8 us
  transfers between devices with their start and end apart: 8, of which 7 were waited for; matrix products, arithmetic and copies ran while one was open for 4% of the time, Pallas kernels for 0%

commit v1 on v0

v1 whole, which is shorter than its diff:
```python
import math

import jax
import jax.numpy as jnp
from jax import lax
from jax.experimental import pallas as pl
from jax.experimental.pallas import tpu as pltpu
from jax.sharding import PartitionSpec as P


HEADS = 16
DH = 128
ROWS = 256
DEEP = 32
SLABS = 4
SLOTS = 4
BF = jnp.bfloat16
F32 = jnp.float32
VMEM_BYTES = 56 * 1024 * 1024


def flipped(value, o_mask, i_mask):
    inner = lax.axis_size("inner")
    count = inner * lax.axis_size("outer")
    mask = o_mask * inner + i_mask
    return lax.ppermute(value, ("outer", "inner"), [(f, f ^ mask) for f in range(count)])


def head_of(place_ref, m, slot):
    shard = place_ref[0] ^ m ^ (6 * (slot >> 1))
    return 2 * shard + ((slot & 1) ^ place_ref[1])


def position_of(row, offset):
    index = row >> 1
    reverse = jnp.zeros_like(index)
    for bit in range(7):
        reverse = reverse | (((index >> bit) & 1) << (6 - bit))
    return ((row & 1) << 7) | (reverse ^ (offset & 127))


def to_order(offset):
    row = lax.broadcasted_iota(jnp.int32, (ROWS, ROWS), 0)
    column = lax.broadcasted_iota(jnp.int32, (ROWS, ROWS), 1)
    return jnp.where(position_of(row, offset) == column, 1.0, 0.0).astype(BF)


def from_order(offset, count):
    row = lax.broadcasted_iota(jnp.int32, (ROWS, count), 0)
    column = lax.broadcasted_iota(jnp.int32, (ROWS, count), 1)
    return jnp.where(position_of(column, offset) == row, 1.0, 0.0).astype(BF)


def project_body(base, place_ref, offsets_ref, x0, x1, x2, x3, w_ref, *rest):
    qkv_ref, deep_q_ref, deep_kv_ref, spread = rest[-4:]
    offset = offsets_ref[head_of(place_ref, 0, base + pl.program_id(0))]
    order = to_order(offset)
    for m, x_ref in enumerate((x0, x1, x2, x3)):
        rows = jnp.dot(x_ref[...], w_ref[...], preferred_element_type=F32).astype(BF)
        rows = jnp.dot(order, rows, preferred_element_type=F32)
        qkv_ref[0, m] = rows.astype(BF)
        for part in range(3):
            spread[part, pl.ds(m, DEEP, stride=SLABS), :] = rows[:DEEP, part * DH : (part + 1) * DH]
    deep_q_ref[0] = spread[0].astype(BF)
    deep_kv_ref[0, :, :DH] = spread[1].astype(BF)
    deep_kv_ref[0, :, DH:] = spread[2].astype(BF)


def project(place, offsets, slabs, weight, base, heads, core_order, carried):
    shapes = (
        jax.ShapeDtypeStruct((SLOTS, SLABS, ROWS, 3 * DH), BF),
        jax.ShapeDtypeStruct((SLOTS, SLABS * DEEP, DH), BF),
        jax.ShapeDtypeStruct((SLOTS, SLABS * DEEP, 2 * DH), BF),
    )
    depth = weight.shape[0]

    def weight_block(j, place_ref, offsets_ref):
        return (0, place_ref[1] ^ j if core_order else j)

    carried = () if carried is None else tuple(carried)
    return pl.pallas_call(
        lambda *refs: project_body(base, *refs),
        out_shape=shapes,
        grid_spec=pltpu.PrefetchScalarGridSpec(
            num_scalar_prefetch=2,
            grid=(heads,),
            in_specs=[pl.BlockSpec((ROWS, depth), lambda j, *_: (0, 0)) for _ in slabs]
            + [pl.BlockSpec((depth, 3 * DH), weight_block)]
            + [pl.BlockSpec(memory_space=pl.ANY) for _ in carried],
            out_specs=[
                pl.BlockSpec((1, SLABS, ROWS, 3 * DH), lambda j, *_: (base + j, 0, 0, 0)),
                pl.BlockSpec((1, SLABS * DEEP, DH), lambda j, *_: (base + j, 0, 0)),
                pl.BlockSpec((1, SLABS * DEEP, 2 * DH), lambda j, *_: (base + j, 0, 0)),
            ],
            scratch_shapes=[pltpu.VMEM((3, SLABS * DEEP, DH), F32)],
        ),
        input_output_aliases={7 + k: k for k in range(len(carried))},
        compiler_params=pltpu.CompilerParams(vmem_limit_bytes=VMEM_BYTES),
        cost_estimate=pl.CostEstimate(
            flops=heads * SLABS * 2 * ROWS * 3 * DH * (depth + ROWS),
            bytes_accessed=SLABS * ROWS * depth * 2 + heads * depth * 3 * DH * 2,
            transcendentals=0,
        ),
        name="project",
    )(place, offsets, *slabs, weight, *carried)


def attend(q, k, v):
    scores = lax.dot_general(q, k, (((1,), (1,)), ((), ())), preferred_element_type=F32)
    scores = scores * (1.0 / math.sqrt(DH))
    top = jnp.max(scores, axis=1, keepdims=True)
    exponent = jnp.exp(scores - top)
    total = jnp.sum(exponent, axis=1, keepdims=True)
    mixed = jnp.dot(exponent.astype(BF), v, preferred_element_type=F32)
    return top, total, mixed


def merge(fine, coarse):
    top = jnp.maximum(fine[0], coarse[0])
    fine_scale = jnp.exp(fine[0] - top)
    coarse_scale = jnp.exp(coarse[0] - top)
    return (
        top,
        fine[1] * fine_scale + coarse[1] * coarse_scale,
        fine[2] * fine_scale + coarse[2] * coarse_scale,
    )


def near_body(place_ref, offsets_ref, qkv_ref, u0, u1, u2, u3, state_ref):
    offset = offsets_ref[head_of(place_ref, 0, pl.program_id(0))]
    back = from_order(offset, ROWS)

    def rows_of(members, count):
        parts = []
        for part in range(3):
            pieces = [qkv_ref[0, m, :count, part * DH : (part + 1) * DH] for m in members]
            parts.append(pieces[0] if len(pieces) == 1 else jnp.concatenate(pieces, axis=0))
        return parts

    second = attend(*rows_of(range(SLABS), ROWS // 4))
    for pair in range(2):
        first = attend(*rows_of((2 * pair, 2 * pair + 1), ROWS // 2))
        for side in range(2):
            m = 2 * pair + side
            dense = attend(*rows_of((m,), ROWS))
            half = merge(
                tuple(value[: ROWS // 2] for value in dense),
                tuple(value[side * ROWS // 2 : (side + 1) * ROWS // 2] for value in first),
            )
            quarter = merge(
                tuple(value[: ROWS // 4] for value in half),
                tuple(value[m * ROWS // 4 : (m + 1) * ROWS // 4] for value in second),
            )
            for part in range(3):
                state_ref[0, part, pl.ds(m, DEEP, stride=SLABS), :] = jnp.broadcast_to(
                    quarter[part][:DEEP], (DEEP, DH)
                )
            done = jnp.concatenate(
                [
                    jnp.zeros((DEEP, DH), F32),
                    quarter[2][DEEP:] / quarter[1][DEEP:],
                    half[2][ROWS // 4 :] / half[1][ROWS // 4 :],
                    dense[2][ROWS // 2 :] / dense[1][ROWS // 2 :],
                ],
                axis=0,
            ).astype(BF)
            (u0, u1, u2, u3)[m][0] = jnp.dot(back, done, preferred_element_type=F32).astype(BF)


def near(place, offsets, qkv):
    return pl.pallas_call(
        near_body,
        out_shape=tuple(jax.ShapeDtypeStruct((SLOTS, ROWS, DH), BF) for _ in range(SLABS))
        + (jax.ShapeDtypeStruct((SLOTS, 3, SLABS * DEEP, DH), F32),),
        grid_spec=pltpu.PrefetchScalarGridSpec(
            num_scalar_prefetch=2,
            grid=(SLOTS,),
            in_specs=[pl.BlockSpec((1, SLABS, ROWS, 3 * DH), lambda j, *_: (j, 0, 0, 0))],
            out_specs=[pl.BlockSpec((1, ROWS, DH), lambda j, *_: (j, 0, 0)) for _ in range(SLABS)]
            + [pl.BlockSpec((1, 3, SLABS * DEEP, DH), lambda j, *_: (j, 0, 0, 0))],
        ),
        compiler_params=pltpu.CompilerParams(vmem_limit_bytes=VMEM_BYTES),
        cost_estimate=pl.CostEstimate(
            flops=SLOTS * 7 * 4 * ROWS * ROWS * DH,
            bytes_accessed=SLOTS * SLABS * ROWS * 4 * DH * 2,
            transcendentals=SLOTS * 7 * ROWS * ROWS,
        ),
        name="near",
    )(place, offsets, qkv)


def far_body(q_ref, state_ref, *refs):
    pairs = refs[:10]
    outs = refs[10:14]
    spread = refs[14]
    combined = tuple(state_ref[0, part] for part in range(3))
    combined = (combined[0][:, :1], combined[1][:, :1], combined[2])
    tails = []
    for level in range(5):
        rows = SLABS * DEEP >> level
        kept_ref, other_ref = pairs[2 * level], pairs[2 * level + 1]
        keys = jnp.concatenate([kept_ref[0, :, :DH], other_ref[0, :, :DH]], axis=0)
        values = jnp.concatenate([kept_ref[0, :, DH:], other_ref[0, :, DH:]], axis=0)
        found = attend(q_ref[0, : max(rows, 16), :], keys, values)
        combined = merge(combined, tuple(value[:rows] for value in found))
        half = rows // 2 if level < 4 else 0
        tails.append(combined[2][half:] / combined[1][half:])
        combined = tuple(value[:half] for value in combined)
    spread[...] = jnp.concatenate(tails[::-1], axis=0)
    for m in range(SLABS):
        outs[m][0] = spread[pl.ds(m, DEEP, stride=SLABS), :].astype(BF)


def far(deep_q, state, pairs):
    rows = SLABS * DEEP
    return pl.pallas_call(
        far_body,
        out_shape=tuple(jax.ShapeDtypeStruct((SLOTS, DEEP, DH), BF) for _ in range(SLABS)),
        grid=(SLOTS,),
        in_specs=[
            pl.BlockSpec((1, rows, DH), lambda j: (j, 0, 0)),
            pl.BlockSpec((1, 3, rows, DH), lambda j: (j, 0, 0, 0)),
        ]
        + [pl.BlockSpec((1, rows, 2 * DH), lambda j: (j, 0, 0)) for _ in pairs],
        out_specs=[pl.BlockSpec((1, DEEP, DH), lambda j: (j, 0, 0)) for _ in range(SLABS)],
        scratch_shapes=[pltpu.VMEM((rows, DH), F32)],
        compiler_params=pltpu.CompilerParams(vmem_limit_bytes=VMEM_BYTES),
        cost_estimate=pl.CostEstimate(
            flops=SLOTS * 2 * 4 * rows * ROWS * DH,
            bytes_accessed=SLOTS * rows * 10 * 2 * DH * 2,
            transcendentals=SLOTS * 2 * rows * ROWS,
        ),
        name="far",
    )(deep_q, state, *pairs)


def place_body(place_ref, offsets_ref, *refs):
    bulk, deep, out_ref = refs[:4], refs[4:8], refs[8]
    for m in range(SLABS):
        for slot in range(SLOTS):
            head = head_of(place_ref, m, slot)
            back = from_order(offsets_ref[head], DEEP)
            rows = jnp.dot(back, deep[m][slot], preferred_element_type=F32)
            column = pl.multiple_of(head * DH, DH)
            out_ref[:, pl.ds(column, DH)] = (bulk[m][slot].astype(F32) + rows).astype(BF)


def placed_heads(place, offsets, bulk, deep):
    whole = pl.BlockSpec(memory_space=pltpu.VMEM)
    scalars = pl.BlockSpec(memory_space=pltpu.SMEM)
    return pl.pallas_call(
        place_body,
        out_shape=jax.ShapeDtypeStruct((ROWS, HEADS * DH), BF),
        in_specs=[scalars, scalars] + [whole] * 8,
        out_specs=whole,
        compiler_params=pltpu.CompilerParams(vmem_limit_bytes=VMEM_BYTES),
        cost_estimate=pl.CostEstimate(
            flops=HEADS * 2 * ROWS * DEEP * DH,
            bytes_accessed=2 * ROWS * HEADS * DH * 2,
            transcendentals=0,
        ),
        name="place",
    )(place, offsets, *bulk, *deep)


def halves(value, pieces):
    heads, rows, width = value.shape
    part = rows // pieces
    return [value[:, k * part : k * part + part // 2] for k in range(pieces)]


def swap_slots(value):
    return jnp.concatenate([value[2:], value[:2]], axis=0)


def swap_cores(value):
    return jnp.concatenate([value[1:2], value[0:1], value[3:4], value[2:3]], axis=0)


def shards(tokens, qkv_weight, offsets):
    inner = lax.axis_index("inner").astype(jnp.int32)
    core = lax.axis_index("outer").astype(jnp.int32) & 1
    place = jnp.stack([inner, core])
    depth = qkv_weight.shape[0]

    sent = lax.dynamic_slice(qkv_weight, (0, core * 3 * DH), (depth, 3 * DH))
    weight_got = flipped(sent, 0, 6)
    slab_z = flipped(tokens, 0, 1)
    slab_y = flipped(tokens, 0, 2)
    slab_d = flipped(tokens, 0, 3)
    weight_rest = flipped(weight_got, 1, 0)
    slabs = (tokens, slab_z, slab_y, slab_d)

    carried = project(place, offsets, slabs, qkv_weight, 0, 2, True, None)
    carried = project(place, offsets, slabs, weight_got, 2, 1, False, carried)
    qkv, deep_q, deep_kv = project(place, offsets, slabs, weight_rest, 3, 1, False, carried)

    other = flipped(swap_slots(deep_kv), 0, 4 | 2)
    pairs = [deep_kv, other]
    kept, pieces = deep_kv, 1
    for level in range(4):
        kept = jnp.concatenate(halves(kept, pieces) + halves(other, pieces), axis=1)
        pieces *= 2
        other = flipped(swap_cores(kept) if level == 0 else kept, 1 << level, 0)
        pairs += [kept, other]

    *bulk, state = near(place, offsets, qkv)
    bulk = [bulk[0]] + [flipped(bulk[m], 0, m) for m in range(1, SLABS)]
    deep = far(deep_q, state, pairs)
    deep = [deep[0]] + [flipped(deep[m], 0, m) for m in range(1, SLABS)]
    return placed_heads(place, offsets, bulk, deep)


def solution(mesh):
    placed = (P(("outer", "inner"), None), P(None, "inner"), P())
    return jax.shard_map(
        shards, mesh=mesh, in_specs=placed, out_specs=P(("outer", "inner"), None), check_vma=False
    )
```

time: 817 us -> 180 us (0.22)
  waiting for transfers between devices: 594 us -> 99.7 us
  local copies, waits for them, and re-layouts: 127 us -> 7.29 us
  Pallas kernels: 0 us -> 44.9 us
  other arithmetic: 36.9 us -> 1.48 us
  matrix products: 29.5 us -> 0 us
  between operations: 14.5 us -> 0.3 us
  starting transfers between devices: 13.5 us -> 25.2 us
    all_gather x1 -> x0, waiting for transfers between devices: 484 us -> none  [shards(): lax.all_gather(qkv_weight, 'inner', axis=1, tiled=True)]
    pallas_call x0 -> x6, Pallas kernels: none -> 44.9 us  [the longest x3 25.5 us: project(): pl.pallas_call(lambda *refs: project_body(base, *refs), out_shape=shapes,...]
    slice x16 -> x6, local copies, waits for them, and re-layouts: 33.3 us -> 2.77 us  [the longest x5 1.79 us: halves(): return [value[:, k * part:k * part + part // 2] for k in range(pieces)]]
    dot_general x17 -> x0, matrix products: 29.5 us -> none  [the longest x1 12.8 us: shards(): jnp.dot(tokens, lax.all_gather(qkv_weight, 'inner', axis=1, tiled=True),...]
    reshape x7 -> x0, local copies, waits for them, and re-layouts: 20.1 us -> none  [the longest x6 17.8 us: select_half(): paired = source.reshape((row_count // 2, 2) + source.shape[1:])]
    mul x22 -> x0, local copies, waits for them, and re-layouts: 18.2 us -> none  [the longest x14 12.8 us: fold_level(): coarse_total[:, :, None] * coarse_scale]
    max x14 -> x0, local copies, waits for them, and re-layouts: 12.1 us -> none  [fold_level(): jnp.maximum(pair_top, coarse_top[:, :, None])]
    ppermute x7 -> x16, starting transfers between devices: 13.5 us -> 25.2 us  [flipped(): lax.ppermute(value, ('outer', 'inner'), [(f, f ^ mask) for f in range(cou...]
  transfers between devices with their start and end apart: 8 -> 16, of which waited for: 7 -> 11; matrix products, arithmetic and copies ran while one was open for 4% -> 3% of each run, Pallas kernels for 0% -> 19%
where the time goes in v1:
time: 180 us; the launch traced here: 179 us
  waiting for transfers between devices  99.7 us (55%)
  Pallas kernels  44.9 us (25%)
  starting transfers between devices  25.2 us (14%)
  local copies, waits for them, and re-layouts  7.29 us (4%)
    ppermute x16, waiting for transfers between devices, flipped(): lax.ppermute(value, ('outer', 'inner'), [(f, f ^ mask) for f in range(cou...  99.7 us
    pallas_call x3, Pallas kernels, project(): pl.pallas_call(lambda *refs: project_body(base, *refs), out_shape=shapes,...  25.5 us
    ppermute x16, starting transfers between devices, flipped(): lax.ppermute(value, ('outer', 'inner'), [(f, f ^ mask) for f in range(cou...  25.2 us
    pallas_call x1, Pallas kernels, near(): pl.pallas_call(near_body, out_shape=tuple((jax.ShapeDtypeStruct((SLOTS, R...  9.99 us
    pallas_call x1, Pallas kernels, far(): pl.pallas_call(far_body, out_shape=tuple((jax.ShapeDtypeStruct((SLOTS, DE...  6.59 us
  transfers between devices with their start and end apart: 16, of which 11 were waited for; matrix products, arithmetic and copies ran while one was open for 3% of the time, Pallas kernels for 19%

profile of v1, /device:TPU:0, one launch (start us, length us, event | category | flops | bytes accessed | tf_op | source)
XLA Modules:
  0.0 178.9 jit_solution(10659075246271529582)
XLA Ops:
  0.0 1.7 constant_dynamic-slice_fusion
  1.7 3.2 %collective-permute-start.3 = (bf16[2048,384]{1,0:T(8,128)(2,1)S(1)}, bf16[2048,384]{1,0:T(8,128)(2,1)}, u32[]{:S(2)}, u32[]{:S(2)}) collective-permute-start(bf16[2048,384]{1,0:T(8,128)(2,1)S(1)} %constant_dynamic-slice_fusion), channel_id=1, source_target_pairs={{0,6},{1,7},{2,4},{3,5},{4,2},{5,3},{6,0},{7,1},{8,14},{9,15},{10,... | collective-permute-start | bytes 4718600 | tf_op jit(solution)/shard_map/ppermute | solution.py:26
  4.8 34.5 %collective-permute-done.3.refs_6_ = bf16[2048,384]{1,0:T(8,128)(2,1)} collective-permute-done((bf16[2048,384]{1,0:T(8,128)(2,1)S(1)}, bf16[2048,384]{1,0:T(8,128)(2,1)}, u32[]{:S(2)}, u32[]{:S(2)}) %collective-permute-start.3) | collective-permute-done | bytes 1572896 | tf_op jit(solution)/shard_map/ppermute | solution.py:26
  39.3 1.9 %collective-permute-start = (bf16[256,2048]{1,0:T(8,128)(2,1)S(1)}, bf16[256,2048]{1,0:T(8,128)(2,1)S(1)}, u32[]{:S(2)}, u32[]{:S(2)}) collective-permute-start(bf16[256,2048]{1,0:T(8,128)(2,1)S(1)} %copy-done), channel_id=1, source_target_pairs={{0,1},{1,0},{2,3},{3,2},{4,5},{5,4},{6,7},{7,6},{8,9},{9,8},{10,11... | collective-permute-start | bytes 3145736 | tf_op jit(solution)/shard_map/ppermute | solution.py:26
  41.6 1.3 collective-permute-start.2
  43.5 21.6 %collective-permute-done.refs_3_ = bf16[256,2048]{1,0:T(8,128)(2,1)S(1)} collective-permute-done((bf16[256,2048]{1,0:T(8,128)(2,1)S(1)}, bf16[256,2048]{1,0:T(8,128)(2,1)S(1)}, u32[]{:S(2)}, u32[]{:S(2)}) %collective-permute-start) | collective-permute-done | bytes 1048608 | tf_op jit(solution)/shard_map/ppermute | solution.py:26
  65.1 2.2 %collective-permute-done.1.refs_4_ = bf16[256,2048]{1,0:T(8,128)(2,1)S(1)} collective-permute-done((bf16[256,2048]{1,0:T(8,128)(2,1)S(1)}, bf16[256,2048]{1,0:T(8,128)(2,1)S(1)}, u32[]{:S(2)}, u32[]{:S(2)}) %collective-permute-start.1) | collective-permute-done | bytes 1048608 | tf_op jit(solution)/shard_map/ppermute | solution.py:26
  67.3 21.6 %collective-permute-done.2.refs_5_ = bf16[256,2048]{1,0:T(8,128)(2,1)} collective-permute-done((bf16[256,2048]{1,0:T(8,128)(2,1)S(1)}, bf16[256,2048]{1,0:T(8,128)(2,1)}, u32[]{:S(2)}, u32[]{:S(2)}) %collective-permute-start.2) | collective-permute-done | bytes 1048608 | tf_op jit(solution)/shard_map/ppermute | solution.py:26
  88.9 10.7 %project.3 = (bf16[4,4,256,384]{3,2,1,0:T(8,128)(2,1)}, bf16[4,128,128]{2,1,0:T(8,128)(2,1)}, bf16[4,128,256]{2,1,0:T(8,128)(2,1)}) custom-call(s32[2]{0:T(128)} %pad_add_fusion.refs_0_.place_ref, s32[16]{0:T(128)} %offsets_ref.3, bf16[256,2048]{1,0:T(8,128)(2,1)} %refs_2_.5, bf16[256,2048]{1,0:T(8,128)(2,1)} %copy-done.1, bf16[256,2048]{1,0:T(8,128)(2,1)} %copy-done.2, ...), custom_call_target="tpu_custom_call" | custom-call | flops 3623878656 | bytes 7340032 | tf_op jit(solution)/shard_map/project/pallas_call | solution.py:81
  99.5 7.4 %project.4 = (bf16[4,4,256,384]{3,2,1,0:T(8,128)(2,1)}, bf16[4,128,128]{2,1,0:T(8,128)(2,1)}, bf16[4,128,256]{2,1,0:T(8,128)(2,1)}) custom-call(s32[2]{0:T(128)} %pad_add_fusion.refs_0_.place_ref, s32[16]{0:T(128)} %offsets_ref.3, bf16[256,2048]{1,0:T(8,128)(2,1)} %refs_2_.5, ...), custom_call_target="tpu_custom_call", output_to_operand_aliasing={{0}: (7, {}), {1}: (8, {}), {2}: (9, {})} | custom-call | flops 1811939328 | bytes 5767168 | tf_op jit(solution)/shard_map/project/pallas_call | solution.py:81
  107.0 7.4 %project.5 = (bf16[4,4,256,384]{3,2,1,0:T(8,128)(2,1)}, bf16[4,128,128]{2,1,0:T(8,128)(2,1)}, bf16[4,128,256]{2,1,0:T(8,128)(2,1)}) custom-call(s32[2]{0:T(128)} %pad_add_fusion.refs_0_.place_ref, s32[16]{0:T(128)} %offsets_ref.3, bf16[256,2048]{1,0:T(8,128)(2,1)} %refs_2_.5, ...), custom_call_target="tpu_custom_call", output_to_operand_aliasing={{0}: (7, {}), {1}: (8, {}), {2}: (9, {})} | custom-call | flops 1811939328 | bytes 5767168 | tf_op jit(solution)/shard_map/project/pallas_call | solution.py:81
  115.4 3.0 %collective-permute-start.8 = (bf16[4,128,256]{2,1,0:T(8,128)(2,1)S(1)}, bf16[4,128,256]{2,1,0:T(8,128)(2,1)S(1)}, u32[]{:S(2)}, u32[]{:S(2)}) collective-permute-start(bf16[4,128,256]{2,1,0:T(8,128)(2,1)S(1)} %pad_maximum_fusion.1), channel_id=1, source_target_pairs={{0,6},{1,7},{2,4},{3,5},{4,2},{5,3},{6,0},{7,1},{8,14},{9,15},{10,... | collective-permute-start | bytes 786440 | tf_op jit(solution)/shard_map/ppermute | solution.py:26
  121.7 2.8 %collective-permute-done.8.refs_1_ = bf16[4,128,256]{2,1,0:T(8,128)(2,1)S(1)} collective-permute-done((bf16[4,128,256]{2,1,0:T(8,128)(2,1)S(1)}, bf16[4,128,256]{2,1,0:T(8,128)(2,1)S(1)}, u32[]{:S(2)}, u32[]{:S(2)}) %collective-permute-start.8) | collective-permute-done | bytes 262176 | tf_op jit(solution)/shard_map/ppermute | solution.py:26
  124.7 1.5 collective-permute-done.9.refs_3_
  126.3 3.5 %collective-permute-start.10 = (bf16[4,128,256]{2,1,0:T(8,128)(2,1)S(1)}, bf16[4,128,256]{2,1,0:T(8,128)(2,1)S(1)}, u32[]{:S(2)}, u32[]{:S(2)}) collective-permute-start(bf16[4,128,256]{2,1,0:T(8,128)(2,1)S(1)} %pad_maximum_fusion.3.refs_4_), channel_id=1, source_target_pairs={{0,16},{1,17},{2,18},{3,19},{4,20},{5,21},{6,22},{7,23},{8,24},{9,... | collective-permute-start | bytes 786440 | tf_op jit(solution)/shard_map/ppermute | solution.py:26
  129.9 6.6 %collective-permute-done.10.refs_5_ = bf16[4,128,256]{2,1,0:T(8,128)(2,1)S(1)} collective-permute-done((bf16[4,128,256]{2,1,0:T(8,128)(2,1)S(1)}, bf16[4,128,256]{2,1,0:T(8,128)(2,1)S(1)}, u32[]{:S(2)}, u32[]{:S(2)}) %collective-permute-start.10) | collective-permute-done | bytes 262176 | tf_op jit(solution)/shard_map/ppermute | solution.py:26
  136.5 1.8 collective-permute-start.11
  138.3 6.2 %collective-permute-done.11.refs_7_ = bf16[4,128,256]{2,1,0:T(8,128)(2,1)S(1)} collective-permute-done((bf16[4,128,256]{2,1,0:T(8,128)(2,1)S(1)}, bf16[4,128,256]{2,1,0:T(8,128)(2,1)S(1)}, u32[]{:S(2)}, u32[]{:S(2)}) %collective-permute-start.11) | collective-permute-done | bytes 262176 | tf_op jit(solution)/shard_map/ppermute | solution.py:26
  144.6 3.0 %collective-permute-start.12 = (bf16[4,128,256]{2,1,0:T(8,128)(2,1)S(1)}, bf16[4,128,256]{2,1,0:T(8,128)(2,1)S(1)}, u32[]{:S(2)}, u32[]{:S(2)}) collective-permute-start(bf16[4,128,256]{2,1,0:T(8,128)(2,1)S(1)} %constant_dynamic-update-slice_fusion.8.refs_8_), channel_id=1, source_target_pairs={{0,64},{1,65},{2,66},{3,67},{4,68},{5,69},{6,70},{7,71},{8,72},{9,... | collective-permute-start | bytes 786440 | tf_op jit(solution)/shard_map/ppermute | solution.py:26
  147.6 10.0 %near.1 = (bf16[4,256,128]{2,1,0:T(8,128)(2,1)}, bf16[4,256,128]{2,1,0:T(8,128)(2,1)}, bf16[4,256,128]{2,1,0:T(8,128)(2,1)}, bf16[4,256,128]{2,1,0:T(8,128)(2,1)}, f32[4,3,128,128]{3,2,1,0:T(8,128)}) custom-call(s32[2]{0:T(128)} %pad_add_fusion.refs_0_.place_ref, s32[16]{0:T(128)} %offsets_ref.3, bf16[4,4,256,384]{3,2,1,0:T(8,128)(2,1)} %get-tuple-element.29.qkv_ref), custom_call_target="tpu_custom_call" | custom-call | flops 939524096 | bytes 4194304 | tf_op jit(solution)/shard_map/near/pallas_call | solution.py:171
  158.7 2.4 %collective-permute-start.7 = (bf16[4,256,128]{2,1,0:T(8,128)(2,1)}, bf16[4,256,128]{2,1,0:T(8,128)(2,1)S(1)}, u32[]{:S(2)}, u32[]{:S(2)}) collective-permute-start(bf16[4,256,128]{2,1,0:T(8,128)(2,1)} %get-tuple-element.33), channel_id=1, source_target_pairs={{0,3},{1,2},{2,1},{3,0},{4,7},{5,6},{6,5},{7,4},{8,11},{9,10},{10,... | collective-permute-start | bytes 786440 | tf_op jit(solution)/shard_map/ppermute | solution.py:26
  162.5 6.6 %far.1 = (bf16[4,32,128]{2,1,0:T(8,128)(2,1)}, bf16[4,32,128]{2,1,0:T(8,128)(2,1)}, bf16[4,32,128]{2,1,0:T(8,128)(2,1)}, bf16[4,32,128]{2,1,0:T(8,128)(2,1)}) custom-call(bf16[4,128,128]{2,1,0:T(8,128)(2,1)} %get-tuple-element.34.q_ref, f32[4,3,128,128]{3,2,1,0:T(8,128)} %get-tuple-element.35.state_ref, bf16[4,128,256]{2,1,0:T(8,128)(2,1)} %get-tuple-element.36.refs_0_, ...), custom_call_target="tpu_custom_call" | custom-call | flops 134217728 | bytes 2621440 | tf_op jit(solution)/shard_map/far/pallas_call | solution.py:216
  170.3 2.4 %collective-permute-start.15 = (bf16[4,32,128]{2,1,0:T(8,128)(2,1)}, bf16[4,32,128]{2,1,0:T(8,128)(2,1)S(1)}, u32[]{:S(2)}, u32[]{:S(2)}) collective-permute-start(bf16[4,32,128]{2,1,0:T(8,128)(2,1)} %get-tuple-element.40), channel_id=1, source_target_pairs={{0,3},{1,2},{2,1},{3,0},{4,7},{5,6},{6,5},{7,4},{8,11},{9,10},{10,... | collective-permute-start | bytes 98312 | tf_op jit(solution)/shard_map/ppermute | solution.py:26
  176.1 2.8 %place.1 = bf16[256,2048]{1,0:T(8,128)(2,1)} custom-call(s32[2]{0:T(128)} %pad_add_fusion.refs_0_.place_ref, s32[16]{0:T(128)} %offsets_ref.3, bf16[4,256,128]{2,1,0:T(8,128)(2,1)} %get-tuple-element.30.refs_0_, bf16[4,256,128]{2,1,0:T(8,128)(2,1)} %copy-done.11, bf16[4,256,128]{2,1,0:T(8,128)(2,1)} %copy-done.12, bf16[4,256,128]{2,1,0:T(8,128)(2,1)} %copy-done.13, ...), custom_call_target="tpu_custom_call" | custom-call | flops 33554432 | bytes 2097152 | tf_op jit(solution)/shard_map/place/pallas_call | solution.py:251
  (85 shorter events, 12.5 us)
Async XLA Ops:
  0.0 39.3 %copy-start = (bf16[256,2048]{1,0:T(8,128)(2,1)S(1)}, bf16[256,2048]{1,0:T(8,128)(2,1)}, u32[]{:S(2)}) copy-start(bf16[256,2048]{1,0:T(8,128)(2,1)} %refs_2_.5) | copy-start | bytes 3145732
  1.7 37.7 %collective-permute-start.3 = (bf16[2048,384]{1,0:T(8,128)(2,1)S(1)}, bf16[2048,384]{1,0:T(8,128)(2,1)}, u32[]{:S(2)}, u32[]{:S(2)}) collective-permute-start(bf16[2048,384]{1,0:T(8,128)(2,1)S(1)} %constant_dynamic-slice_fusion), channel_id=1, source_target_pairs={{0,6},{1,7},{2,4},{3,5},{4,2},{5,3},{6,0},{7,1},{8,14},{9,15},{10,... | collective-permute-start | bytes 4718600 | tf_op jit(solution)/shard_map/ppermute | solution.py:26
  39.3 67.6 %collective-permute-start.4 = (bf16[2048,384]{1,0:T(8,128)(2,1)}, bf16[2048,384]{1,0:T(8,128)(2,1)}, u32[]{:S(2)}, u32[]{:S(2)}) collective-permute-start(bf16[2048,384]{1,0:T(8,128)(2,1)} %collective-permute-done.3.refs_6_), channel_id=1, source_target_pairs={{0,8},{1,9},{2,10},{3,11},{4,12},{5,13},{6,14},{7,15},{8,0},{9,1},... | collective-permute-start | bytes 4718600 | tf_op jit(solution)/shard_map/ppermute | solution.py:26
  39.3 25.7 %collective-permute-start = (bf16[256,2048]{1,0:T(8,128)(2,1)S(1)}, bf16[256,2048]{1,0:T(8,128)(2,1)S(1)}, u32[]{:S(2)}, u32[]{:S(2)}) collective-permute-start(bf16[256,2048]{1,0:T(8,128)(2,1)S(1)} %copy-done), channel_id=1, source_target_pairs={{0,1},{1,0},{2,3},{3,2},{4,5},{5,4},{6,7},{7,6},{8,9},{9,8},{10,11... | collective-permute-start | bytes 3145736 | tf_op jit(solution)/shard_map/ppermute | solution.py:26
  41.3 26.0 %collective-permute-start.1 = (bf16[256,2048]{1,0:T(8,128)(2,1)S(1)}, bf16[256,2048]{1,0:T(8,128)(2,1)S(1)}, u32[]{:S(2)}, u32[]{:S(2)}) collective-permute-start(bf16[256,2048]{1,0:T(8,128)(2,1)S(1)} %copy-done), channel_id=1, source_target_pairs={{0,2},{1,3},{2,0},{3,1},{4,6},{5,7},{6,4},{7,5},{8,10},{9,11},{10,... | collective-permute-start | bytes 3145736 | tf_op jit(solution)/shard_map/ppermute | solution.py:26
  41.6 47.3 %collective-permute-start.2 = (bf16[256,2048]{1,0:T(8,128)(2,1)S(1)}, bf16[256,2048]{1,0:T(8,128)(2,1)}, u32[]{:S(2)}, u32[]{:S(2)}) collective-permute-start(bf16[256,2048]{1,0:T(8,128)(2,1)S(1)} %copy-done), channel_id=1, source_target_pairs={{0,3},{1,2},{2,1},{3,0},{4,7},{5,6},{6,5},{7,4},{8,11},{9,10},{10,... | collective-permute-start | bytes 3145736 | tf_op jit(solution)/shard_map/ppermute | solution.py:26
  65.1 23.8 %copy-start.1 = (bf16[256,2048]{1,0:T(8,128)(2,1)}, bf16[256,2048]{1,0:T(8,128)(2,1)S(1)}, u32[]{:S(2)}) copy-start(bf16[256,2048]{1,0:T(8,128)(2,1)S(1)} %collective-permute-done.refs_3_) | copy-start | bytes 3145732
  67.3 21.6 %copy-start.2 = (bf16[256,2048]{1,0:T(8,128)(2,1)}, bf16[256,2048]{1,0:T(8,128)(2,1)S(1)}, u32[]{:S(2)}) copy-start(bf16[256,2048]{1,0:T(8,128)(2,1)S(1)} %collective-permute-done.1.refs_4_) | copy-start | bytes 3145732
  115.4 9.1 %collective-permute-start.8 = (bf16[4,128,256]{2,1,0:T(8,128)(2,1)S(1)}, bf16[4,128,256]{2,1,0:T(8,128)(2,1)S(1)}, u32[]{:S(2)}, u32[]{:S(2)}) collective-permute-start(bf16[4,128,256]{2,1,0:T(8,128)(2,1)S(1)} %pad_maximum_fusion.1), channel_id=1, source_target_pairs={{0,6},{1,7},{2,4},{3,5},{4,2},{5,3},{6,0},{7,1},{8,14},{9,15},{10,... | collective-permute-start | bytes 786440 | tf_op jit(solution)/shard_map/ppermute | solution.py:26
  124.5 33.1 %copy-start.4 = (bf16[4,128,256]{2,1,0:T(8,128)(2,1)}, bf16[4,128,256]{2,1,0:T(8,128)(2,1)S(1)}, u32[]{:S(2)}) copy-start(bf16[4,128,256]{2,1,0:T(8,128)(2,1)S(1)} %collective-permute-done.8.refs_1_) | copy-start | bytes 786436
  124.6 1.6 collective-permute-start.9
  126.2 35.6 %copy-start.5 = (bf16[4,128,256]{2,1,0:T(8,128)(2,1)}, bf16[4,128,256]{2,1,0:T(8,128)(2,1)S(1)}, u32[]{:S(2)}) copy-start(bf16[4,128,256]{2,1,0:T(8,128)(2,1)S(1)} %collective-permute-done.9.refs_3_) | copy-start | bytes 786436
  126.3 35.6 %copy-start.3 = (bf16[4,128,256]{2,1,0:T(8,128)(2,1)}, bf16[4,128,256]{2,1,0:T(8,128)(2,1)S(1)}, u32[]{:S(2)}) copy-start(bf16[4,128,256]{2,1,0:T(8,128)(2,1)S(1)} %pad_maximum_fusion.3.refs_4_) | copy-start | bytes 786436
  126.3 10.2 %collective-permute-start.10 = (bf16[4,128,256]{2,1,0:T(8,128)(2,1)S(1)}, bf16[4,128,256]{2,1,0:T(8,128)(2,1)S(1)}, u32[]{:S(2)}, u32[]{:S(2)}) collective-permute-start(bf16[4,128,256]{2,1,0:T(8,128)(2,1)S(1)} %pad_maximum_fusion.3.refs_4_), channel_id=1, source_target_pairs={{0,16},{1,17},{2,18},{3,19},{4,20},{5,21},{6,22},{7,23},{8,24},{9,... | collective-permute-start | bytes 786440 | tf_op jit(solution)/shard_map/ppermute | solution.py:26
  136.4 25.4 %copy-start.6 = (bf16[4,128,256]{2,1,0:T(8,128)(2,1)}, bf16[4,128,256]{2,1,0:T(8,128)(2,1)S(1)}, u32[]{:S(2)}) copy-start(bf16[4,128,256]{2,1,0:T(8,128)(2,1)S(1)} %collective-permute-done.10.refs_5_) | copy-start | bytes 786436
  136.5 25.4 %copy-start.8 = (bf16[4,128,256]{2,1,0:T(8,128)(2,1)}, bf16[4,128,256]{2,1,0:T(8,128)(2,1)S(1)}, u32[]{:S(2)}) copy-start(bf16[4,128,256]{2,1,0:T(8,128)(2,1)S(1)} %constant_dynamic-update-slice_fusion.refs_6_) | copy-start | bytes 786436
  136.5 8.0 %collective-permute-start.11 = (bf16[4,128,256]{2,1,0:T(8,128)(2,1)S(1)}, bf16[4,128,256]{2,1,0:T(8,128)(2,1)S(1)}, u32[]{:S(2)}, u32[]{:S(2)}) collective-permute-start(bf16[4,128,256]{2,1,0:T(8,128)(2,1)S(1)} %constant_dynamic-update-slice_fusion.refs_6_), channel_id=1, source_target_pairs={{0,32},{1,33},{2,34},{3,35},{4,36},{5,37},{6,38},{7,39},{8,40},{9,... | collective-permute-start | bytes 786440 | tf_op jit(solution)/shard_map/ppermute | solution.py:26
  144.6 17.2 %collective-permute-start.12 = (bf16[4,128,256]{2,1,0:T(8,128)(2,1)S(1)}, bf16[4,128,256]{2,1,0:T(8,128)(2,1)S(1)}, u32[]{:S(2)}, u32[]{:S(2)}) collective-permute-start(bf16[4,128,256]{2,1,0:T(8,128)(2,1)S(1)} %constant_dynamic-update-slice_fusion.8.refs_8_), channel_id=1, source_target_pairs={{0,64},{1,65},{2,66},{3,67},{4,68},{5,69},{6,70},{7,71},{8,72},{9,... | collective-permute-start | bytes 786440 | tf_op jit(solution)/shard_map/ppermute | solution.py:26
  157.6 12.7 %collective-permute-start.5 = (bf16[4,256,128]{2,1,0:T(8,128)(2,1)}, bf16[4,256,128]{2,1,0:T(8,128)(2,1)S(1)}, u32[]{:S(2)}, u32[]{:S(2)}) collective-permute-start(bf16[4,256,128]{2,1,0:T(8,128)(2,1)} %get-tuple-element.31), channel_id=1, source_target_pairs={{0,1},{1,0},{2,3},{3,2},{4,5},{5,4},{6,7},{7,6},{8,9},{9,8},{10,11... | collective-permute-start | bytes 786440 | tf_op jit(solution)/shard_map/ppermute | solution.py:26
  158.7 14.0 %collective-permute-start.6 = (bf16[4,256,128]{2,1,0:T(8,128)(2,1)}, bf16[4,256,128]{2,1,0:T(8,128)(2,1)S(1)}, u32[]{:S(2)}, u32[]{:S(2)}) collective-permute-start(bf16[4,256,128]{2,1,0:T(8,128)(2,1)} %get-tuple-element.32), channel_id=1, source_target_pairs={{0,2},{1,3},{2,0},{3,1},{4,6},{5,7},{6,4},{7,5},{8,10},{9,11},{10,... | collective-permute-start | bytes 786440 | tf_op jit(solution)/shard_map/ppermute | solution.py:26
  158.7 14.0 %collective-permute-start.7 = (bf16[4,256,128]{2,1,0:T(8,128)(2,1)}, bf16[4,256,128]{2,1,0:T(8,128)(2,1)S(1)}, u32[]{:S(2)}, u32[]{:S(2)}) collective-permute-start(bf16[4,256,128]{2,1,0:T(8,128)(2,1)} %get-tuple-element.33), channel_id=1, source_target_pairs={{0,3},{1,2},{2,1},{3,0},{4,7},{5,6},{6,5},{7,4},{8,11},{9,10},{10,... | collective-permute-start | bytes 786440 | tf_op jit(solution)/shard_map/ppermute | solution.py:26
  169.1 4.2 %collective-permute-start.13 = (bf16[4,32,128]{2,1,0:T(8,128)(2,1)}, bf16[4,32,128]{2,1,0:T(8,128)(2,1)S(1)}, u32[]{:S(2)}, u32[]{:S(2)}) collective-permute-start(bf16[4,32,128]{2,1,0:T(8,128)(2,1)} %get-tuple-element.38), channel_id=1, source_target_pairs={{0,1},{1,0},{2,3},{3,2},{4,5},{5,4},{6,7},{7,6},{8,9},{9,8},{10,11... | collective-permute-start | bytes 98312 | tf_op jit(solution)/shard_map/ppermute | solution.py:26
  170.3 4.1 %collective-permute-start.14 = (bf16[4,32,128]{2,1,0:T(8,128)(2,1)}, bf16[4,32,128]{2,1,0:T(8,128)(2,1)S(1)}, u32[]{:S(2)}, u32[]{:S(2)}) collective-permute-start(bf16[4,32,128]{2,1,0:T(8,128)(2,1)} %get-tuple-element.39), channel_id=1, source_target_pairs={{0,2},{1,3},{2,0},{3,1},{4,6},{5,7},{6,4},{7,5},{8,10},{9,11},{10,... | collective-permute-start | bytes 98312 | tf_op jit(solution)/shard_map/ppermute | solution.py:26
  170.3 5.1 %collective-permute-start.15 = (bf16[4,32,128]{2,1,0:T(8,128)(2,1)}, bf16[4,32,128]{2,1,0:T(8,128)(2,1)S(1)}, u32[]{:S(2)}, u32[]{:S(2)}) collective-permute-start(bf16[4,32,128]{2,1,0:T(8,128)(2,1)} %get-tuple-element.40), channel_id=1, source_target_pairs={{0,3},{1,2},{2,1},{3,0},{4,7},{5,6},{6,5},{7,4},{8,11},{9,10},{10,... | collective-permute-start | bytes 98312 | tf_op jit(solution)/shard_map/ppermute | solution.py:26
  (9 other events, 49.6 us)

commit v2 on v0

v2 whole, which is shorter than its diff:
```python
import math

import jax
import jax.numpy as jnp
from jax import lax
from jax.experimental import pallas as pl
from jax.experimental.pallas import tpu as pltpu
from jax.sharding import PartitionSpec as P


HEADS = 16
DH = 128
ROWS = 256
DEEP = 32
SLABS = 4
SLOTS = 4
DROWS = SLABS * DEEP
BF = jnp.bfloat16
F32 = jnp.float32
I32 = jnp.int32
VMEM_BYTES = 24 * 1024 * 1024
LOW = -1e30


def flipped(value, o_mask, i_mask):
    inner = lax.axis_size("inner")
    count = inner * lax.axis_size("outer")
    mask = o_mask * inner + i_mask
    return lax.ppermute(value, ("outer", "inner"), [(f, f ^ mask) for f in range(count)])


def head_of(place_ref, m, slot):
    shard = place_ref[0] ^ m ^ (6 * (slot >> 1))
    return 2 * shard + (slot & 1)


def position_of(row, offset):
    index = row >> 1
    reverse = jnp.zeros_like(index)
    for bit in range(7):
        reverse = reverse | (((index >> bit) & 1) << (6 - bit))
    return ((row & 1) << 7) | (reverse ^ (offset & 127))


def to_order(offset):
    row = lax.broadcasted_iota(I32, (ROWS, 1), 0)
    column = lax.broadcasted_iota(I32, (ROWS, ROWS), 1)
    return jnp.where(position_of(row, offset) == column, 1.0, 0.0).astype(BF)


def from_order(offset, count):
    row = lax.broadcasted_iota(I32, (ROWS, count), 0)
    column = lax.broadcasted_iota(I32, (1, count), 1)
    return jnp.where(position_of(column, offset) == row, 1.0, 0.0).astype(BF)


def project_body(groups, n_x, n_w, first_slot, last_deep, *refs):
    place_ref, offsets_ref = refs[:2]
    xs, ws = refs[2 : 2 + n_x], refs[2 + n_x : 2 + n_x + n_w]
    qkv_ref, orders = refs[-2 - 2 * last_deep], refs[-1]
    for k in range(2):
        orders[k] = to_order(offsets_ref[head_of(place_ref, 0, first_slot + k)])
    chunk = ws[0].shape[0]
    for members in groups:
        total = None
        for index, w_ref in enumerate(ws):
            if n_w == 1:
                columns = slice(None)
            else:
                per_core = n_w // 2
                start = (place_ref[1] ^ (index // per_core)) * per_core + index % per_core
                columns = pl.ds(pl.multiple_of(start * chunk, chunk), chunk)
            rows = [xs[piece][:, columns] for _, pieces in members for piece in pieces]
            rows = rows[0] if len(rows) == 1 else jnp.concatenate(rows, axis=0)
            product = jnp.dot(rows, w_ref[...], preferred_element_type=F32)
            total = product if total is None else total + product
        total = total.astype(BF)
        for number, (m, _) in enumerate(members):
            for k in range(2):
                found = total[number * ROWS : (number + 1) * ROWS, k * 3 * DH : (k + 1) * 3 * DH]
                found = jnp.dot(orders[k], found, preferred_element_type=F32)
                qkv_ref[m, first_slot + k] = found.astype(BF)


def spread_body(qkv_ref, deep_q_ref, deep_kv_ref, spread):
    for slot in range(SLOTS):
        for part in range(3):
            for m in range(SLABS):
                piece = qkv_ref[m, slot, :DEEP, part * DH : (part + 1) * DH].astype(F32)
                spread[slot, part, pl.ds(m, DEEP, stride=SLABS), :] = piece
        deep_q_ref[slot] = spread[slot, 0].astype(BF)
        deep_kv_ref[slot, :, :DH] = spread[slot, 1].astype(BF)
        deep_kv_ref[slot, :, DH:] = spread[slot, 2].astype(BF)


def project(place, offsets, xs, ws, groups, first_slot, carried, last_deep):
    whole = pl.BlockSpec(memory_space=pltpu.VMEM)
    scalars = pl.BlockSpec(memory_space=pltpu.SMEM)
    out_shape = [jax.ShapeDtypeStruct((SLABS, SLOTS, ROWS, 3 * DH), BF)]
    scratch = [pltpu.VMEM((2, ROWS, ROWS), BF)]
    if last_deep:
        out_shape += [
            jax.ShapeDtypeStruct((SLOTS, DROWS, DH), BF),
            jax.ShapeDtypeStruct((SLOTS, DROWS, 2 * DH), BF),
        ]
        scratch.append(pltpu.VMEM((SLOTS, 3, DROWS, DH), F32))
    extra = [] if carried is None else [carried]

    def body(*refs):
        if not last_deep:
            project_body(groups, len(xs), len(ws), first_slot, 0, *refs)
            return
        *front, qkv_ref, deep_q_ref, deep_kv_ref, orders, spread = refs
        project_body(groups, len(xs), len(ws), first_slot, 0, *front, qkv_ref, orders)
        spread_body(qkv_ref, deep_q_ref, deep_kv_ref, spread)

    slabs = sum(len(members) for members in groups)
    depth, width = xs[0].shape[1], ws[0].shape[1]
    return pl.pallas_call(
        body,
        out_shape=out_shape,
        in_specs=[scalars, scalars] + [whole] * (len(xs) + len(ws) + len(extra)),
        out_specs=[whole] * len(out_shape),
        scratch_shapes=scratch,
        input_output_aliases={2 + len(xs) + len(ws): 0} if extra else {},
        compiler_params=pltpu.CompilerParams(vmem_limit_bytes=VMEM_BYTES),
        cost_estimate=pl.CostEstimate(
            flops=slabs * 2 * ROWS * width * (depth + ROWS),
            bytes_accessed=slabs * ROWS * depth * 2 + depth * width * 2,
            transcendentals=0,
        ),
        name="project",
    )(place, offsets, *xs, *ws, *extra)


def scores_of(q, k):
    scores = lax.dot_general(q, k, (((1,), (1,)), ((), ())), preferred_element_type=F32)
    return scores * (1.0 / math.sqrt(DH))


def weigh(scores, top, v, count):
    exponent = jnp.exp(scores - top)
    if count is not None:
        exponent = exponent * count
    total = jnp.sum(exponent, axis=1, keepdims=True)
    return total, jnp.dot(exponent.astype(BF), v, preferred_element_type=F32)


def near_body(base, heads, n_extra, place_ref, offsets_ref, qkv_ref, *refs):
    *outs, state_ref = refs[n_extra:]

    @pl.loop(0, heads)
    def _(j):
        slot = base + j
        back = from_order(offsets_ref[head_of(place_ref, 0, slot)], ROWS)

        def rows_of(members, count):
            parts = []
            for part in range(3):
                pieces = [qkv_ref[m, slot, :count, part * DH : (part + 1) * DH] for m in members]
                parts.append(pieces[0] if len(pieces) == 1 else jnp.concatenate(pieces, axis=0))
            return parts

        sets = [rows_of((m,), ROWS) for m in range(SLABS)]
        sets += [rows_of((0, 1), ROWS // 2), rows_of((2, 3), ROWS // 2), rows_of(range(SLABS), ROWS // 4)]
        scores = [scores_of(q, k) for q, k, _ in sets]
        wide = [jnp.maximum(score[:, :DH], score[:, DH:]) for score in scores]
        tops = []
        for m in range(SLABS):
            pair = wide[4 + m // 2][m % 2 * 128 : m % 2 * 128 + 128]
            four = wide[6][m * 64 : m * 64 + 64]
            first = jnp.maximum(wide[m][:64], jnp.maximum(pair[:64], four))
            second = jnp.maximum(wide[m][64:128], pair[64:])
            top = jnp.concatenate([first, second, wide[m][128:]], axis=0)
            tops.append(jnp.max(top, axis=1, keepdims=True))
        tops += [jnp.concatenate([top[:128] for top in tops[2 * k : 2 * k + 2]], axis=0) for k in range(2)]
        tops.append(jnp.concatenate([top[:64] for top in tops[:SLABS]], axis=0))
        found = [weigh(scores[k], tops[k], sets[k][2], None) for k in range(7)]
        for m in range(SLABS):
            sums = []
            for part in range(2):
                dense, four = found[m][part], found[6][part][m * 64 : m * 64 + 64]
                pair = found[4 + m // 2][part][m % 2 * 128 : m % 2 * 128 + 128]
                sums.append((dense[:64] + pair[:64] + four, dense[64:128] + pair[64:], dense[128:]))
            for part, value in enumerate((tops[m], sums[0][0], sums[1][0])):
                state_ref[slot, part, pl.ds(m, DEEP, stride=SLABS), :] = jnp.broadcast_to(
                    value[:DEEP], (DEEP, DH)
                )
            done = jnp.concatenate(
                [jnp.zeros((DEEP, DH), F32), sums[1][0][DEEP:] / sums[0][0][DEEP:]]
                + [sums[1][k] / sums[0][k] for k in (1, 2)],
                axis=0,
            ).astype(BF)
            outs[m][slot] = jnp.dot(back, done, preferred_element_type=F32).astype(BF)


def near(place, offsets, qkv, base, heads, carried):
    whole = pl.BlockSpec(memory_space=pltpu.VMEM)
    scalars = pl.BlockSpec(memory_space=pltpu.SMEM)
    return pl.pallas_call(
        lambda *refs: near_body(base, heads, len(carried), *refs),
        out_shape=tuple(jax.ShapeDtypeStruct((SLOTS, ROWS, DH), BF) for _ in range(SLABS))
        + (jax.ShapeDtypeStruct((SLOTS, 3, DROWS, DH), F32),),
        in_specs=[scalars, scalars] + [whole] * (1 + len(carried)),
        out_specs=[whole] * 5,
        input_output_aliases={3 + k: k for k in range(len(carried))},
        compiler_params=pltpu.CompilerParams(vmem_limit_bytes=VMEM_BYTES),
        cost_estimate=pl.CostEstimate(
            flops=heads * 7 * 4 * ROWS * ROWS * DH,
            bytes_accessed=heads * SLABS * ROWS * 4 * DH * 2,
            transcendentals=heads * 7 * ROWS * ROWS,
        ),
        name="near",
    )(place, offsets, qkv, *carried)


def level_of(row):
    level = jnp.full_like(row, 3)
    for deeper in range(4):
        level = level + jnp.where(row < (64 >> deeper), 1, 0)
    return level


def count_of(rows, pieces, piece, lowest):
    query = level_of(lax.broadcasted_iota(I32, (rows, 1), 0))
    key = level_of(lax.broadcasted_iota(I32, (1, pieces * piece), 1) & (piece - 1))
    return jnp.maximum(jnp.minimum(query, key) - (lowest - 1), 0).astype(F32)


def join(state, scores, counts, values):
    old_top, old_total, old_mixed = state
    masked = [jnp.where(count > 0, score, LOW) for score, count in zip(scores, counts)]
    top = old_top
    for score in masked:
        top = jnp.maximum(top, jnp.max(score, axis=1, keepdims=True))
    scale = jnp.exp(old_top - top)
    total, mixed = old_total * scale, old_mixed * scale
    for score, count, value in zip(masked, counts, values):
        more_total, more_mixed = weigh(score, top, value, count)
        total, mixed = total + more_total, mixed + more_mixed
    return top, total, mixed


def middle_body(q_ref, near_ref, own_ref, other_ref, core_ref, done_ref, state_ref):
    for slot in range(SLOTS):
        state = tuple(near_ref[slot, part] for part in range(3))
        state = (state[0][:, :1], state[1][:, :1], state[2])
        keys = [own_ref[slot, :, :DH], other_ref[slot, :, :DH], core_ref[slot, :, :DH]]
        values = [own_ref[slot, :, DH:], other_ref[slot, :, DH:], core_ref[slot, :, DH:]]
        scores = [scores_of(q_ref[slot], key) for key in keys]
        counts = [count_of(DROWS, 1, DROWS, 3), count_of(DROWS, 1, DROWS, 3), count_of(DROWS, 2, 64, 4)]
        top, total, mixed = join(state, scores, counts, values)
        done_ref[slot] = mixed[DEEP:] / total[DEEP:]
        for part, value in enumerate((top, total, mixed)):
            state_ref[slot, part] = jnp.broadcast_to(value[:DEEP], (DEEP, DH))


def middle(deep_q, state, own, other, core):
    whole = pl.BlockSpec(memory_space=pltpu.VMEM)
    return pl.pallas_call(
        middle_body,
        out_shape=(
            jax.ShapeDtypeStruct((SLOTS, DROWS - DEEP, DH), F32),
            jax.ShapeDtypeStruct((SLOTS, 3, DEEP, DH), F32),
        ),
        in_specs=[whole] * 5,
        out_specs=[whole] * 2,
        compiler_params=pltpu.CompilerParams(vmem_limit_bytes=VMEM_BYTES),
        cost_estimate=pl.CostEstimate(
            flops=SLOTS * 4 * DROWS * 3 * DROWS * DH,
            bytes_accessed=SLOTS * DROWS * 10 * DH * 2,
            transcendentals=SLOTS * DROWS * 3 * DROWS,
        ),
        name="middle",
    )(deep_q, state, own, other, core)


def far_body(place_ref, q_ref, state_ref, done_ref, mine5, mine6, mine7, their5, their6, their7, *rest):
    outs, spread = rest[:SLABS], rest[SLABS]
    core = place_ref[1]
    for slot in range(SLOTS):
        state = tuple(state_ref[slot, part] for part in range(3))
        state = (state[0][:, :1], state[1][:, :1], state[2])
        keys, values = [], []
        for mine, their in ((mine5, their5), (mine6, their6), (mine7, their7)):
            found = jnp.where(core == slot % 2, mine[slot // 2], their[slot // 2])
            keys.append(found[:, :DH])
            values.append(found[:, DH:])
        scores = [scores_of(q_ref[slot, :DEEP], key) for key in keys]
        counts = [count_of(DEEP, 4, 32, 5), count_of(DEEP, 8, 16, 6), count_of(DEEP, 16, 8, 7)]
        _, total, mixed = join(state, scores, counts, values)
        spread[slot, :DEEP] = mixed / total
        spread[slot, DEEP:] = done_ref[slot]
        for m in range(SLABS):
            outs[m][slot] = spread[slot, pl.ds(m, DEEP, stride=SLABS), :].astype(BF)


def far(place, deep_q, state, done, mine, their):
    whole = pl.BlockSpec(memory_space=pltpu.VMEM)
    return pl.pallas_call(
        far_body,
        out_shape=tuple(jax.ShapeDtypeStruct((SLOTS, DEEP, DH), BF) for _ in range(SLABS)),
        in_specs=[pl.BlockSpec(memory_space=pltpu.SMEM)] + [whole] * 9,
        out_specs=[whole] * SLABS,
        scratch_shapes=[pltpu.VMEM((SLOTS, DROWS, DH), F32)],
        compiler_params=pltpu.CompilerParams(vmem_limit_bytes=VMEM_BYTES),
        cost_estimate=pl.CostEstimate(
            flops=SLOTS * 4 * DEEP * 3 * DROWS * DH,
            bytes_accessed=SLOTS * DROWS * 8 * DH * 2,
            transcendentals=SLOTS * DEEP * 3 * DROWS,
        ),
        name="far",
    )(place, deep_q, state, done, *mine, *their)


def place_body(place_ref, offsets_ref, *refs):
    bulk, deep, out_ref = refs[:4], refs[4:8], refs[8]
    for m in range(SLABS):
        for slot in range(SLOTS):
            head = head_of(place_ref, m, slot)
            back = from_order(offsets_ref[head], DEEP)
            rows = jnp.dot(back, deep[m][slot], preferred_element_type=F32)
            column = pl.multiple_of(head * DH, DH)
            early = bulk[m][slot]
            out_ref[:, pl.ds(column, DH)] = (early.astype(F32) + rows).astype(BF)


def placed_heads(place, offsets, bulk, deep):
    whole = pl.BlockSpec(memory_space=pltpu.VMEM)
    scalars = pl.BlockSpec(memory_space=pltpu.SMEM)
    return pl.pallas_call(
        place_body,
        out_shape=jax.ShapeDtypeStruct((ROWS, HEADS * DH), BF),
        in_specs=[scalars, scalars] + [whole] * 8,
        out_specs=whole,
        compiler_params=pltpu.CompilerParams(vmem_limit_bytes=VMEM_BYTES),
        cost_estimate=pl.CostEstimate(
            flops=HEADS * 2 * ROWS * DEEP * DH,
            bytes_accessed=2 * ROWS * HEADS * DH * 2,
            transcendentals=0,
        ),
        name="place",
    )(place, offsets, *bulk, *deep)


def halves(value, pieces):
    part = value.shape[1] // pieces
    return [value[:, k * part : k * part + part // 2] for k in range(pieces)]


def swap_pairs(value):
    return jnp.concatenate([value[2:], value[:2]], axis=0)


def half_slots(value, core):
    return jnp.where(core == 0, value[0::2], value[1::2])


def shards(tokens, qkv_weight, offsets):
    inner = lax.axis_index("inner").astype(I32)
    core = lax.axis_index("outer").astype(I32) & 1
    place = jnp.stack([inner, core])
    depth, width = qkv_weight.shape
    half, chunk = ROWS // 2, depth // 4
    upper, lower = tokens[:half], tokens[half:]

    y_upper = flipped(upper, 0, 2)
    z_lower = flipped(lower, 0, 1)
    chunks = [
        lax.dynamic_slice(qkv_weight, ((2 * core + k) * chunk, 0), (chunk, width)) for k in range(2)
    ]
    got = [flipped(piece, 0, 6) for piece in chunks]
    y_lower = flipped(lower, 0, 2)
    z_upper = flipped(upper, 0, 1)
    (qkv,) = project(place, offsets, [tokens], [qkv_weight], [[(0, (0,))]], 0, None, False)
    y_upper, z_lower, got[0], qkv = lax.optimization_barrier((y_upper, z_lower, got[0], qkv))
    d_upper = flipped(y_upper, 0, 1)
    d_lower = flipped(z_lower, 0, 2)
    rest = [flipped(got[0], 1, 0)]
    slabs = [z_upper, z_lower, y_upper, y_lower]
    (qkv,) = project(
        place, offsets, slabs, [qkv_weight], [[(1, (0, 1)), (2, (2, 3))]], 0, qkv, False
    )
    got[1], d_upper, d_lower, qkv = lax.optimization_barrier((got[1], d_upper, d_lower, qkv))
    rest.append(flipped(got[1], 1, 0))
    slabs = [d_upper, d_lower]
    (qkv,) = project(place, offsets, slabs, [qkv_weight], [[(3, (0, 1))]], 0, qkv, False)
    slabs = [tokens, z_upper, z_lower, y_upper, y_lower, d_upper, d_lower]
    qkv, deep_q, deep_kv = project(
        place,
        offsets,
        slabs,
        got + rest,
        [[(0, (0,)), (1, (1, 2))], [(2, (3, 4)), (3, (5, 6))]],
        2,
        qkv,
        True,
    )

    other3 = flipped(swap_pairs(deep_kv), 0, 6)
    found = near(place, offsets, qkv, 0, 2, ())
    kept = jnp.concatenate(halves(deep_kv, 1) + halves(other3, 1), axis=1)
    kept, found = lax.optimization_barrier((kept, found))
    other4 = flipped(kept, 1, 0)
    kept, other, pieces = half_slots(kept, core), half_slots(other4, core), 2
    mine, their = [], []
    for level in range(1, 4):
        kept = jnp.concatenate(halves(kept, pieces) + halves(other, pieces), axis=1)
        pieces *= 2
        if level == 2:
            *bulk, state = near(place, offsets, qkv, 2, 2, found)
            kept, bulk, state = lax.optimization_barrier((kept, bulk, state))
        if level == 3:
            bulk = [bulk[0]] + [flipped(bulk[m], 0, m) for m in range(1, SLABS)]
            done, state = middle(deep_q, state, deep_kv, other3, other4)
            kept, done, state = lax.optimization_barrier((kept, done, state))
        other = flipped(kept, 1 << level, 0)
        mine.append(other)
        their.append(flipped(other, 1, 0))
    deep = far(place, deep_q, state, done, mine, their)
    deep = [deep[0]] + [flipped(deep[m], 0, m) for m in range(1, SLABS)]
    return placed_heads(place, offsets, bulk, deep)


def solution(mesh):
    placed = (P(("outer", "inner"), None), P(None, "inner"), P())
    return jax.shard_map(
        shards, mesh=mesh, in_specs=placed, out_specs=P(("outer", "inner"), None), check_vma=False
    )
```

time: 817 us -> 104 us (0.13)
  waiting for transfers between devices: 594 us -> 39.6 us
  local copies, waits for them, and re-layouts: 127 us -> 7.9 us
  other arithmetic: 36.9 us -> 0.87 us
  matrix products: 29.5 us -> 0 us
  Pallas kernels: 0 us -> 28.8 us
  between operations: 14.5 us -> 0.32 us
  starting transfers between devices: 13.5 us -> 26.2 us
    all_gather x1 -> x0, waiting for transfers between devices: 484 us -> none  [shards(): lax.all_gather(qkv_weight, 'inner', axis=1, tiled=True)]
    ppermute x7 -> x24, waiting for transfers between devices: 109 us -> 39.6 us  [flipped(): lax.ppermute(value, ('outer', 'inner'), [(f, f ^ mask) for f in range(cou...]
    slice x16 -> x6, local copies, waits for them, and re-layouts: 33.3 us -> 2.01 us  [the longest x1 1.05 us: shards(): upper, lower = (tokens[:half], tokens[half:])]
    dot_general x17 -> x0, matrix products: 29.5 us -> none  [the longest x1 12.8 us: shards(): jnp.dot(tokens, lax.all_gather(qkv_weight, 'inner', axis=1, tiled=True),...]
    pallas_call x0 -> x9, Pallas kernels: none -> 28.8 us  [the longest x4 14.9 us: project(): pl.pallas_call(body, out_shape=out_shape, in_specs=[scalars, scalars] + [...]
    reshape x7 -> x0, local copies, waits for them, and re-layouts: 20.1 us -> none  [the longest x6 17.8 us: select_half(): paired = source.reshape((row_count // 2, 2) + source.shape[1:])]
    mul x22 -> x0, local copies, waits for them, and re-layouts: 18.2 us -> none  [the longest x14 12.8 us: fold_level(): coarse_total[:, :, None] * coarse_scale]
    ppermute x7 -> x24, starting transfers between devices: 13.5 us -> 26.2 us  [flipped(): lax.ppermute(value, ('outer', 'inner'), [(f, f ^ mask) for f in range(cou...]
  transfers between devices with their start and end apart: 8 -> 24, of which waited for: 7 -> 15; matrix products, arithmetic and copies ran while one was open for 4% -> 1% of each run, Pallas kernels for 0% -> 19%
where the time goes in v2:
time: 104 us
  waiting for transfers between devices  39.6 us (38%)
  Pallas kernels  28.8 us (28%)
  starting transfers between devices  26.2 us (25%)
  local copies, waits for them, and re-layouts  7.9 us (8%)
    ppermute x24, waiting for transfers between devices, flipped(): lax.ppermute(value, ('outer', 'inner'), [(f, f ^ mask) for f in range(cou...  39.6 us
    ppermute x24, starting transfers between devices, flipped(): lax.ppermute(value, ('outer', 'inner'), [(f, f ^ mask) for f in range(cou...  26.2 us
    pallas_call x4, Pallas kernels, project(): pl.pallas_call(body, out_shape=out_shape, in_specs=[scalars, scalars] + [...  14.9 us
    pallas_call x2, Pallas kernels, near(): pl.pallas_call(lambda *refs: near_body(base, heads, len(carried), *refs),...  6.96 us
    unnamed x34, local copies, waits for them, and re-layouts  3.19 us
    dynamic_slice x1, local copies, waits for them, and re-layouts, shards(): lax.dynamic_slice(qkv_weight, ((2 * core + k) * chunk, 0), (chunk, width))  2.69 us
    pallas_call x1, Pallas kernels, middle(): pl.pallas_call(middle_body, out_shape=(jax.ShapeDtypeStruct((SLOTS, DROWS...  2.57 us
    pallas_call x1, Pallas kernels, far(): pl.pallas_call(far_body, out_shape=tuple((jax.ShapeDtypeStruct((SLOTS, DE...  2.16 us
  transfers between devices with their start and end apart: 24, of which 15 were waited for; matrix products, arithmetic and copies ran while one was open for 1% of the time, Pallas kernels for 19%

profile of v2, /device:TPU:0, one launch (start us, length us, event | category | flops | bytes accessed | tf_op | source)
XLA Modules:
  0.0 103.7 jit_solution(264901734364348355)
XLA Ops:
  0.0 2.7 %constant_dynamic-slice_fusion = (bf16[512,768]{1,0:T(8,128)(2,1)}, bf16[512,768]{1,0:T(8,128)(2,1)}) fusion(bf16[2048,768]{1,0:T(8,128)(2,1)} %refs_4_.1, s32[]{:T(128)S(6)} %select_n.20, s32[]{:T(128)S(6)} %select_n.19), kind=kLoop, calls=%fused_computation.30 | loop fusion | bytes 3145736 | tf_op jit(solution)/shard_map/dynamic_slice | solution.py:370
  2.7 3.1 %collective-permute-start.3 = (bf16[512,768]{1,0:T(8,128)(2,1)}, bf16[512,768]{1,0:T(8,128)(2,1)}, u32[]{:S(2)}, u32[]{:S(2)}) collective-permute-start(bf16[512,768]{1,0:T(8,128)(2,1)} %get-tuple-element.90), channel_id=1, source_target_pairs={{0,6},{1,7},{2,4},{3,5},{4,2},{5,3},{6,0},{7,1},{8,14},{9,15},{10,... | collective-permute-start | bytes 2359304 | tf_op jit(solution)/shard_map/ppermute | solution.py:29
  6.8 1.9 %collective-permute-start.2 = (bf16[128,2048]{1,0:T(8,128)(2,1)}, bf16[128,2048]{1,0:T(8,128)(2,1)S(1)}, u32[]{:S(2)}, u32[]{:S(2)}) collective-permute-start(bf16[128,2048]{1,0:T(8,128)(2,1)} %get-tuple-element.91), channel_id=1, source_target_pairs={{0,1},{1,0},{2,3},{3,2},{4,5},{5,4},{6,7},{7,6},{8,9},{9,8},{10,11... | collective-permute-start | bytes 1572872 | tf_op jit(solution)/shard_map/ppermute | solution.py:29
  10.8 9.8 %collective-permute-done.2.refs_3_.refs_4_ = bf16[128,2048]{1,0:T(8,128)(2,1)S(1)} collective-permute-done((bf16[128,2048]{1,0:T(8,128)(2,1)}, bf16[128,2048]{1,0:T(8,128)(2,1)S(1)}, u32[]{:S(2)}, u32[]{:S(2)}) %collective-permute-start.2) | collective-permute-done | bytes 524320 | tf_op jit(solution)/shard_map/ppermute | solution.py:29
  20.6 1.7 %collective-permute-start = (bf16[128,2048]{1,0:T(8,128)(2,1)}, bf16[128,2048]{1,0:T(8,128)(2,1)S(1)}, u32[]{:S(2)}, u32[]{:S(2)}) collective-permute-start(bf16[128,2048]{1,0:T(8,128)(2,1)} %get-tuple-element.92), channel_id=1, source_target_pairs={{0,1},{1,0},{2,3},{3,2},{4,5},{5,4},{6,7},{7,6},{8,9},{9,8},{10,11... | collective-permute-start | bytes 1572872 | tf_op jit(solution)/shard_map/ppermute | solution.py:29
  22.4 1.9 %copy-done = bf16[2048,768]{1,0:T(8,128)(2,1)S(1)} copy-done((bf16[2048,768]{1,0:T(8,128)(2,1)S(1)}, bf16[2048,768]{1,0:T(8,128)(2,1)}, u32[]{:S(2)}) %copy-start) | copy-done | bytes 3145752
  25.6 1.9 %project.4.refs_7_ = bf16[4,4,256,384]{3,2,1,0:T(8,128)(2,1)S(1)} custom-call(s32[2]{0:T(128)S(1)} %pad_add_fusion.refs_0_.place_ref, s32[16]{0:T(128)S(1)} %copy-done.5, bf16[256,2048]{1,0:T(8,128)(2,1)S(1)} %copy-done.2, bf16[2048,768]{1,0:T(8,128)(2,1)S(1)} %copy-done), custom_call_target="tpu_custom_call" | custom-call | flops 905969664 | bytes 4194304 | tf_op jit(solution)/shard_map/project/pallas_call | solution.py:119
  28.5 6.6 %collective-permute-done.4.refs_5_.refs_6_ = bf16[128,2048]{1,0:T(8,128)(2,1)} collective-permute-done((bf16[128,2048]{1,0:T(8,128)(2,1)}, bf16[128,2048]{1,0:T(8,128)(2,1)}, u32[]{:S(2)}, u32[]{:S(2)}) %collective-permute-start.4) | collective-permute-done | bytes 524320 | tf_op jit(solution)/shard_map/ppermute | solution.py:29
  35.7 3.8 %project.5.refs_5_ = bf16[4,4,256,384]{3,2,1,0:T(8,128)(2,1)S(1)} custom-call(s32[2]{0:T(128)S(1)} %pad_add_fusion.refs_0_.place_ref, s32[16]{0:T(128)S(1)} %copy-done.5, bf16[128,2048]{1,0:T(8,128)(2,1)S(1)} %collective-permute-done.refs_2_.refs_3_, bf16[128,2048]{1,0:T(8,128)(2,1)S(1)} %copy-done.4, ...), custom_call_target="tpu_custom_call", output_to_operand_aliasing={{}: (7, {})} | custom-call | flops 1811939328 | bytes 5242880 | tf_op jit(solution)/shard_map/project/pallas_call | solution.py:119
  40.5 4.1 %collective-permute-done.7.refs_3_.refs_8_ = bf16[128,2048]{1,0:T(8,128)(2,1)S(1)} collective-permute-done((bf16[128,2048]{1,0:T(8,128)(2,1)S(1)}, bf16[128,2048]{1,0:T(8,128)(2,1)S(1)}, u32[]{:S(2)}, u32[]{:S(2)}) %collective-permute-start.7) | collective-permute-done | bytes 524320 | tf_op jit(solution)/shard_map/ppermute | solution.py:29
  44.8 1.9 %project.6.refs_13_ = bf16[4,4,256,384]{3,2,1,0:T(8,128)(2,1)S(1)} custom-call(s32[2]{0:T(128)S(1)} %pad_add_fusion.refs_0_.place_ref, s32[16]{0:T(128)S(1)} %copy-done.5, bf16[128,2048]{1,0:T(8,128)(2,1)S(1)} %collective-permute-done.6.refs_2_.refs_7_, bf16[128,2048]{1,0:T(8,128)(2,1)S(1)} %collective-permute-done.7.refs_3_.refs_8_, ...), custom_call_target="tpu_custom_call", output_to_operand_aliasing={{}: (5, {})} | custom-call | flops 905969664 | bytes 4194304 | tf_op jit(solution)/shard_map/project/pallas_call | solution.py:119
  47.3 7.3 %project.7 = (bf16[4,4,256,384]{3,2,1,0:T(8,128)(2,1)S(1)}, bf16[4,128,128]{2,1,0:T(8,128)(2,1)S(1)}, bf16[4,128,256]{2,1,0:T(8,128)(2,1)S(1)}) custom-call(s32[2]{0:T(128)S(1)} %pad_add_fusion.refs_0_.place_ref, s32[16]{0:T(128)S(1)} %copy-done.5, bf16[256,2048]{1,0:T(8,128)(2,1)S(1)} %copy-done.2, ...), custom_call_target="tpu_custom_call", output_to_operand_aliasing={{0}: (13, {})} | custom-call | flops 3623878656 | bytes 7340032 | tf_op jit(solution)/shard_map/project/pallas_call | solution.py:119
  55.8 3.5 %near.2 = (bf16[4,256,128]{2,1,0:T(8,128)(2,1)S(1)}, bf16[4,256,128]{2,1,0:T(8,128)(2,1)S(1)}, bf16[4,256,128]{2,1,0:T(8,128)(2,1)S(1)}, bf16[4,256,128]{2,1,0:T(8,128)(2,1)S(1)}, f32[4,3,128,128]{3,2,1,0:T(8,128)S(1)}) custom-call(s32[2]{0:T(128)S(1)} %pad_add_fusion.refs_0_.place_ref, s32[16]{0:T(128)S(1)} %copy-done.5, ...), custom_call_target="tpu_custom_call" | custom-call | flops 469762048 | bytes 2097152 | tf_op jit(solution)/shard_map/near/pallas_call | solution.py:200
  59.3 5.9 %collective-permute-done.10.other_ref = bf16[4,128,256]{2,1,0:T(8,128)(2,1)} collective-permute-done((bf16[4,128,256]{2,1,0:T(8,128)(2,1)}, bf16[4,128,256]{2,1,0:T(8,128)(2,1)}, u32[]{:S(2)}, u32[]{:S(2)}) %collective-permute-start.10) | collective-permute-done | bytes 262176 | tf_op jit(solution)/shard_map/ppermute | solution.py:29
  66.3 3.5 %near.3 = (bf16[4,256,128]{2,1,0:T(8,128)(2,1)S(1)}, bf16[4,256,128]{2,1,0:T(8,128)(2,1)S(1)}, bf16[4,256,128]{2,1,0:T(8,128)(2,1)S(1)}, bf16[4,256,128]{2,1,0:T(8,128)(2,1)S(1)}, f32[4,3,128,128]{3,2,1,0:T(8,128)S(1)}) custom-call(s32[2]{0:T(128)S(1)} %pad_add_fusion.refs_0_.place_ref, ...), custom_call_target="tpu_custom_call", output_to_operand_aliasing={{0}: (3, {}), {1}: (4, {}), {2}: (5, {}), {3}: (6, {}), {4}... | custom-call | flops 469762048 | bytes 2097152 | tf_op jit(solution)/shard_map/near/pallas_call | solution.py:200
  69.9 3.6 %collective-permute-start.12 = (bf16[2,128,256]{2,1,0:T(8,128)(2,1)S(1)}, bf16[2,128,256]{2,1,0:T(8,128)(2,1)S(1)}, u32[]{:S(2)}, u32[]{:S(2)}) collective-permute-start(bf16[2,128,256]{2,1,0:T(8,128)(2,1)S(1)} %pad_maximum_fusion.2), channel_id=1, source_target_pairs={{0,16},{1,17},{2,18},{3,19},{4,20},{5,21},{6,22},{7,23},{8,24},{9,... | collective-permute-start | bytes 393224 | tf_op jit(solution)/shard_map/ppermute | solution.py:29
  73.5 4.1 %collective-permute-done.12.mine5 = bf16[2,128,256]{2,1,0:T(8,128)(2,1)S(1)} collective-permute-done((bf16[2,128,256]{2,1,0:T(8,128)(2,1)S(1)}, bf16[2,128,256]{2,1,0:T(8,128)(2,1)S(1)}, u32[]{:S(2)}, u32[]{:S(2)}) %collective-permute-start.12) | collective-permute-done | bytes 131104 | tf_op jit(solution)/shard_map/ppermute | solution.py:29
  79.4 2.6 %middle.1 = (f32[4,96,128]{2,1,0:T(8,128)S(1)}, f32[4,3,32,128]{3,2,1,0:T(8,128)S(1)}) custom-call(bf16[4,128,128]{2,1,0:T(8,128)(2,1)S(1)} %get-tuple-element.77.q_ref, f32[4,3,128,128]{3,2,1,0:T(8,128)S(1)} %get-tuple-element.79.near_ref, bf16[4,128,256]{2,1,0:T(8,128)(2,1)S(1)} %get-tuple-element.55.own_ref, ...), custom_call_target="tpu_custom_call" | custom-call | flops 100663296 | bytes 1310720 | tf_op jit(solution)/shard_map/middle/pallas_call | solution.py:260
  83.1 3.1 %collective-permute-start.17 = (bf16[2,128,256]{2,1,0:T(8,128)(2,1)S(1)}, bf16[2,128,256]{2,1,0:T(8,128)(2,1)S(1)}, u32[]{:S(2)}, u32[]{:S(2)}) collective-permute-start(bf16[2,128,256]{2,1,0:T(8,128)(2,1)S(1)} %constant_dynamic-update-slice_fusion.8), channel_id=1, source_target_pairs={{0,64},{1,65},{2,66},{3,67},{4,68},{5,69},{6,70},{7,71},{8,72},{9,... | collective-permute-start | bytes 393224 | tf_op jit(solution)/shard_map/ppermute | solution.py:29
  87.3 2.4 %collective-permute-start.15 = (bf16[4,256,128]{2,1,0:T(8,128)(2,1)S(1)}, bf16[4,256,128]{2,1,0:T(8,128)(2,1)S(1)}, u32[]{:S(2)}, u32[]{:S(2)}) collective-permute-start(bf16[4,256,128]{2,1,0:T(8,128)(2,1)S(1)} %get-tuple-element.76), channel_id=1, source_target_pairs={{0,3},{1,2},{2,1},{3,0},{4,7},{5,6},{6,5},{7,4},{8,11},{9,10},{10,... | collective-permute-start | bytes 786440 | tf_op jit(solution)/shard_map/ppermute | solution.py:29
  91.3 2.2 %far.1 = (bf16[4,32,128]{2,1,0:T(8,128)(2,1)S(1)}, bf16[4,32,128]{2,1,0:T(8,128)(2,1)S(1)}, bf16[4,32,128]{2,1,0:T(8,128)(2,1)S(1)}, bf16[4,32,128]{2,1,0:T(8,128)(2,1)S(1)}) custom-call(s32[2]{0:T(128)S(1)} %pad_add_fusion.refs_0_.place_ref, bf16[4,128,128]{2,1,0:T(8,128)(2,1)S(1)} %get-tuple-element.77.q_ref, ...), custom_call_target="tpu_custom_call" | custom-call | flops 25165824 | bytes 1048576 | tf_op jit(solution)/shard_map/far/pallas_call | solution.py:300
  94.6 2.4 %collective-permute-start.23 = (bf16[4,32,128]{2,1,0:T(8,128)(2,1)S(1)}, bf16[4,32,128]{2,1,0:T(8,128)(2,1)S(1)}, u32[]{:S(2)}, u32[]{:S(2)}) collective-permute-start(bf16[4,32,128]{2,1,0:T(8,128)(2,1)S(1)} %get-tuple-element.88), channel_id=1, source_target_pairs={{0,3},{1,2},{2,1},{3,0},{4,7},{5,6},{6,5},{7,4},{8,11},{9,10},{10,... | collective-permute-start | bytes 98312 | tf_op jit(solution)/shard_map/ppermute | solution.py:29
  97.0 3.9 %collective-permute-done.15.refs_3_ = bf16[4,256,128]{2,1,0:T(8,128)(2,1)S(1)} collective-permute-done((bf16[4,256,128]{2,1,0:T(8,128)(2,1)S(1)}, bf16[4,256,128]{2,1,0:T(8,128)(2,1)S(1)}, u32[]{:S(2)}, u32[]{:S(2)}) %collective-permute-start.15) | collective-permute-done | bytes 262176 | tf_op jit(solution)/shard_map/ppermute | solution.py:29
  101.5 2.1 %place.1 = bf16[256,2048]{1,0:T(8,128)(2,1)} custom-call(s32[2]{0:T(128)S(1)} %pad_add_fusion.refs_0_.place_ref, s32[16]{0:T(128)S(1)} %copy-done.5, bf16[4,256,128]{2,1,0:T(8,128)(2,1)S(1)} %get-tuple-element.73.refs_0_, bf16[4,256,128]{2,1,0:T(8,128)(2,1)S(1)} %collective-permute-done.13.refs_1_, bf16[4,256,128]{2,1,0:T(8,128)(2,1)S(1)} %collective-permute-done.14.refs_2_, ...), custom_call_target="tpu_custom_call" | custom-call | flops 33554432 | bytes 2097152 | tf_op jit(solution)/shard_map/place/pallas_call | solution.py:331
  (82 shorter events, 17.3 us)
Async XLA Ops:
  2.7 24.8 %collective-permute-start.3 = (bf16[512,768]{1,0:T(8,128)(2,1)}, bf16[512,768]{1,0:T(8,128)(2,1)}, u32[]{:S(2)}, u32[]{:S(2)}) collective-permute-start(bf16[512,768]{1,0:T(8,128)(2,1)} %get-tuple-element.90), channel_id=1, source_target_pairs={{0,6},{1,7},{2,4},{3,5},{4,2},{5,3},{6,0},{7,1},{8,14},{9,15},{10,... | collective-permute-start | bytes 2359304 | tf_op jit(solution)/shard_map/ppermute | solution.py:29
  6.8 13.8 %collective-permute-start.2 = (bf16[128,2048]{1,0:T(8,128)(2,1)}, bf16[128,2048]{1,0:T(8,128)(2,1)S(1)}, u32[]{:S(2)}, u32[]{:S(2)}) collective-permute-start(bf16[128,2048]{1,0:T(8,128)(2,1)} %get-tuple-element.91), channel_id=1, source_target_pairs={{0,1},{1,0},{2,3},{3,2},{4,5},{5,4},{6,7},{7,6},{8,9},{9,8},{10,11... | collective-permute-start | bytes 1572872 | tf_op jit(solution)/shard_map/ppermute | solution.py:29
  8.8 18.8 %collective-permute-start.1 = (bf16[128,2048]{1,0:T(8,128)(2,1)}, bf16[128,2048]{1,0:T(8,128)(2,1)}, u32[]{:S(2)}, u32[]{:S(2)}) collective-permute-start(bf16[128,2048]{1,0:T(8,128)(2,1)} %get-tuple-element.92), channel_id=1, source_target_pairs={{0,2},{1,3},{2,0},{3,1},{4,6},{5,7},{6,4},{7,5},{8,10},{9,11},{10,... | collective-permute-start | bytes 1572872 | tf_op jit(solution)/shard_map/ppermute | solution.py:29
  8.9 31.6 %collective-permute-start.5 = (bf16[512,768]{1,0:T(8,128)(2,1)}, bf16[512,768]{1,0:T(8,128)(2,1)}, u32[]{:S(2)}, u32[]{:S(2)}) collective-permute-start(bf16[512,768]{1,0:T(8,128)(2,1)} %get-tuple-element.89), channel_id=1, source_target_pairs={{0,6},{1,7},{2,4},{3,5},{4,2},{5,3},{6,0},{7,1},{8,14},{9,15},{10,... | collective-permute-start | bytes 2359304 | tf_op jit(solution)/shard_map/ppermute | solution.py:29
  10.0 25.2 %collective-permute-start.4 = (bf16[128,2048]{1,0:T(8,128)(2,1)}, bf16[128,2048]{1,0:T(8,128)(2,1)}, u32[]{:S(2)}, u32[]{:S(2)}) collective-permute-start(bf16[128,2048]{1,0:T(8,128)(2,1)} %get-tuple-element.91), channel_id=1, source_target_pairs={{0,2},{1,3},{2,0},{3,1},{4,6},{5,7},{6,4},{7,5},{8,10},{9,11},{10,... | collective-permute-start | bytes 1572872 | tf_op jit(solution)/shard_map/ppermute | solution.py:29
  20.6 15.1 %collective-permute-start = (bf16[128,2048]{1,0:T(8,128)(2,1)}, bf16[128,2048]{1,0:T(8,128)(2,1)S(1)}, u32[]{:S(2)}, u32[]{:S(2)}) collective-permute-start(bf16[128,2048]{1,0:T(8,128)(2,1)} %get-tuple-element.92), channel_id=1, source_target_pairs={{0,1},{1,0},{2,3},{3,2},{4,5},{5,4},{6,7},{7,6},{8,9},{9,8},{10,11... | collective-permute-start | bytes 1572872 | tf_op jit(solution)/shard_map/ppermute | solution.py:29
  27.5 17.0 %collective-permute-start.7 = (bf16[128,2048]{1,0:T(8,128)(2,1)S(1)}, bf16[128,2048]{1,0:T(8,128)(2,1)S(1)}, u32[]{:S(2)}, u32[]{:S(2)}) collective-permute-start(bf16[128,2048]{1,0:T(8,128)(2,1)S(1)} %copy-done.4), channel_id=1, source_target_pairs={{0,2},{1,3},{2,0},{3,1},{4,6},{5,7},{6,4},{7,5},{8,10},{9,11},{10,... | collective-permute-start | bytes 1572872 | tf_op jit(solution)/shard_map/ppermute | solution.py:29
  27.8 17.1 %collective-permute-start.6 = (bf16[128,2048]{1,0:T(8,128)(2,1)}, bf16[128,2048]{1,0:T(8,128)(2,1)S(1)}, u32[]{:S(2)}, u32[]{:S(2)}) collective-permute-start(bf16[128,2048]{1,0:T(8,128)(2,1)} %collective-permute-done.1.refs_4_.refs_5_), channel_id=1, source_target_pairs={{0,1},{1,0},{2,3},{3,2},{4,5},{5,4},{6,7},{7,6},{8,9},{9,8},{10,11... | collective-permute-start | bytes 1572872 | tf_op jit(solution)/shard_map/ppermute | solution.py:29
  35.2 11.6 %collective-permute-start.8 = (bf16[512,768]{1,0:T(8,128)(2,1)}, bf16[512,768]{1,0:T(8,128)(2,1)S(1)}, u32[]{:S(2)}, u32[]{:S(2)}) collective-permute-start(bf16[512,768]{1,0:T(8,128)(2,1)} %collective-permute-done.3.refs_9_), channel_id=1, source_target_pairs={{0,8},{1,9},{2,10},{3,11},{4,12},{5,13},{6,14},{7,15},{8,0},{9,1},... | collective-permute-start | bytes 2359304 | tf_op jit(solution)/shard_map/ppermute | solution.py:29
  44.8 2.5 %collective-permute-start.9 = (bf16[512,768]{1,0:T(8,128)(2,1)}, bf16[512,768]{1,0:T(8,128)(2,1)S(1)}, u32[]{:S(2)}, u32[]{:S(2)}) collective-permute-start(bf16[512,768]{1,0:T(8,128)(2,1)} %collective-permute-done.5.refs_10_), channel_id=1, source_target_pairs={{0,8},{1,9},{2,10},{3,11},{4,12},{5,13},{6,14},{7,15},{8,0},{9,1},... | collective-permute-start | bytes 2359304 | tf_op jit(solution)/shard_map/ppermute | solution.py:29
  55.4 9.9 %collective-permute-start.10 = (bf16[4,128,256]{2,1,0:T(8,128)(2,1)}, bf16[4,128,256]{2,1,0:T(8,128)(2,1)}, u32[]{:S(2)}, u32[]{:S(2)}) collective-permute-start(bf16[4,128,256]{2,1,0:T(8,128)(2,1)} %pad_maximum_fusion), channel_id=1, source_target_pairs={{0,6},{1,7},{2,4},{3,5},{4,2},{5,3},{6,0},{7,1},{8,14},{9,15},{10,... | collective-permute-start | bytes 786440 | tf_op jit(solution)/shard_map/ppermute | solution.py:29
  66.2 3.6 %collective-permute-start.11 = (bf16[4,128,256]{2,1,0:T(8,128)(2,1)S(1)}, bf16[4,128,256]{2,1,0:T(8,128)(2,1)S(1)}, u32[]{:S(2)}, u32[]{:S(2)}) collective-permute-start(bf16[4,128,256]{2,1,0:T(8,128)(2,1)S(1)} %pad_maximum_fusion.1), channel_id=1, source_target_pairs={{0,8},{1,9},{2,10},{3,11},{4,12},{5,13},{6,14},{7,15},{8,0},{9,1},... | collective-permute-start | bytes 786440 | tf_op jit(solution)/shard_map/ppermute | solution.py:29
  69.9 7.7 %collective-permute-start.12 = (bf16[2,128,256]{2,1,0:T(8,128)(2,1)S(1)}, bf16[2,128,256]{2,1,0:T(8,128)(2,1)S(1)}, u32[]{:S(2)}, u32[]{:S(2)}) collective-permute-start(bf16[2,128,256]{2,1,0:T(8,128)(2,1)S(1)} %pad_maximum_fusion.2), channel_id=1, source_target_pairs={{0,16},{1,17},{2,18},{3,19},{4,20},{5,21},{6,22},{7,23},{8,24},{9,... | collective-permute-start | bytes 393224 | tf_op jit(solution)/shard_map/ppermute | solution.py:29
  77.7 5.4 %collective-permute-start.16 = (bf16[2,128,256]{2,1,0:T(8,128)(2,1)S(1)}, bf16[2,128,256]{2,1,0:T(8,128)(2,1)S(1)}, u32[]{:S(2)}, u32[]{:S(2)}) collective-permute-start(bf16[2,128,256]{2,1,0:T(8,128)(2,1)S(1)} %constant_dynamic-update-slice_fusion), channel_id=1, source_target_pairs={{0,32},{1,33},{2,34},{3,35},{4,36},{5,37},{6,38},{7,39},{8,40},{9,... | collective-permute-start | bytes 393224 | tf_op jit(solution)/shard_map/ppermute | solution.py:29
  79.3 10.4 %collective-permute-start.18 = (bf16[2,128,256]{2,1,0:T(8,128)(2,1)S(1)}, bf16[2,128,256]{2,1,0:T(8,128)(2,1)S(1)}, u32[]{:S(2)}, u32[]{:S(2)}) collective-permute-start(bf16[2,128,256]{2,1,0:T(8,128)(2,1)S(1)} %collective-permute-done.12.mine5), channel_id=1, source_target_pairs={{0,8},{1,9},{2,10},{3,11},{4,12},{5,13},{6,14},{7,15},{8,0},{9,1},... | collective-permute-start | bytes 393224 | tf_op jit(solution)/shard_map/ppermute | solution.py:29
  83.1 6.6 %collective-permute-start.17 = (bf16[2,128,256]{2,1,0:T(8,128)(2,1)S(1)}, bf16[2,128,256]{2,1,0:T(8,128)(2,1)S(1)}, u32[]{:S(2)}, u32[]{:S(2)}) collective-permute-start(bf16[2,128,256]{2,1,0:T(8,128)(2,1)S(1)} %constant_dynamic-update-slice_fusion.8), channel_id=1, source_target_pairs={{0,64},{1,65},{2,66},{3,67},{4,68},{5,69},{6,70},{7,71},{8,72},{9,... | collective-permute-start | bytes 393224 | tf_op jit(solution)/shard_map/ppermute | solution.py:29
  86.3 8.4 %collective-permute-start.13 = (bf16[4,256,128]{2,1,0:T(8,128)(2,1)S(1)}, bf16[4,256,128]{2,1,0:T(8,128)(2,1)S(1)}, u32[]{:S(2)}, u32[]{:S(2)}) collective-permute-start(bf16[4,256,128]{2,1,0:T(8,128)(2,1)S(1)} %get-tuple-element.74), channel_id=1, source_target_pairs={{0,1},{1,0},{2,3},{3,2},{4,5},{5,4},{6,7},{7,6},{8,9},{9,8},{10,11... | collective-permute-start | bytes 786440 | tf_op jit(solution)/shard_map/ppermute | solution.py:29
  87.3 9.7 %collective-permute-start.14 = (bf16[4,256,128]{2,1,0:T(8,128)(2,1)S(1)}, bf16[4,256,128]{2,1,0:T(8,128)(2,1)S(1)}, u32[]{:S(2)}, u32[]{:S(2)}) collective-permute-start(bf16[4,256,128]{2,1,0:T(8,128)(2,1)S(1)} %get-tuple-element.75), channel_id=1, source_target_pairs={{0,2},{1,3},{2,0},{3,1},{4,6},{5,7},{6,4},{7,5},{8,10},{9,11},{10,... | collective-permute-start | bytes 786440 | tf_op jit(solution)/shard_map/ppermute | solution.py:29
  87.3 13.5 %collective-permute-start.15 = (bf16[4,256,128]{2,1,0:T(8,128)(2,1)S(1)}, bf16[4,256,128]{2,1,0:T(8,128)(2,1)S(1)}, u32[]{:S(2)}, u32[]{:S(2)}) collective-permute-start(bf16[4,256,128]{2,1,0:T(8,128)(2,1)S(1)} %get-tuple-element.76), channel_id=1, source_target_pairs={{0,3},{1,2},{2,1},{3,0},{4,7},{5,6},{6,5},{7,4},{8,11},{9,10},{10,... | collective-permute-start | bytes 786440 | tf_op jit(solution)/shard_map/ppermute | solution.py:29
  89.7 1.3 %collective-permute-start.19 = (bf16[2,128,256]{2,1,0:T(8,128)(2,1)S(1)}, bf16[2,128,256]{2,1,0:T(8,128)(2,1)S(1)}, u32[]{:S(2)}, u32[]{:S(2)}) collective-permute-start(bf16[2,128,256]{2,1,0:T(8,128)(2,1)S(1)} %collective-permute-done.16.mine6), channel_id=1, source_target_pairs={{0,8},{1,9},{2,10},{3,11},{4,12},{5,13},{6,14},{7,15},{8,0},{9,1},... | collective-permute-start | bytes 393224 | tf_op jit(solution)/shard_map/ppermute | solution.py:29
  89.8 1.5 %collective-permute-start.20 = (bf16[2,128,256]{2,1,0:T(8,128)(2,1)S(1)}, bf16[2,128,256]{2,1,0:T(8,128)(2,1)S(1)}, u32[]{:S(2)}, u32[]{:S(2)}) collective-permute-start(bf16[2,128,256]{2,1,0:T(8,128)(2,1)S(1)} %collective-permute-done.17.mine7), channel_id=1, source_target_pairs={{0,8},{1,9},{2,10},{3,11},{4,12},{5,13},{6,14},{7,15},{8,0},{9,1},... | collective-permute-start | bytes 393224 | tf_op jit(solution)/shard_map/ppermute | solution.py:29
  93.4 7.5 %collective-permute-start.21 = (bf16[4,32,128]{2,1,0:T(8,128)(2,1)S(1)}, bf16[4,32,128]{2,1,0:T(8,128)(2,1)S(1)}, u32[]{:S(2)}, u32[]{:S(2)}) collective-permute-start(bf16[4,32,128]{2,1,0:T(8,128)(2,1)S(1)} %get-tuple-element.86), channel_id=1, source_target_pairs={{0,1},{1,0},{2,3},{3,2},{4,5},{5,4},{6,7},{7,6},{8,9},{9,8},{10,11... | collective-permute-start | bytes 98312 | tf_op jit(solution)/shard_map/ppermute | solution.py:29
  94.6 6.4 %collective-permute-start.22 = (bf16[4,32,128]{2,1,0:T(8,128)(2,1)S(1)}, bf16[4,32,128]{2,1,0:T(8,128)(2,1)S(1)}, u32[]{:S(2)}, u32[]{:S(2)}) collective-permute-start(bf16[4,32,128]{2,1,0:T(8,128)(2,1)S(1)} %get-tuple-element.87), channel_id=1, source_target_pairs={{0,2},{1,3},{2,0},{3,1},{4,6},{5,7},{6,4},{7,5},{8,10},{9,11},{10,... | collective-permute-start | bytes 98312 | tf_op jit(solution)/shard_map/ppermute | solution.py:29
  94.6 6.9 %collective-permute-start.23 = (bf16[4,32,128]{2,1,0:T(8,128)(2,1)S(1)}, bf16[4,32,128]{2,1,0:T(8,128)(2,1)S(1)}, u32[]{:S(2)}, u32[]{:S(2)}) collective-permute-start(bf16[4,32,128]{2,1,0:T(8,128)(2,1)S(1)} %get-tuple-element.88), channel_id=1, source_target_pairs={{0,3},{1,2},{2,1},{3,0},{4,7},{5,6},{6,5},{7,4},{8,11},{9,10},{10,... | collective-permute-start | bytes 98312 | tf_op jit(solution)/shard_map/ppermute | solution.py:29
  (6 other events, 35.1 us)

commit v3 on v2

--- a/solution.py
+++ b/solution.py
@@ -82,15 +82,20 @@
                 qkv_ref[m, first_slot + k] = found.astype(BF)
 
 
-def spread_body(qkv_ref, deep_q_ref, deep_kv_ref, spread):
+def interleave():
+    row = lax.broadcasted_iota(I32, (DROWS, DROWS), 0)
+    column = lax.broadcasted_iota(I32, (DROWS, DROWS), 1)
+    return jnp.where((row & 3) * DEEP + (row >> 2) == column, 1.0, 0.0).astype(BF)
+
+
+def spread_body(qkv_ref, deep_q_ref, low_ref, high_ref, low_sent_ref, high_sent_ref):
+    half = DROWS // 2
     for slot in range(SLOTS):
-        for part in range(3):
-            for m in range(SLABS):
-                piece = qkv_ref[m, slot, :DEEP, part * DH : (part + 1) * DH].astype(F32)
-                spread[slot, part, pl.ds(m, DEEP, stride=SLABS), :] = piece
-        deep_q_ref[slot] = spread[slot, 0].astype(BF)
-        deep_kv_ref[slot, :, :DH] = spread[slot, 1].astype(BF)
-        deep_kv_ref[slot, :, DH:] = spread[slot, 2].astype(BF)
+        rows = jnp.concatenate([qkv_ref[m, slot, :DEEP] for m in range(SLABS)], axis=0)
+        rows = jnp.dot(interleave(), rows, preferred_element_type=F32).astype(BF)
+        deep_q_ref[slot] = rows[:, :DH]
+        low_ref[slot], high_ref[slot] = rows[:half, DH:], rows[half:, DH:]
+        low_sent_ref[slot ^ 2], high_sent_ref[slot ^ 2] = rows[:half, DH:], rows[half:, DH:]
 
 
 def project(place, offsets, xs, ws, groups, first_slot, carried, last_deep):
@@ -101,18 +106,16 @@
     if last_deep:
         out_shape += [
             jax.ShapeDtypeStruct((SLOTS, DROWS, DH), BF),
-            jax.ShapeDtypeStruct((SLOTS, DROWS, 2 * DH), BF),
-        ]
-        scratch.append(pltpu.VMEM((SLOTS, 3, DROWS, DH), F32))
+        ] + [jax.ShapeDtypeStruct((SLOTS, DROWS // 2, 2 * DH), BF) for _ in range(4)]
     extra = [] if carried is None else [carried]
 
     def body(*refs):
         if not last_deep:
             project_body(groups, len(xs), len(ws), first_slot, 0, *refs)
             return
-        *front, qkv_ref, deep_q_ref, deep_kv_ref, orders, spread = refs
+        *front, qkv_ref, deep_q_ref, low, high, low_sent, high_sent, orders = refs
         project_body(groups, len(xs), len(ws), first_slot, 0, *front, qkv_ref, orders)
-        spread_body(qkv_ref, deep_q_ref, deep_kv_ref, spread)
+        spread_body(qkv_ref, deep_q_ref, low, high, low_sent, high_sent)
 
     slabs = sum(len(members) for members in groups)
     depth, width = xs[0].shape[1], ws[0].shape[1]
@@ -348,10 +351,6 @@
     return [value[:, k * part : k * part + part // 2] for k in range(pieces)]
 
 
-def swap_pairs(value):
-    return jnp.concatenate([value[2:], value[:2]], axis=0)
-
-
 def half_slots(value, core):
     return jnp.where(core == 0, value[0::2], value[1::2])
 
@@ -386,7 +385,7 @@
     slabs = [d_upper, d_lower]
     (qkv,) = project(place, offsets, slabs, [qkv_weight], [[(3, (0, 1))]], 0, qkv, False)
     slabs = [tokens, z_upper, z_lower, y_upper, y_lower, d_upper, d_lower]
-    qkv, deep_q, deep_kv = project(
+    qkv, deep_q, low, high, low_sent, high_sent = project(
         place,
         offsets,
         slabs,
@@ -397,11 +396,13 @@
         True,
     )
 
-    other3 = flipped(swap_pairs(deep_kv), 0, 6)
+    low_other = flipped(low_sent, 0, 6)
     found = near(place, offsets, qkv, 0, 2, ())
-    kept = jnp.concatenate(halves(deep_kv, 1) + halves(other3, 1), axis=1)
+    kept = jnp.concatenate([low, low_other], axis=1)
     kept, found = lax.optimization_barrier((kept, found))
     other4 = flipped(kept, 1, 0)
+    other4, found, high_sent = lax.optimization_barrier((other4, found, high_sent))
+    high_other = flipped(high_sent, 0, 6)
     kept, other, pieces = half_slots(kept, core), half_slots(other4, core), 2
     mine, their = [], []
     for level in range(1, 4):
@@ -412,9 +413,13 @@
             kept, bulk, state = lax.optimization_barrier((kept, bulk, state))
         if level == 3:
             bulk = [bulk[0]] + [flipped(bulk[m], 0, m) for m in range(1, SLABS)]
+            deep_kv = jnp.concatenate([low, high], axis=1)
+            other3 = jnp.concatenate([low_other, high_other], axis=1)
             done, state = middle(deep_q, state, deep_kv, other3, other4)
             kept, done, state = lax.optimization_barrier((kept, done, state))
         other = flipped(kept, 1 << level, 0)
+        if level == 3:
+            other, bulk[1], bulk[2] = lax.optimization_barrier((other, bulk[1], bulk[2]))
         mine.append(other)
         their.append(flipped(other, 1, 0))
     deep = far(place, deep_q, state, done, mine, their)

time: 104 us -> 99 us (0.952)
  waiting for transfers between devices: 39.6 us -> 33.9 us
  other arithmetic: 0.87 us -> 1.98 us
    ppermute x24 -> x25, waiting for transfers between devices: 39.6 us -> 33.9 us  [flipped(): lax.ppermute(value, ('outer', 'inner'), [(f, f ^ mask) for f in range(cou...]
    concatenate x2, other arithmetic: 0.75 us -> 1.87 us  [the longest x1 0.94 us: shards(): deep_kv = jnp.concatenate([low, high], axis=1)]
    unnamed x34 -> x38, local copies, waits for them, and re-layouts: 3.19 us -> 3.85 us
    ppermute x24 -> x25, starting transfers between devices: 26.2 us -> 26.3 us  [flipped(): lax.ppermute(value, ('outer', 'inner'), [(f, f ^ mask) for f in range(cou...]
  transfers between devices with their start and end apart: 24 -> 25, of which waited for: 15 -> 15; matrix products, arithmetic and copies ran while one was open for 1% -> 2% of each run, Pallas kernels for 19% -> 19%
where the time goes in v3:
time: 99 us; the launch traced here: 98.7 us
  waiting for transfers between devices  33.9 us (34%)
  Pallas kernels  28.5 us (29%)
  starting transfers between devices  26.3 us (27%)
  local copies, waits for them, and re-layouts  7.61 us (8%)
  other arithmetic  1.98 us (2%)
    ppermute x25, waiting for transfers between devices, flipped(): lax.ppermute(value, ('outer', 'inner'), [(f, f ^ mask) for f in range(cou...  33.9 us
    ppermute x25, starting transfers between devices, flipped(): lax.ppermute(value, ('outer', 'inner'), [(f, f ^ mask) for f in range(cou...  26.3 us
    pallas_call x4, Pallas kernels, project(): pl.pallas_call(body, out_shape=out_shape, in_specs=[scalars, scalars] + [...  15.7 us
    pallas_call x2, Pallas kernels, near(): pl.pallas_call(lambda *refs: near_body(base, heads, len(carried), *refs),...  6.95 us
    unnamed x38, local copies, waits for them, and re-layouts  3.85 us
    dynamic_slice x1, local copies, waits for them, and re-layouts, shards(): lax.dynamic_slice(qkv_weight, ((2 * core + k) * chunk, 0), (chunk, width))  2.7 us
    pallas_call x1, Pallas kernels, far(): pl.pallas_call(far_body, out_shape=tuple((jax.ShapeDtypeStruct((SLOTS, DE...  2.16 us
    pallas_call x1, Pallas kernels, placed_heads(): pl.pallas_call(place_body, out_shape=jax.ShapeDtypeStruct((ROWS, HEADS *...  2.15 us
  transfers between devices with their start and end apart: 25, of which 15 were waited for; matrix products, arithmetic and copies ran while one was open for 2% of the time, Pallas kernels for 19%

profile of v3, /device:TPU:0, one launch (start us, length us, event | category | flops | bytes accessed | tf_op | source)
XLA Modules:
  0.0 98.7 jit_solution(12546178890959255835)
XLA Ops:
  0.0 2.7 %constant_dynamic-slice_fusion = (bf16[512,768]{1,0:T(8,128)(2,1)}, bf16[512,768]{1,0:T(8,128)(2,1)}) fusion(bf16[2048,768]{1,0:T(8,128)(2,1)} %refs_4_.1, s32[]{:T(128)S(6)} %select_n.20, s32[]{:T(128)S(6)} %select_n.19), kind=kLoop, calls=%fused_computation.31 | loop fusion | bytes 3145736 | tf_op jit(solution)/shard_map/dynamic_slice | solution.py:369
  2.7 3.1 %collective-permute-start.3 = (bf16[512,768]{1,0:T(8,128)(2,1)}, bf16[512,768]{1,0:T(8,128)(2,1)}, u32[]{:S(2)}, u32[]{:S(2)}) collective-permute-start(bf16[512,768]{1,0:T(8,128)(2,1)} %get-tuple-element.116), channel_id=1, source_target_pairs={{0,6},{1,7},{2,4},{3,5},{4,2},{5,3},{6,0},{7,1},{8,14},{9,15},{10,... | collective-permute-start | bytes 2359304 | tf_op jit(solution)/shard_map/ppermute | solution.py:29
  6.8 1.9 %collective-permute-start.2 = (bf16[128,2048]{1,0:T(8,128)(2,1)}, bf16[128,2048]{1,0:T(8,128)(2,1)S(1)}, u32[]{:S(2)}, u32[]{:S(2)}) collective-permute-start(bf16[128,2048]{1,0:T(8,128)(2,1)} %get-tuple-element.117), channel_id=1, source_target_pairs={{0,1},{1,0},{2,3},{3,2},{4,5},{5,4},{6,7},{7,6},{8,9},{9,8},{10,11... | collective-permute-start | bytes 1572872 | tf_op jit(solution)/shard_map/ppermute | solution.py:29
  10.8 9.8 %collective-permute-done.2.refs_3_.refs_4_ = bf16[128,2048]{1,0:T(8,128)(2,1)S(1)} collective-permute-done((bf16[128,2048]{1,0:T(8,128)(2,1)}, bf16[128,2048]{1,0:T(8,128)(2,1)S(1)}, u32[]{:S(2)}, u32[]{:S(2)}) %collective-permute-start.2) | collective-permute-done | bytes 524320 | tf_op jit(solution)/shard_map/ppermute | solution.py:29
  20.6 1.7 %collective-permute-start = (bf16[128,2048]{1,0:T(8,128)(2,1)}, bf16[128,2048]{1,0:T(8,128)(2,1)S(1)}, u32[]{:S(2)}, u32[]{:S(2)}) collective-permute-start(bf16[128,2048]{1,0:T(8,128)(2,1)} %get-tuple-element.118), channel_id=1, source_target_pairs={{0,1},{1,0},{2,3},{3,2},{4,5},{5,4},{6,7},{7,6},{8,9},{9,8},{10,11... | collective-permute-start | bytes 1572872 | tf_op jit(solution)/shard_map/ppermute | solution.py:29
  22.4 1.9 %copy-done = bf16[2048,768]{1,0:T(8,128)(2,1)S(1)} copy-done((bf16[2048,768]{1,0:T(8,128)(2,1)S(1)}, bf16[2048,768]{1,0:T(8,128)(2,1)}, u32[]{:S(2)}) %copy-start) | copy-done | bytes 3145752
  25.6 1.9 %project.4.refs_7_ = bf16[4,4,256,384]{3,2,1,0:T(8,128)(2,1)S(1)} custom-call(s32[2]{0:T(128)S(1)} %pad_add_fusion.refs_0_.place_ref, s32[16]{0:T(128)S(1)} %copy-done.5, bf16[256,2048]{1,0:T(8,128)(2,1)S(1)} %copy-done.2, bf16[2048,768]{1,0:T(8,128)(2,1)S(1)} %copy-done), custom_call_target="tpu_custom_call" | custom-call | flops 905969664 | bytes 4194304 | tf_op jit(solution)/shard_map/project/pallas_call | solution.py:122
  28.6 6.6 %collective-permute-done.4.refs_5_.refs_6_ = bf16[128,2048]{1,0:T(8,128)(2,1)} collective-permute-done((bf16[128,2048]{1,0:T(8,128)(2,1)}, bf16[128,2048]{1,0:T(8,128)(2,1)}, u32[]{:S(2)}, u32[]{:S(2)}) %collective-permute-start.4) | collective-permute-done | bytes 524320 | tf_op jit(solution)/shard_map/ppermute | solution.py:29
  35.7 3.8 %project.5.refs_5_ = bf16[4,4,256,384]{3,2,1,0:T(8,128)(2,1)S(1)} custom-call(s32[2]{0:T(128)S(1)} %pad_add_fusion.refs_0_.place_ref, s32[16]{0:T(128)S(1)} %copy-done.5, bf16[128,2048]{1,0:T(8,128)(2,1)S(1)} %collective-permute-done.refs_2_.refs_3_, bf16[128,2048]{1,0:T(8,128)(2,1)S(1)} %copy-done.4, ...), custom_call_target="tpu_custom_call", output_to_operand_aliasing={{}: (7, {})} | custom-call | flops 1811939328 | bytes 5242880 | tf_op jit(solution)/shard_map/project/pallas_call | solution.py:122
  40.5 4.0 %collective-permute-done.7.refs_3_.refs_8_ = bf16[128,2048]{1,0:T(8,128)(2,1)S(1)} collective-permute-done((bf16[128,2048]{1,0:T(8,128)(2,1)S(1)}, bf16[128,2048]{1,0:T(8,128)(2,1)S(1)}, u32[]{:S(2)}, u32[]{:S(2)}) %collective-permute-start.7) | collective-permute-done | bytes 524320 | tf_op jit(solution)/shard_map/ppermute | solution.py:29
  44.8 1.9 %project.6.refs_13_ = bf16[4,4,256,384]{3,2,1,0:T(8,128)(2,1)S(1)} custom-call(s32[2]{0:T(128)S(1)} %pad_add_fusion.refs_0_.place_ref, s32[16]{0:T(128)S(1)} %copy-done.5, bf16[128,2048]{1,0:T(8,128)(2,1)S(1)} %collective-permute-done.6.refs_2_.refs_7_, bf16[128,2048]{1,0:T(8,128)(2,1)S(1)} %collective-permute-done.7.refs_3_.refs_8_, ...), custom_call_target="tpu_custom_call", output_to_operand_aliasing={{}: (5, {})} | custom-call | flops 905969664 | bytes 4194304 | tf_op jit(solution)/shard_map/project/pallas_call | solution.py:122
  47.3 8.0 %project.7 = (bf16[4,4,256,384]{3,2,1,0:T(8,128)(2,1)S(1)}, bf16[4,128,128]{2,1,0:T(8,128)(2,1)S(1)}, bf16[4,64,256]{2,1,0:T(8,128)(2,1)S(1)}, bf16[4,64,256]{2,...) custom-call(s32[2]{0:T(128)S(1)} %pad_add_fusion.refs_0_.place_ref, ...), custom_call_target="tpu_custom_call", output_to_operand_aliasing={{0}: (13, {})} | custom-call | flops 3623878656 | bytes 7340032 | tf_op jit(solution)/shard_map/project/pallas_call | solution.py:122
  56.4 3.5 %near.2 = (bf16[4,256,128]{2,1,0:T(8,128)(2,1)S(1)}, bf16[4,256,128]{2,1,0:T(8,128)(2,1)S(1)}, bf16[4,256,128]{2,1,0:T(8,128)(2,1)S(1)}, bf16[4,256,128]{2,1,0:T(8,128)(2,1)S(1)}, f32[4,3,128,128]{3,2,1,0:T(8,128)S(1)}) custom-call(s32[2]{0:T(128)S(1)} %pad_add_fusion.refs_0_.place_ref, s32[16]{0:T(128)S(1)} %copy-done.5, ...), custom_call_target="tpu_custom_call" | custom-call | flops 469762048 | bytes 2097152 | tf_op jit(solution)/shard_map/near/pallas_call | solution.py:203
  59.9 3.1 %collective-permute-done.10 = bf16[4,64,256]{2,1,0:T(8,128)(2,1)} collective-permute-done((bf16[4,64,256]{2,1,0:T(8,128)(2,1)}, bf16[4,64,256]{2,1,0:T(8,128)(2,1)}, u32[]{:S(2)}, u32[]{:S(2)}) %collective-permute-start.10) | collective-permute-done | bytes 131104 | tf_op jit(solution)/shard_map/ppermute | solution.py:29
  65.7 3.6 %collective-permute-start.12 = (bf16[2,128,256]{2,1,0:T(8,128)(2,1)S(1)}, bf16[2,128,256]{2,1,0:T(8,128)(2,1)S(1)}, u32[]{:S(2)}, u32[]{:S(2)}) collective-permute-start(bf16[2,128,256]{2,1,0:T(8,128)(2,1)S(1)} %pad_maximum_fusion.3), channel_id=1, source_target_pairs={{0,16},{1,17},{2,18},{3,19},{4,20},{5,21},{6,22},{7,23},{8,24},{9,... | collective-permute-start | bytes 393224 | tf_op jit(solution)/shard_map/ppermute | solution.py:29
  69.6 3.5 %near.3 = (bf16[4,256,128]{2,1,0:T(8,128)(2,1)S(1)}, bf16[4,256,128]{2,1,0:T(8,128)(2,1)S(1)}, bf16[4,256,128]{2,1,0:T(8,128)(2,1)S(1)}, bf16[4,256,128]{2,1,0:T(8,128)(2,1)S(1)}, f32[4,3,128,128]{3,2,1,0:T(8,128)S(1)}) custom-call(s32[2]{0:T(128)S(1)} %pad_add_fusion.refs_0_.place_ref, ...), custom_call_target="tpu_custom_call", output_to_operand_aliasing={{0}: (3, {}), {1}: (4, {}), {2}: (5, {}), {3}: (6, {}), {4}... | custom-call | flops 469762048 | bytes 2097152 | tf_op jit(solution)/shard_map/near/pallas_call | solution.py:203
  73.2 1.6 %collective-permute-start.13 = (bf16[2,128,256]{2,1,0:T(8,128)(2,1)S(1)}, bf16[2,128,256]{2,1,0:T(8,128)(2,1)S(1)}, u32[]{:S(2)}, u32[]{:S(2)}) collective-permute-start(bf16[2,128,256]{2,1,0:T(8,128)(2,1)S(1)} %constant_dynamic-update-slice_fusion), channel_id=1, source_target_pairs={{0,32},{1,33},{2,34},{3,35},{4,36},{5,37},{6,38},{7,39},{8,40},{9,... | collective-permute-start | bytes 393224 | tf_op jit(solution)/shard_map/ppermute | solution.py:29
  77.0 1.6 %middle.1 = (f32[4,96,128]{2,1,0:T(8,128)S(1)}, f32[4,3,32,128]{3,2,1,0:T(8,128)S(1)}) custom-call(bf16[4,128,128]{2,1,0:T(8,128)(2,1)S(1)} %get-tuple-element.96.q_ref, f32[4,3,128,128]{3,2,1,0:T(8,128)S(1)} %get-tuple-element.97.near_ref, bf16[4,128,256]{2,1,0:T(8,128)(2,1)S(1)} %get-tuple-element.119.own_ref, ...), custom_call_target="tpu_custom_call" | custom-call | flops 100663296 | bytes 1310720 | tf_op jit(solution)/shard_map/middle/pallas_call | solution.py:263
  78.7 2.8 %collective-permute-start.15 = (bf16[2,128,256]{2,1,0:T(8,128)(2,1)S(1)}, bf16[2,128,256]{2,1,0:T(8,128)(2,1)S(1)}, u32[]{:S(2)}, u32[]{:S(2)}) collective-permute-start(bf16[2,128,256]{2,1,0:T(8,128)(2,1)S(1)} %constant_dynamic-update-slice_fusion.8), channel_id=1, source_target_pairs={{0,64},{1,65},{2,66},{3,67},{4,68},{5,69},{6,70},{7,71},{8,72},{9,... | collective-permute-start | bytes 393224 | tf_op jit(solution)/shard_map/ppermute | solution.py:29
  81.5 2.3 %collective-permute-start.18 = (bf16[4,256,128]{2,1,0:T(8,128)(2,1)S(1)}, bf16[4,256,128]{2,1,0:T(8,128)(2,1)S(1)}, u32[]{:S(2)}, u32[]{:S(2)}) collective-permute-start(bf16[4,256,128]{2,1,0:T(8,128)(2,1)S(1)} %get-tuple-element.107), channel_id=1, source_target_pairs={{0,3},{1,2},{2,1},{3,0},{4,7},{5,6},{6,5},{7,4},{8,11},{9,10},{10,... | collective-permute-start | bytes 786440 | tf_op jit(solution)/shard_map/ppermute | solution.py:29
  86.6 2.2 %far.1 = (bf16[4,32,128]{2,1,0:T(8,128)(2,1)S(1)}, bf16[4,32,128]{2,1,0:T(8,128)(2,1)S(1)}, bf16[4,32,128]{2,1,0:T(8,128)(2,1)S(1)}, bf16[4,32,128]{2,1,0:T(8,128)(2,1)S(1)}) custom-call(s32[2]{0:T(128)S(1)} %pad_add_fusion.refs_0_.place_ref, bf16[4,128,128]{2,1,0:T(8,128)(2,1)S(1)} %get-tuple-element.96.q_ref, ...), custom_call_target="tpu_custom_call" | custom-call | flops 25165824 | bytes 1048576 | tf_op jit(solution)/shard_map/far/pallas_call | solution.py:303
  89.7 2.0 %collective-permute-start.23 = (bf16[4,32,128]{2,1,0:T(8,128)(2,1)S(1)}, bf16[4,32,128]{2,1,0:T(8,128)(2,1)S(1)}, u32[]{:S(2)}, u32[]{:S(2)}) collective-permute-start(bf16[4,32,128]{2,1,0:T(8,128)(2,1)S(1)} %get-tuple-element.113), channel_id=1, source_target_pairs={{0,2},{1,3},{2,0},{3,1},{4,6},{5,7},{6,4},{7,5},{8,10},{9,11},{10,... | collective-permute-start | bytes 98312 | tf_op jit(solution)/shard_map/ppermute | solution.py:29
  93.6 2.9 %collective-permute-done.24.refs_7_ = bf16[4,32,128]{2,1,0:T(8,128)(2,1)S(1)} collective-permute-done((bf16[4,32,128]{2,1,0:T(8,128)(2,1)S(1)}, bf16[4,32,128]{2,1,0:T(8,128)(2,1)S(1)}, u32[]{:S(2)}, u32[]{:S(2)}) %collective-permute-start.24) | collective-permute-done | bytes 32800 | tf_op jit(solution)/shard_map/ppermute | solution.py:29
  96.5 2.1 %place.1 = bf16[256,2048]{1,0:T(8,128)(2,1)} custom-call(s32[2]{0:T(128)S(1)} %pad_add_fusion.refs_0_.place_ref, s32[16]{0:T(128)S(1)} %copy-done.5, bf16[4,256,128]{2,1,0:T(8,128)(2,1)S(1)} %get-tuple-element.94.refs_0_, bf16[4,256,128]{2,1,0:T(8,128)(2,1)S(1)} %collective-permute-done.16.refs_1_, bf16[4,256,128]{2,1,0:T(8,128)(2,1)S(1)} %collective-permute-done.17.refs_2_, ...), custom_call_target="tpu_custom_call" | custom-call | flops 33554432 | bytes 2097152 | tf_op jit(solution)/shard_map/place/pallas_call | solution.py:334
  (85 shorter events, 19.7 us)
Async XLA Ops:
  2.7 24.8 %collective-permute-start.3 = (bf16[512,768]{1,0:T(8,128)(2,1)}, bf16[512,768]{1,0:T(8,128)(2,1)}, u32[]{:S(2)}, u32[]{:S(2)}) collective-permute-start(bf16[512,768]{1,0:T(8,128)(2,1)} %get-tuple-element.116), channel_id=1, source_target_pairs={{0,6},{1,7},{2,4},{3,5},{4,2},{5,3},{6,0},{7,1},{8,14},{9,15},{10,... | collective-permute-start | bytes 2359304 | tf_op jit(solution)/shard_map/ppermute | solution.py:29
  6.8 13.8 %collective-permute-start.2 = (bf16[128,2048]{1,0:T(8,128)(2,1)}, bf16[128,2048]{1,0:T(8,128)(2,1)S(1)}, u32[]{:S(2)}, u32[]{:S(2)}) collective-permute-start(bf16[128,2048]{1,0:T(8,128)(2,1)} %get-tuple-element.117), channel_id=1, source_target_pairs={{0,1},{1,0},{2,3},{3,2},{4,5},{5,4},{6,7},{7,6},{8,9},{9,8},{10,11... | collective-permute-start | bytes 1572872 | tf_op jit(solution)/shard_map/ppermute | solution.py:29
  8.8 18.8 %collective-permute-start.1 = (bf16[128,2048]{1,0:T(8,128)(2,1)}, bf16[128,2048]{1,0:T(8,128)(2,1)}, u32[]{:S(2)}, u32[]{:S(2)}) collective-permute-start(bf16[128,2048]{1,0:T(8,128)(2,1)} %get-tuple-element.118), channel_id=1, source_target_pairs={{0,2},{1,3},{2,0},{3,1},{4,6},{5,7},{6,4},{7,5},{8,10},{9,11},{10,... | collective-permute-start | bytes 1572872 | tf_op jit(solution)/shard_map/ppermute | solution.py:29
  8.9 31.6 %collective-permute-start.5 = (bf16[512,768]{1,0:T(8,128)(2,1)}, bf16[512,768]{1,0:T(8,128)(2,1)}, u32[]{:S(2)}, u32[]{:S(2)}) collective-permute-start(bf16[512,768]{1,0:T(8,128)(2,1)} %get-tuple-element.115), channel_id=1, source_target_pairs={{0,6},{1,7},{2,4},{3,5},{4,2},{5,3},{6,0},{7,1},{8,14},{9,15},{10,... | collective-permute-start | bytes 2359304 | tf_op jit(solution)/shard_map/ppermute | solution.py:29
  10.0 25.2 %collective-permute-start.4 = (bf16[128,2048]{1,0:T(8,128)(2,1)}, bf16[128,2048]{1,0:T(8,128)(2,1)}, u32[]{:S(2)}, u32[]{:S(2)}) collective-permute-start(bf16[128,2048]{1,0:T(8,128)(2,1)} %get-tuple-element.117), channel_id=1, source_target_pairs={{0,2},{1,3},{2,0},{3,1},{4,6},{5,7},{6,4},{7,5},{8,10},{9,11},{10,... | collective-permute-start | bytes 1572872 | tf_op jit(solution)/shard_map/ppermute | solution.py:29
  20.6 15.1 %collective-permute-start = (bf16[128,2048]{1,0:T(8,128)(2,1)}, bf16[128,2048]{1,0:T(8,128)(2,1)S(1)}, u32[]{:S(2)}, u32[]{:S(2)}) collective-permute-start(bf16[128,2048]{1,0:T(8,128)(2,1)} %get-tuple-element.118), channel_id=1, source_target_pairs={{0,1},{1,0},{2,3},{3,2},{4,5},{5,4},{6,7},{7,6},{8,9},{9,8},{10,11... | collective-permute-start | bytes 1572872 | tf_op jit(solution)/shard_map/ppermute | solution.py:29
  27.5 17.0 %collective-permute-start.7 = (bf16[128,2048]{1,0:T(8,128)(2,1)S(1)}, bf16[128,2048]{1,0:T(8,128)(2,1)S(1)}, u32[]{:S(2)}, u32[]{:S(2)}) collective-permute-start(bf16[128,2048]{1,0:T(8,128)(2,1)S(1)} %copy-done.4), channel_id=1, source_target_pairs={{0,2},{1,3},{2,0},{3,1},{4,6},{5,7},{6,4},{7,5},{8,10},{9,11},{10,... | collective-permute-start | bytes 1572872 | tf_op jit(solution)/shard_map/ppermute | solution.py:29
  27.8 17.1 %collective-permute-start.6 = (bf16[128,2048]{1,0:T(8,128)(2,1)}, bf16[128,2048]{1,0:T(8,128)(2,1)S(1)}, u32[]{:S(2)}, u32[]{:S(2)}) collective-permute-start(bf16[128,2048]{1,0:T(8,128)(2,1)} %collective-permute-done.1.refs_4_.refs_5_), channel_id=1, source_target_pairs={{0,1},{1,0},{2,3},{3,2},{4,5},{5,4},{6,7},{7,6},{8,9},{9,8},{10,11... | collective-permute-start | bytes 1572872 | tf_op jit(solution)/shard_map/ppermute | solution.py:29
  35.2 11.6 %collective-permute-start.8 = (bf16[512,768]{1,0:T(8,128)(2,1)}, bf16[512,768]{1,0:T(8,128)(2,1)S(1)}, u32[]{:S(2)}, u32[]{:S(2)}) collective-permute-start(bf16[512,768]{1,0:T(8,128)(2,1)} %collective-permute-done.3.refs_9_), channel_id=1, source_target_pairs={{0,8},{1,9},{2,10},{3,11},{4,12},{5,13},{6,14},{7,15},{8,0},{9,1},... | collective-permute-start | bytes 2359304 | tf_op jit(solution)/shard_map/ppermute | solution.py:29
  44.8 2.5 %collective-permute-start.9 = (bf16[512,768]{1,0:T(8,128)(2,1)}, bf16[512,768]{1,0:T(8,128)(2,1)S(1)}, u32[]{:S(2)}, u32[]{:S(2)}) collective-permute-start(bf16[512,768]{1,0:T(8,128)(2,1)} %collective-permute-done.5.refs_10_), channel_id=1, source_target_pairs={{0,8},{1,9},{2,10},{3,11},{4,12},{5,13},{6,14},{7,15},{8,0},{9,1},... | collective-permute-start | bytes 2359304 | tf_op jit(solution)/shard_map/ppermute | solution.py:29
  56.0 7.1 %collective-permute-start.10 = (bf16[4,64,256]{2,1,0:T(8,128)(2,1)}, bf16[4,64,256]{2,1,0:T(8,128)(2,1)}, u32[]{:S(2)}, u32[]{:S(2)}) collective-permute-start(bf16[4,64,256]{2,1,0:T(8,128)(2,1)} %get-tuple-element.69), channel_id=1, source_target_pairs={{0,6},{1,7},{2,4},{3,5},{4,2},{5,3},{6,0},{7,1},{8,14},{9,15},{10,... | collective-permute-start | bytes 393224 | tf_op jit(solution)/shard_map/ppermute | solution.py:29
  64.0 1.6 %collective-permute-start.11 = (bf16[4,128,256]{2,1,0:T(8,128)(2,1)S(1)}, bf16[4,128,256]{2,1,0:T(8,128)(2,1)S(1)}, u32[]{:S(2)}, u32[]{:S(2)}) collective-permute-start(bf16[4,128,256]{2,1,0:T(8,128)(2,1)S(1)} %get-tuple-element.76), channel_id=1, source_target_pairs={{0,8},{1,9},{2,10},{3,11},{4,12},{5,13},{6,14},{7,15},{8,0},{9,1},... | collective-permute-start | bytes 786440 | tf_op jit(solution)/shard_map/ppermute | solution.py:29
  65.7 7.4 %collective-permute-start.12 = (bf16[2,128,256]{2,1,0:T(8,128)(2,1)S(1)}, bf16[2,128,256]{2,1,0:T(8,128)(2,1)S(1)}, u32[]{:S(2)}, u32[]{:S(2)}) collective-permute-start(bf16[2,128,256]{2,1,0:T(8,128)(2,1)S(1)} %pad_maximum_fusion.3), channel_id=1, source_target_pairs={{0,16},{1,17},{2,18},{3,19},{4,20},{5,21},{6,22},{7,23},{8,24},{9,... | collective-permute-start | bytes 393224 | tf_op jit(solution)/shard_map/ppermute | solution.py:29
  69.3 6.8 %collective-permute-start.14 = (bf16[4,64,256]{2,1,0:T(8,128)(2,1)S(1)}, bf16[4,64,256]{2,1,0:T(8,128)(2,1)S(1)}, u32[]{:S(2)}, u32[]{:S(2)}) collective-permute-start(bf16[4,64,256]{2,1,0:T(8,128)(2,1)S(1)} %copy-done.7), channel_id=1, source_target_pairs={{0,6},{1,7},{2,4},{3,5},{4,2},{5,3},{6,0},{7,1},{8,14},{9,15},{10,... | collective-permute-start | bytes 393224 | tf_op jit(solution)/shard_map/ppermute | solution.py:29
  73.2 5.5 %collective-permute-start.13 = (bf16[2,128,256]{2,1,0:T(8,128)(2,1)S(1)}, bf16[2,128,256]{2,1,0:T(8,128)(2,1)S(1)}, u32[]{:S(2)}, u32[]{:S(2)}) collective-permute-start(bf16[2,128,256]{2,1,0:T(8,128)(2,1)S(1)} %constant_dynamic-update-slice_fusion), channel_id=1, source_target_pairs={{0,32},{1,33},{2,34},{3,35},{4,36},{5,37},{6,38},{7,39},{8,40},{9,... | collective-permute-start | bytes 393224 | tf_op jit(solution)/shard_map/ppermute | solution.py:29
  74.8 9.1 %collective-permute-start.16 = (bf16[4,256,128]{2,1,0:T(8,128)(2,1)S(1)}, bf16[4,256,128]{2,1,0:T(8,128)(2,1)S(1)}, u32[]{:S(2)}, u32[]{:S(2)}) collective-permute-start(bf16[4,256,128]{2,1,0:T(8,128)(2,1)S(1)} %get-tuple-element.103), channel_id=1, source_target_pairs={{0,1},{1,0},{2,3},{3,2},{4,5},{5,4},{6,7},{7,6},{8,9},{9,8},{10,11... | collective-permute-start | bytes 786440 | tf_op jit(solution)/shard_map/ppermute | solution.py:29
  76.0 8.3 %collective-permute-start.17 = (bf16[4,256,128]{2,1,0:T(8,128)(2,1)S(1)}, bf16[4,256,128]{2,1,0:T(8,128)(2,1)S(1)}, u32[]{:S(2)}, u32[]{:S(2)}) collective-permute-start(bf16[4,256,128]{2,1,0:T(8,128)(2,1)S(1)} %get-tuple-element.104), channel_id=1, source_target_pairs={{0,2},{1,3},{2,0},{3,1},{4,6},{5,7},{6,4},{7,5},{8,10},{9,11},{10,... | collective-permute-start | bytes 786440 | tf_op jit(solution)/shard_map/ppermute | solution.py:29
  78.7 6.6 %collective-permute-start.15 = (bf16[2,128,256]{2,1,0:T(8,128)(2,1)S(1)}, bf16[2,128,256]{2,1,0:T(8,128)(2,1)S(1)}, u32[]{:S(2)}, u32[]{:S(2)}) collective-permute-start(bf16[2,128,256]{2,1,0:T(8,128)(2,1)S(1)} %constant_dynamic-update-slice_fusion.8), channel_id=1, source_target_pairs={{0,64},{1,65},{2,66},{3,67},{4,68},{5,69},{6,70},{7,71},{8,72},{9,... | collective-permute-start | bytes 393224 | tf_op jit(solution)/shard_map/ppermute | solution.py:29
  81.5 10.8 %collective-permute-start.18 = (bf16[4,256,128]{2,1,0:T(8,128)(2,1)S(1)}, bf16[4,256,128]{2,1,0:T(8,128)(2,1)S(1)}, u32[]{:S(2)}, u32[]{:S(2)}) collective-permute-start(bf16[4,256,128]{2,1,0:T(8,128)(2,1)S(1)} %get-tuple-element.107), channel_id=1, source_target_pairs={{0,3},{1,2},{2,1},{3,0},{4,7},{5,6},{6,5},{7,4},{8,11},{9,10},{10,... | collective-permute-start | bytes 786440 | tf_op jit(solution)/shard_map/ppermute | solution.py:29
  83.8 1.5 %collective-permute-start.19 = (bf16[2,128,256]{2,1,0:T(8,128)(2,1)S(1)}, bf16[2,128,256]{2,1,0:T(8,128)(2,1)S(1)}, u32[]{:S(2)}, u32[]{:S(2)}) collective-permute-start(bf16[2,128,256]{2,1,0:T(8,128)(2,1)S(1)} %collective-permute-done.12.mine5), channel_id=1, source_target_pairs={{0,8},{1,9},{2,10},{3,11},{4,12},{5,13},{6,14},{7,15},{8,0},{9,1},... | collective-permute-start | bytes 393224 | tf_op jit(solution)/shard_map/ppermute | solution.py:29
  83.8 1.5 %collective-permute-start.20 = (bf16[2,128,256]{2,1,0:T(8,128)(2,1)S(1)}, bf16[2,128,256]{2,1,0:T(8,128)(2,1)S(1)}, u32[]{:S(2)}, u32[]{:S(2)}) collective-permute-start(bf16[2,128,256]{2,1,0:T(8,128)(2,1)S(1)} %collective-permute-done.13.mine6), channel_id=1, source_target_pairs={{0,8},{1,9},{2,10},{3,11},{4,12},{5,13},{6,14},{7,15},{8,0},{9,1},... | collective-permute-start | bytes 393224 | tf_op jit(solution)/shard_map/ppermute | solution.py:29
  88.8 4.0 %collective-permute-start.22 = (bf16[4,32,128]{2,1,0:T(8,128)(2,1)S(1)}, bf16[4,32,128]{2,1,0:T(8,128)(2,1)S(1)}, u32[]{:S(2)}, u32[]{:S(2)}) collective-permute-start(bf16[4,32,128]{2,1,0:T(8,128)(2,1)S(1)} %get-tuple-element.112), channel_id=1, source_target_pairs={{0,1},{1,0},{2,3},{3,2},{4,5},{5,4},{6,7},{7,6},{8,9},{9,8},{10,11... | collective-permute-start | bytes 98312 | tf_op jit(solution)/shard_map/ppermute | solution.py:29
  89.7 3.9 %collective-permute-start.23 = (bf16[4,32,128]{2,1,0:T(8,128)(2,1)S(1)}, bf16[4,32,128]{2,1,0:T(8,128)(2,1)S(1)}, u32[]{:S(2)}, u32[]{:S(2)}) collective-permute-start(bf16[4,32,128]{2,1,0:T(8,128)(2,1)S(1)} %get-tuple-element.113), channel_id=1, source_target_pairs={{0,2},{1,3},{2,0},{3,1},{4,6},{5,7},{6,4},{7,5},{8,10},{9,11},{10,... | collective-permute-start | bytes 98312 | tf_op jit(solution)/shard_map/ppermute | solution.py:29
  91.7 4.8 %collective-permute-start.24 = (bf16[4,32,128]{2,1,0:T(8,128)(2,1)S(1)}, bf16[4,32,128]{2,1,0:T(8,128)(2,1)S(1)}, u32[]{:S(2)}, u32[]{:S(2)}) collective-permute-start(bf16[4,32,128]{2,1,0:T(8,128)(2,1)S(1)} %get-tuple-element.114), channel_id=1, source_target_pairs={{0,3},{1,2},{2,1},{3,0},{4,7},{5,6},{6,5},{7,4},{8,11},{9,10},{10,... | collective-permute-start | bytes 98312 | tf_op jit(solution)/shard_map/ppermute | solution.py:29
  (9 other events, 49.9 us)

commit v4 on v3

--- a/solution.py
+++ b/solution.py
@@ -398,12 +398,14 @@
 
     low_other = flipped(low_sent, 0, 6)
     found = near(place, offsets, qkv, 0, 2, ())
-    kept = jnp.concatenate([low, low_other], axis=1)
-    kept, found = lax.optimization_barrier((kept, found))
-    other4 = flipped(kept, 1, 0)
+    low, low_other, found = lax.optimization_barrier((low, low_other, found))
+    low_core = flipped(low, 1, 0)
+    low_both = flipped(low_other, 1, 0)
+    other4 = jnp.concatenate([low_core, low_both], axis=1)
     other4, found, high_sent = lax.optimization_barrier((other4, found, high_sent))
     high_other = flipped(high_sent, 0, 6)
-    kept, other, pieces = half_slots(kept, core), half_slots(other4, core), 2
+    kept = jnp.concatenate([half_slots(low, core), half_slots(low_other, core)], axis=1)
+    other, pieces = half_slots(other4, core), 2
     mine, their = [], []
     for level in range(1, 4):
         kept = jnp.concatenate(halves(kept, pieces) + halves(other, pieces), axis=1)

time: 99 us -> 98.3 us (level)
  waiting for transfers between devices: 33.9 us -> 32.8 us
    ppermute x25 -> x26, waiting for transfers between devices: 33.9 us -> 32.8 us  [flipped(): lax.ppermute(value, ('outer', 'inner'), [(f, f ^ mask) for f in range(cou...]
    ppermute x25 -> x26, starting transfers between devices: 26.3 us -> 26.7 us  [flipped(): lax.ppermute(value, ('outer', 'inner'), [(f, f ^ mask) for f in range(cou...]
  transfers between devices with their start and end apart: 25 -> 26, of which waited for: 15 -> 15; matrix products, arithmetic and copies ran while one was open for 2% -> 3% of each run, Pallas kernels for 19% -> 19%
where the time goes in v4:
time: 98.3 us; the launch traced here: 98 us
  waiting for transfers between devices  32.8 us (33%)
  Pallas kernels  28.5 us (29%)
  starting transfers between devices  26.7 us (27%)
  local copies, waits for them, and re-layouts  7.6 us (8%)
  other arithmetic  1.96 us (2%)
    ppermute x26, waiting for transfers between devices, flipped(): lax.ppermute(value, ('outer', 'inner'), [(f, f ^ mask) for f in range(cou...  32.8 us
    ppermute x26, starting transfers between devices, flipped(): lax.ppermute(value, ('outer', 'inner'), [(f, f ^ mask) for f in range(cou...  26.7 us
    pallas_call x4, Pallas kernels, project(): pl.pallas_call(body, out_shape=out_shape, in_specs=[scalars, scalars] + [...  15.7 us
    pallas_call x2, Pallas kernels, near(): pl.pallas_call(lambda *refs: near_body(base, heads, len(carried), *refs),...  6.96 us
    unnamed x38, local copies, waits for them, and re-layouts  3.84 us
    dynamic_slice x1, local copies, waits for them, and re-layouts, shards(): lax.dynamic_slice(qkv_weight, ((2 * core + k) * chunk, 0), (chunk, width))  2.7 us
    pallas_call x1, Pallas kernels, far(): pl.pallas_call(far_body, out_shape=tuple((jax.ShapeDtypeStruct((SLOTS, DE...  2.16 us
    pallas_call x1, Pallas kernels, placed_heads(): pl.pallas_call(place_body, out_shape=jax.ShapeDtypeStruct((ROWS, HEADS *...  2.14 us
  transfers between devices with their start and end apart: 26, of which 15 were waited for; matrix products, arithmetic and copies ran while one was open for 3% of the time, Pallas kernels for 19%

profile of v4, /device:TPU:0, one launch (start us, length us, event | category | flops | bytes accessed | tf_op | source)
XLA Modules:
  0.0 98.0 jit_solution(12606838667238435550)
XLA Ops:
  0.0 2.7 %constant_dynamic-slice_fusion = (bf16[512,768]{1,0:T(8,128)(2,1)}, bf16[512,768]{1,0:T(8,128)(2,1)}) fusion(bf16[2048,768]{1,0:T(8,128)(2,1)} %refs_4_.1, s32[]{:T(128)S(6)} %select_n.28, s32[]{:T(128)S(6)} %select_n.27), kind=kLoop, calls=%fused_computation.32 | loop fusion | bytes 3145736 | tf_op jit(solution)/shard_map/dynamic_slice | solution.py:369
  2.7 3.1 %collective-permute-start.3 = (bf16[512,768]{1,0:T(8,128)(2,1)}, bf16[512,768]{1,0:T(8,128)(2,1)}, u32[]{:S(2)}, u32[]{:S(2)}) collective-permute-start(bf16[512,768]{1,0:T(8,128)(2,1)} %get-tuple-element.118), channel_id=1, source_target_pairs={{0,6},{1,7},{2,4},{3,5},{4,2},{5,3},{6,0},{7,1},{8,14},{9,15},{10,... | collective-permute-start | bytes 2359304 | tf_op jit(solution)/shard_map/ppermute | solution.py:29
  6.8 1.9 %collective-permute-start.2 = (bf16[128,2048]{1,0:T(8,128)(2,1)}, bf16[128,2048]{1,0:T(8,128)(2,1)S(1)}, u32[]{:S(2)}, u32[]{:S(2)}) collective-permute-start(bf16[128,2048]{1,0:T(8,128)(2,1)} %get-tuple-element.119), channel_id=1, source_target_pairs={{0,1},{1,0},{2,3},{3,2},{4,5},{5,4},{6,7},{7,6},{8,9},{9,8},{10,11... | collective-permute-start | bytes 1572872 | tf_op jit(solution)/shard_map/ppermute | solution.py:29
  10.8 9.8 %collective-permute-done.2.refs_3_.refs_4_ = bf16[128,2048]{1,0:T(8,128)(2,1)S(1)} collective-permute-done((bf16[128,2048]{1,0:T(8,128)(2,1)}, bf16[128,2048]{1,0:T(8,128)(2,1)S(1)}, u32[]{:S(2)}, u32[]{:S(2)}) %collective-permute-start.2) | collective-permute-done | bytes 524320 | tf_op jit(solution)/shard_map/ppermute | solution.py:29
  20.6 1.7 %collective-permute-start = (bf16[128,2048]{1,0:T(8,128)(2,1)}, bf16[128,2048]{1,0:T(8,128)(2,1)S(1)}, u32[]{:S(2)}, u32[]{:S(2)}) collective-permute-start(bf16[128,2048]{1,0:T(8,128)(2,1)} %get-tuple-element.120), channel_id=1, source_target_pairs={{0,1},{1,0},{2,3},{3,2},{4,5},{5,4},{6,7},{7,6},{8,9},{9,8},{10,11... | collective-permute-start | bytes 1572872 | tf_op jit(solution)/shard_map/ppermute | solution.py:29
  22.4 1.9 %copy-done = bf16[2048,768]{1,0:T(8,128)(2,1)S(1)} copy-done((bf16[2048,768]{1,0:T(8,128)(2,1)S(1)}, bf16[2048,768]{1,0:T(8,128)(2,1)}, u32[]{:S(2)}) %copy-start) | copy-done | bytes 3145752
  25.6 1.9 %project.4.refs_7_ = bf16[4,4,256,384]{3,2,1,0:T(8,128)(2,1)S(1)} custom-call(s32[2]{0:T(128)S(1)} %pad_add_fusion.refs_0_.place_ref, s32[16]{0:T(128)S(1)} %copy-done.5, bf16[256,2048]{1,0:T(8,128)(2,1)S(1)} %copy-done.2, bf16[2048,768]{1,0:T(8,128)(2,1)S(1)} %copy-done), custom_call_target="tpu_custom_call" | custom-call | flops 905969664 | bytes 4194304 | tf_op jit(solution)/shard_map/project/pallas_call | solution.py:122
  28.6 6.6 %collective-permute-done.4.refs_5_.refs_6_ = bf16[128,2048]{1,0:T(8,128)(2,1)} collective-permute-done((bf16[128,2048]{1,0:T(8,128)(2,1)}, bf16[128,2048]{1,0:T(8,128)(2,1)}, u32[]{:S(2)}, u32[]{:S(2)}) %collective-permute-start.4) | collective-permute-done | bytes 524320 | tf_op jit(solution)/shard_map/ppermute | solution.py:29
  35.7 3.8 %project.5.refs_5_ = bf16[4,4,256,384]{3,2,1,0:T(8,128)(2,1)S(1)} custom-call(s32[2]{0:T(128)S(1)} %pad_add_fusion.refs_0_.place_ref, s32[16]{0:T(128)S(1)} %copy-done.5, bf16[128,2048]{1,0:T(8,128)(2,1)S(1)} %collective-permute-done.refs_2_.refs_3_, bf16[128,2048]{1,0:T(8,128)(2,1)S(1)} %copy-done.4, ...), custom_call_target="tpu_custom_call", output_to_operand_aliasing={{}: (7, {})} | custom-call | flops 1811939328 | bytes 5242880 | tf_op jit(solution)/shard_map/project/pallas_call | solution.py:122
  40.5 4.0 %collective-permute-done.7.refs_3_.refs_8_ = bf16[128,2048]{1,0:T(8,128)(2,1)S(1)} collective-permute-done((bf16[128,2048]{1,0:T(8,128)(2,1)S(1)}, bf16[128,2048]{1,0:T(8,128)(2,1)S(1)}, u32[]{:S(2)}, u32[]{:S(2)}) %collective-permute-start.7) | collective-permute-done | bytes 524320 | tf_op jit(solution)/shard_map/ppermute | solution.py:29
  44.8 1.9 %project.6.refs_13_ = bf16[4,4,256,384]{3,2,1,0:T(8,128)(2,1)S(1)} custom-call(s32[2]{0:T(128)S(1)} %pad_add_fusion.refs_0_.place_ref, s32[16]{0:T(128)S(1)} %copy-done.5, bf16[128,2048]{1,0:T(8,128)(2,1)S(1)} %collective-permute-done.6.refs_2_.refs_7_, bf16[128,2048]{1,0:T(8,128)(2,1)S(1)} %collective-permute-done.7.refs_3_.refs_8_, ...), custom_call_target="tpu_custom_call", output_to_operand_aliasing={{}: (5, {})} | custom-call | flops 905969664 | bytes 4194304 | tf_op jit(solution)/shard_map/project/pallas_call | solution.py:122
  47.3 8.0 %project.7 = (bf16[4,4,256,384]{3,2,1,0:T(8,128)(2,1)S(1)}, bf16[4,128,128]{2,1,0:T(8,128)(2,1)S(1)}, bf16[4,64,256]{2,1,0:T(8,128)(2,1)S(1)}, bf16[4,64,256]{2,...) custom-call(s32[2]{0:T(128)S(1)} %pad_add_fusion.refs_0_.place_ref, ...), custom_call_target="tpu_custom_call", output_to_operand_aliasing={{0}: (13, {})} | custom-call | flops 3623878656 | bytes 7340032 | tf_op jit(solution)/shard_map/project/pallas_call | solution.py:122
  56.4 3.5 %near.2 = (bf16[4,256,128]{2,1,0:T(8,128)(2,1)S(1)}, bf16[4,256,128]{2,1,0:T(8,128)(2,1)S(1)}, bf16[4,256,128]{2,1,0:T(8,128)(2,1)S(1)}, bf16[4,256,128]{2,1,0:T(8,128)(2,1)S(1)}, f32[4,3,128,128]{3,2,1,0:T(8,128)S(1)}) custom-call(s32[2]{0:T(128)S(1)} %pad_add_fusion.refs_0_.place_ref, s32[16]{0:T(128)S(1)} %copy-done.5, ...), custom_call_target="tpu_custom_call" | custom-call | flops 469762048 | bytes 2097152 | tf_op jit(solution)/shard_map/near/pallas_call | solution.py:203
  59.9 3.1 %collective-permute-done.10 = bf16[4,64,256]{2,1,0:T(8,128)(2,1)} collective-permute-done((bf16[4,64,256]{2,1,0:T(8,128)(2,1)}, bf16[4,64,256]{2,1,0:T(8,128)(2,1)}, u32[]{:S(2)}, u32[]{:S(2)}) %collective-permute-start.10) | collective-permute-done | bytes 131104 | tf_op jit(solution)/shard_map/ppermute | solution.py:29
  64.9 3.6 %collective-permute-start.13 = (bf16[2,128,256]{2,1,0:T(8,128)(2,1)S(1)}, bf16[2,128,256]{2,1,0:T(8,128)(2,1)S(1)}, u32[]{:S(2)}, u32[]{:S(2)}) collective-permute-start(bf16[2,128,256]{2,1,0:T(8,128)(2,1)S(1)} %pad_maximum_fusion.3), channel_id=1, source_target_pairs={{0,16},{1,17},{2,18},{3,19},{4,20},{5,21},{6,22},{7,23},{8,24},{9,... | collective-permute-start | bytes 393224 | tf_op jit(solution)/shard_map/ppermute | solution.py:29
  68.8 3.5 %near.3 = (bf16[4,256,128]{2,1,0:T(8,128)(2,1)S(1)}, bf16[4,256,128]{2,1,0:T(8,128)(2,1)S(1)}, bf16[4,256,128]{2,1,0:T(8,128)(2,1)S(1)}, bf16[4,256,128]{2,1,0:T(8,128)(2,1)S(1)}, f32[4,3,128,128]{3,2,1,0:T(8,128)S(1)}) custom-call(s32[2]{0:T(128)S(1)} %pad_add_fusion.refs_0_.place_ref, ...), custom_call_target="tpu_custom_call", output_to_operand_aliasing={{0}: (3, {}), {1}: (4, {}), {2}: (5, {}), {3}: (6, {}), {4}... | custom-call | flops 469762048 | bytes 2097152 | tf_op jit(solution)/shard_map/near/pallas_call | solution.py:203
  72.5 1.6 %collective-permute-start.14 = (bf16[2,128,256]{2,1,0:T(8,128)(2,1)S(1)}, bf16[2,128,256]{2,1,0:T(8,128)(2,1)S(1)}, u32[]{:S(2)}, u32[]{:S(2)}) collective-permute-start(bf16[2,128,256]{2,1,0:T(8,128)(2,1)S(1)} %constant_dynamic-update-slice_fusion), channel_id=1, source_target_pairs={{0,32},{1,33},{2,34},{3,35},{4,36},{5,37},{6,38},{7,39},{8,40},{9,... | collective-permute-start | bytes 393224 | tf_op jit(solution)/shard_map/ppermute | solution.py:29
  76.4 1.6 %middle.1 = (f32[4,96,128]{2,1,0:T(8,128)S(1)}, f32[4,3,32,128]{3,2,1,0:T(8,128)S(1)}) custom-call(bf16[4,128,128]{2,1,0:T(8,128)(2,1)S(1)} %get-tuple-element.98.q_ref, f32[4,3,128,128]{3,2,1,0:T(8,128)S(1)} %get-tuple-element.99.near_ref, bf16[4,128,256]{2,1,0:T(8,128)(2,1)S(1)} %pad_maximum_fusion.1.own_ref, ...), custom_call_target="tpu_custom_call" | custom-call | flops 100663296 | bytes 1310720 | tf_op jit(solution)/shard_map/middle/pallas_call | solution.py:263
  78.1 2.8 %collective-permute-start.16 = (bf16[2,128,256]{2,1,0:T(8,128)(2,1)S(1)}, bf16[2,128,256]{2,1,0:T(8,128)(2,1)S(1)}, u32[]{:S(2)}, u32[]{:S(2)}) collective-permute-start(bf16[2,128,256]{2,1,0:T(8,128)(2,1)S(1)} %constant_dynamic-update-slice_fusion.8), channel_id=1, source_target_pairs={{0,64},{1,65},{2,66},{3,67},{4,68},{5,69},{6,70},{7,71},{8,72},{9,... | collective-permute-start | bytes 393224 | tf_op jit(solution)/shard_map/ppermute | solution.py:29
  81.0 2.2 %collective-permute-start.19 = (bf16[4,256,128]{2,1,0:T(8,128)(2,1)S(1)}, bf16[4,256,128]{2,1,0:T(8,128)(2,1)S(1)}, u32[]{:S(2)}, u32[]{:S(2)}) collective-permute-start(bf16[4,256,128]{2,1,0:T(8,128)(2,1)S(1)} %get-tuple-element.109), channel_id=1, source_target_pairs={{0,3},{1,2},{2,1},{3,0},{4,7},{5,6},{6,5},{7,4},{8,11},{9,10},{10,... | collective-permute-start | bytes 786440 | tf_op jit(solution)/shard_map/ppermute | solution.py:29
  86.0 2.2 %far.1 = (bf16[4,32,128]{2,1,0:T(8,128)(2,1)S(1)}, bf16[4,32,128]{2,1,0:T(8,128)(2,1)S(1)}, bf16[4,32,128]{2,1,0:T(8,128)(2,1)S(1)}, bf16[4,32,128]{2,1,0:T(8,128)(2,1)S(1)}) custom-call(s32[2]{0:T(128)S(1)} %pad_add_fusion.refs_0_.place_ref, bf16[4,128,128]{2,1,0:T(8,128)(2,1)S(1)} %get-tuple-element.98.q_ref, ...), custom_call_target="tpu_custom_call" | custom-call | flops 25165824 | bytes 1048576 | tf_op jit(solution)/shard_map/far/pallas_call | solution.py:303
  89.0 2.0 %collective-permute-start.24 = (bf16[4,32,128]{2,1,0:T(8,128)(2,1)S(1)}, bf16[4,32,128]{2,1,0:T(8,128)(2,1)S(1)}, u32[]{:S(2)}, u32[]{:S(2)}) collective-permute-start(bf16[4,32,128]{2,1,0:T(8,128)(2,1)S(1)} %get-tuple-element.115), channel_id=1, source_target_pairs={{0,2},{1,3},{2,0},{3,1},{4,6},{5,7},{6,4},{7,5},{8,10},{9,11},{10,... | collective-permute-start | bytes 98312 | tf_op jit(solution)/shard_map/ppermute | solution.py:29
  92.9 2.9 %collective-permute-done.25.refs_7_ = bf16[4,32,128]{2,1,0:T(8,128)(2,1)S(1)} collective-permute-done((bf16[4,32,128]{2,1,0:T(8,128)(2,1)S(1)}, bf16[4,32,128]{2,1,0:T(8,128)(2,1)S(1)}, u32[]{:S(2)}, u32[]{:S(2)}) %collective-permute-start.25) | collective-permute-done | bytes 32800 | tf_op jit(solution)/shard_map/ppermute | solution.py:29
  95.8 2.1 %place.1 = bf16[256,2048]{1,0:T(8,128)(2,1)} custom-call(s32[2]{0:T(128)S(1)} %pad_add_fusion.refs_0_.place_ref, s32[16]{0:T(128)S(1)} %copy-done.5, bf16[4,256,128]{2,1,0:T(8,128)(2,1)S(1)} %get-tuple-element.96.refs_0_, bf16[4,256,128]{2,1,0:T(8,128)(2,1)S(1)} %collective-permute-done.17.refs_1_, bf16[4,256,128]{2,1,0:T(8,128)(2,1)S(1)} %collective-permute-done.18.refs_2_, ...), custom_call_target="tpu_custom_call" | custom-call | flops 33554432 | bytes 2097152 | tf_op jit(solution)/shard_map/place/pallas_call | solution.py:334
  (89 shorter events, 19.1 us)
Async XLA Ops:
  2.7 24.8 %collective-permute-start.3 = (bf16[512,768]{1,0:T(8,128)(2,1)}, bf16[512,768]{1,0:T(8,128)(2,1)}, u32[]{:S(2)}, u32[]{:S(2)}) collective-permute-start(bf16[512,768]{1,0:T(8,128)(2,1)} %get-tuple-element.118), channel_id=1, source_target_pairs={{0,6},{1,7},{2,4},{3,5},{4,2},{5,3},{6,0},{7,1},{8,14},{9,15},{10,... | collective-permute-start | bytes 2359304 | tf_op jit(solution)/shard_map/ppermute | solution.py:29
  6.8 13.8 %collective-permute-start.2 = (bf16[128,2048]{1,0:T(8,128)(2,1)}, bf16[128,2048]{1,0:T(8,128)(2,1)S(1)}, u32[]{:S(2)}, u32[]{:S(2)}) collective-permute-start(bf16[128,2048]{1,0:T(8,128)(2,1)} %get-tuple-element.119), channel_id=1, source_target_pairs={{0,1},{1,0},{2,3},{3,2},{4,5},{5,4},{6,7},{7,6},{8,9},{9,8},{10,11... | collective-permute-start | bytes 1572872 | tf_op jit(solution)/shard_map/ppermute | solution.py:29
  8.8 18.8 %collective-permute-start.1 = (bf16[128,2048]{1,0:T(8,128)(2,1)}, bf16[128,2048]{1,0:T(8,128)(2,1)}, u32[]{:S(2)}, u32[]{:S(2)}) collective-permute-start(bf16[128,2048]{1,0:T(8,128)(2,1)} %get-tuple-element.120), channel_id=1, source_target_pairs={{0,2},{1,3},{2,0},{3,1},{4,6},{5,7},{6,4},{7,5},{8,10},{9,11},{10,... | collective-permute-start | bytes 1572872 | tf_op jit(solution)/shard_map/ppermute | solution.py:29
  8.9 31.6 %collective-permute-start.5 = (bf16[512,768]{1,0:T(8,128)(2,1)}, bf16[512,768]{1,0:T(8,128)(2,1)}, u32[]{:S(2)}, u32[]{:S(2)}) collective-permute-start(bf16[512,768]{1,0:T(8,128)(2,1)} %get-tuple-element.117), channel_id=1, source_target_pairs={{0,6},{1,7},{2,4},{3,5},{4,2},{5,3},{6,0},{7,1},{8,14},{9,15},{10,... | collective-permute-start | bytes 2359304 | tf_op jit(solution)/shard_map/ppermute | solution.py:29
  10.0 25.2 %collective-permute-start.4 = (bf16[128,2048]{1,0:T(8,128)(2,1)}, bf16[128,2048]{1,0:T(8,128)(2,1)}, u32[]{:S(2)}, u32[]{:S(2)}) collective-permute-start(bf16[128,2048]{1,0:T(8,128)(2,1)} %get-tuple-element.119), channel_id=1, source_target_pairs={{0,2},{1,3},{2,0},{3,1},{4,6},{5,7},{6,4},{7,5},{8,10},{9,11},{10,... | collective-permute-start | bytes 1572872 | tf_op jit(solution)/shard_map/ppermute | solution.py:29
  20.6 15.1 %collective-permute-start = (bf16[128,2048]{1,0:T(8,128)(2,1)}, bf16[128,2048]{1,0:T(8,128)(2,1)S(1)}, u32[]{:S(2)}, u32[]{:S(2)}) collective-permute-start(bf16[128,2048]{1,0:T(8,128)(2,1)} %get-tuple-element.120), channel_id=1, source_target_pairs={{0,1},{1,0},{2,3},{3,2},{4,5},{5,4},{6,7},{7,6},{8,9},{9,8},{10,11... | collective-permute-start | bytes 1572872 | tf_op jit(solution)/shard_map/ppermute | solution.py:29
  27.5 17.0 %collective-permute-start.7 = (bf16[128,2048]{1,0:T(8,128)(2,1)S(1)}, bf16[128,2048]{1,0:T(8,128)(2,1)S(1)}, u32[]{:S(2)}, u32[]{:S(2)}) collective-permute-start(bf16[128,2048]{1,0:T(8,128)(2,1)S(1)} %copy-done.4), channel_id=1, source_target_pairs={{0,2},{1,3},{2,0},{3,1},{4,6},{5,7},{6,4},{7,5},{8,10},{9,11},{10,... | collective-permute-start | bytes 1572872 | tf_op jit(solution)/shard_map/ppermute | solution.py:29
  27.8 17.1 %collective-permute-start.6 = (bf16[128,2048]{1,0:T(8,128)(2,1)}, bf16[128,2048]{1,0:T(8,128)(2,1)S(1)}, u32[]{:S(2)}, u32[]{:S(2)}) collective-permute-start(bf16[128,2048]{1,0:T(8,128)(2,1)} %collective-permute-done.1.refs_4_.refs_5_), channel_id=1, source_target_pairs={{0,1},{1,0},{2,3},{3,2},{4,5},{5,4},{6,7},{7,6},{8,9},{9,8},{10,11... | collective-permute-start | bytes 1572872 | tf_op jit(solution)/shard_map/ppermute | solution.py:29
  35.2 11.6 %collective-permute-start.8 = (bf16[512,768]{1,0:T(8,128)(2,1)}, bf16[512,768]{1,0:T(8,128)(2,1)S(1)}, u32[]{:S(2)}, u32[]{:S(2)}) collective-permute-start(bf16[512,768]{1,0:T(8,128)(2,1)} %collective-permute-done.3.refs_9_), channel_id=1, source_target_pairs={{0,8},{1,9},{2,10},{3,11},{4,12},{5,13},{6,14},{7,15},{8,0},{9,1},... | collective-permute-start | bytes 2359304 | tf_op jit(solution)/shard_map/ppermute | solution.py:29
  44.8 2.5 %collective-permute-start.9 = (bf16[512,768]{1,0:T(8,128)(2,1)}, bf16[512,768]{1,0:T(8,128)(2,1)S(1)}, u32[]{:S(2)}, u32[]{:S(2)}) collective-permute-start(bf16[512,768]{1,0:T(8,128)(2,1)} %collective-permute-done.5.refs_10_), channel_id=1, source_target_pairs={{0,8},{1,9},{2,10},{3,11},{4,12},{5,13},{6,14},{7,15},{8,0},{9,1},... | collective-permute-start | bytes 2359304 | tf_op jit(solution)/shard_map/ppermute | solution.py:29
  56.0 7.1 %collective-permute-start.10 = (bf16[4,64,256]{2,1,0:T(8,128)(2,1)}, bf16[4,64,256]{2,1,0:T(8,128)(2,1)}, u32[]{:S(2)}, u32[]{:S(2)}) collective-permute-start(bf16[4,64,256]{2,1,0:T(8,128)(2,1)} %get-tuple-element.70), channel_id=1, source_target_pairs={{0,6},{1,7},{2,4},{3,5},{4,2},{5,3},{6,0},{7,1},{8,14},{9,15},{10,... | collective-permute-start | bytes 393224 | tf_op jit(solution)/shard_map/ppermute | solution.py:29
  63.0 1.7 %collective-permute-start.12 = (bf16[4,64,256]{2,1,0:T(8,128)(2,1)}, bf16[4,64,256]{2,1,0:T(8,128)(2,1)S(1)}, u32[]{:S(2)}, u32[]{:S(2)}) collective-permute-start(bf16[4,64,256]{2,1,0:T(8,128)(2,1)} %collective-permute-done.10), channel_id=1, source_target_pairs={{0,8},{1,9},{2,10},{3,11},{4,12},{5,13},{6,14},{7,15},{8,0},{9,1},... | collective-permute-start | bytes 393224 | tf_op jit(solution)/shard_map/ppermute | solution.py:29
  64.9 7.6 %collective-permute-start.13 = (bf16[2,128,256]{2,1,0:T(8,128)(2,1)S(1)}, bf16[2,128,256]{2,1,0:T(8,128)(2,1)S(1)}, u32[]{:S(2)}, u32[]{:S(2)}) collective-permute-start(bf16[2,128,256]{2,1,0:T(8,128)(2,1)S(1)} %pad_maximum_fusion.3), channel_id=1, source_target_pairs={{0,16},{1,17},{2,18},{3,19},{4,20},{5,21},{6,22},{7,23},{8,24},{9,... | collective-permute-start | bytes 393224 | tf_op jit(solution)/shard_map/ppermute | solution.py:29
  68.5 7.0 %collective-permute-start.15 = (bf16[4,64,256]{2,1,0:T(8,128)(2,1)S(1)}, bf16[4,64,256]{2,1,0:T(8,128)(2,1)S(1)}, u32[]{:S(2)}, u32[]{:S(2)}) collective-permute-start(bf16[4,64,256]{2,1,0:T(8,128)(2,1)S(1)} %copy-done.7), channel_id=1, source_target_pairs={{0,6},{1,7},{2,4},{3,5},{4,2},{5,3},{6,0},{7,1},{8,14},{9,15},{10,... | collective-permute-start | bytes 393224 | tf_op jit(solution)/shard_map/ppermute | solution.py:29
  72.5 5.6 %collective-permute-start.14 = (bf16[2,128,256]{2,1,0:T(8,128)(2,1)S(1)}, bf16[2,128,256]{2,1,0:T(8,128)(2,1)S(1)}, u32[]{:S(2)}, u32[]{:S(2)}) collective-permute-start(bf16[2,128,256]{2,1,0:T(8,128)(2,1)S(1)} %constant_dynamic-update-slice_fusion), channel_id=1, source_target_pairs={{0,32},{1,33},{2,34},{3,35},{4,36},{5,37},{6,38},{7,39},{8,40},{9,... | collective-permute-start | bytes 393224 | tf_op jit(solution)/shard_map/ppermute | solution.py:29
  74.1 9.1 %collective-permute-start.17 = (bf16[4,256,128]{2,1,0:T(8,128)(2,1)S(1)}, bf16[4,256,128]{2,1,0:T(8,128)(2,1)S(1)}, u32[]{:S(2)}, u32[]{:S(2)}) collective-permute-start(bf16[4,256,128]{2,1,0:T(8,128)(2,1)S(1)} %get-tuple-element.105), channel_id=1, source_target_pairs={{0,1},{1,0},{2,3},{3,2},{4,5},{5,4},{6,7},{7,6},{8,9},{9,8},{10,11... | collective-permute-start | bytes 786440 | tf_op jit(solution)/shard_map/ppermute | solution.py:29
  75.4 8.2 %collective-permute-start.18 = (bf16[4,256,128]{2,1,0:T(8,128)(2,1)S(1)}, bf16[4,256,128]{2,1,0:T(8,128)(2,1)S(1)}, u32[]{:S(2)}, u32[]{:S(2)}) collective-permute-start(bf16[4,256,128]{2,1,0:T(8,128)(2,1)S(1)} %get-tuple-element.106), channel_id=1, source_target_pairs={{0,2},{1,3},{2,0},{3,1},{4,6},{5,7},{6,4},{7,5},{8,10},{9,11},{10,... | collective-permute-start | bytes 786440 | tf_op jit(solution)/shard_map/ppermute | solution.py:29
  78.1 6.6 %collective-permute-start.16 = (bf16[2,128,256]{2,1,0:T(8,128)(2,1)S(1)}, bf16[2,128,256]{2,1,0:T(8,128)(2,1)S(1)}, u32[]{:S(2)}, u32[]{:S(2)}) collective-permute-start(bf16[2,128,256]{2,1,0:T(8,128)(2,1)S(1)} %constant_dynamic-update-slice_fusion.8), channel_id=1, source_target_pairs={{0,64},{1,65},{2,66},{3,67},{4,68},{5,69},{6,70},{7,71},{8,72},{9,... | collective-permute-start | bytes 393224 | tf_op jit(solution)/shard_map/ppermute | solution.py:29
  81.0 10.8 %collective-permute-start.19 = (bf16[4,256,128]{2,1,0:T(8,128)(2,1)S(1)}, bf16[4,256,128]{2,1,0:T(8,128)(2,1)S(1)}, u32[]{:S(2)}, u32[]{:S(2)}) collective-permute-start(bf16[4,256,128]{2,1,0:T(8,128)(2,1)S(1)} %get-tuple-element.109), channel_id=1, source_target_pairs={{0,3},{1,2},{2,1},{3,0},{4,7},{5,6},{6,5},{7,4},{8,11},{9,10},{10,... | collective-permute-start | bytes 786440 | tf_op jit(solution)/shard_map/ppermute | solution.py:29
  83.1 1.6 %collective-permute-start.20 = (bf16[2,128,256]{2,1,0:T(8,128)(2,1)S(1)}, bf16[2,128,256]{2,1,0:T(8,128)(2,1)S(1)}, u32[]{:S(2)}, u32[]{:S(2)}) collective-permute-start(bf16[2,128,256]{2,1,0:T(8,128)(2,1)S(1)} %collective-permute-done.13.mine5), channel_id=1, source_target_pairs={{0,8},{1,9},{2,10},{3,11},{4,12},{5,13},{6,14},{7,15},{8,0},{9,1},... | collective-permute-start | bytes 393224 | tf_op jit(solution)/shard_map/ppermute | solution.py:29
  83.1 1.6 %collective-permute-start.21 = (bf16[2,128,256]{2,1,0:T(8,128)(2,1)S(1)}, bf16[2,128,256]{2,1,0:T(8,128)(2,1)S(1)}, u32[]{:S(2)}, u32[]{:S(2)}) collective-permute-start(bf16[2,128,256]{2,1,0:T(8,128)(2,1)S(1)} %collective-permute-done.14.mine6), channel_id=1, source_target_pairs={{0,8},{1,9},{2,10},{3,11},{4,12},{5,13},{6,14},{7,15},{8,0},{9,1},... | collective-permute-start | bytes 393224 | tf_op jit(solution)/shard_map/ppermute | solution.py:29
  88.2 4.0 %collective-permute-start.23 = (bf16[4,32,128]{2,1,0:T(8,128)(2,1)S(1)}, bf16[4,32,128]{2,1,0:T(8,128)(2,1)S(1)}, u32[]{:S(2)}, u32[]{:S(2)}) collective-permute-start(bf16[4,32,128]{2,1,0:T(8,128)(2,1)S(1)} %get-tuple-element.114), channel_id=1, source_target_pairs={{0,1},{1,0},{2,3},{3,2},{4,5},{5,4},{6,7},{7,6},{8,9},{9,8},{10,11... | collective-permute-start | bytes 98312 | tf_op jit(solution)/shard_map/ppermute | solution.py:29
  89.0 3.9 %collective-permute-start.24 = (bf16[4,32,128]{2,1,0:T(8,128)(2,1)S(1)}, bf16[4,32,128]{2,1,0:T(8,128)(2,1)S(1)}, u32[]{:S(2)}, u32[]{:S(2)}) collective-permute-start(bf16[4,32,128]{2,1,0:T(8,128)(2,1)S(1)} %get-tuple-element.115), channel_id=1, source_target_pairs={{0,2},{1,3},{2,0},{3,1},{4,6},{5,7},{6,4},{7,5},{8,10},{9,11},{10,... | collective-permute-start | bytes 98312 | tf_op jit(solution)/shard_map/ppermute | solution.py:29
  91.0 4.8 %collective-permute-start.25 = (bf16[4,32,128]{2,1,0:T(8,128)(2,1)S(1)}, bf16[4,32,128]{2,1,0:T(8,128)(2,1)S(1)}, u32[]{:S(2)}, u32[]{:S(2)}) collective-permute-start(bf16[4,32,128]{2,1,0:T(8,128)(2,1)S(1)} %get-tuple-element.116), channel_id=1, source_target_pairs={{0,3},{1,2},{2,1},{3,0},{4,7},{5,6},{6,5},{7,4},{8,11},{9,10},{10,... | collective-permute-start | bytes 98312 | tf_op jit(solution)/shard_map/ppermute | solution.py:29
  (10 other events, 50.6 us)

commit v5 on v4

--- a/solution.py
+++ b/solution.py
@@ -88,14 +88,14 @@
     return jnp.where((row & 3) * DEEP + (row >> 2) == column, 1.0, 0.0).astype(BF)
 
 
-def spread_body(qkv_ref, deep_q_ref, low_ref, high_ref, low_sent_ref, high_sent_ref):
+def spread_body(qkv_ref, deep_q_ref, low_ref, high_ref, low_sent_ref):
     half = DROWS // 2
     for slot in range(SLOTS):
         rows = jnp.concatenate([qkv_ref[m, slot, :DEEP] for m in range(SLABS)], axis=0)
         rows = jnp.dot(interleave(), rows, preferred_element_type=F32).astype(BF)
         deep_q_ref[slot] = rows[:, :DH]
         low_ref[slot], high_ref[slot] = rows[:half, DH:], rows[half:, DH:]
-        low_sent_ref[slot ^ 2], high_sent_ref[slot ^ 2] = rows[:half, DH:], rows[half:, DH:]
+        low_sent_ref[slot ^ 2] = rows[:half, DH:]
 
 
 def project(place, offsets, xs, ws, groups, first_slot, carried, last_deep):
@@ -106,16 +106,16 @@
     if last_deep:
         out_shape += [
             jax.ShapeDtypeStruct((SLOTS, DROWS, DH), BF),
-        ] + [jax.ShapeDtypeStruct((SLOTS, DROWS // 2, 2 * DH), BF) for _ in range(4)]
+        ] + [jax.ShapeDtypeStruct((SLOTS, DROWS // 2, 2 * DH), BF) for _ in range(3)]
     extra = [] if carried is None else [carried]
 
     def body(*refs):
         if not last_deep:
             project_body(groups, len(xs), len(ws), first_slot, 0, *refs)
             return
-        *front, qkv_ref, deep_q_ref, low, high, low_sent, high_sent, orders = refs
+        *front, qkv_ref, deep_q_ref, low, high, low_sent, orders = refs
         project_body(groups, len(xs), len(ws), first_slot, 0, *front, qkv_ref, orders)
-        spread_body(qkv_ref, deep_q_ref, low, high, low_sent, high_sent)
+        spread_body(qkv_ref, deep_q_ref, low, high, low_sent)
 
     slabs = sum(len(members) for members in groups)
     depth, width = xs[0].shape[1], ws[0].shape[1]
@@ -232,7 +232,10 @@
 
 def join(state, scores, counts, values):
     old_top, old_total, old_mixed = state
-    masked = [jnp.where(count > 0, score, LOW) for score, count in zip(scores, counts)]
+    masked = [
+        score if count is None else jnp.where(count > 0, score, LOW)
+        for score, count in zip(scores, counts)
+    ]
     top = old_top
     for score in masked:
         top = jnp.maximum(top, jnp.max(score, axis=1, keepdims=True))
@@ -244,21 +247,25 @@
     return top, total, mixed
 
 
-def middle_body(q_ref, near_ref, own_ref, other_ref, core_ref, done_ref, state_ref):
+def middle_body(q_ref, near_ref, *refs):
+    key_refs, done_ref, state_ref = refs[:6], refs[6], refs[7]
+    half = DROWS // 2
+    counts = [count_of(DROWS, 1, half, 3)] * 2 + [None] * 2 + [count_of(DROWS, 1, half, 4)] * 2
     for slot in range(SLOTS):
         state = tuple(near_ref[slot, part] for part in range(3))
         state = (state[0][:, :1], state[1][:, :1], state[2])
-        keys = [own_ref[slot, :, :DH], other_ref[slot, :, :DH], core_ref[slot, :, :DH]]
-        values = [own_ref[slot, :, DH:], other_ref[slot, :, DH:], core_ref[slot, :, DH:]]
-        scores = [scores_of(q_ref[slot], key) for key in keys]
-        counts = [count_of(DROWS, 1, DROWS, 3), count_of(DROWS, 1, DROWS, 3), count_of(DROWS, 2, 64, 4)]
-        top, total, mixed = join(state, scores, counts, values)
+        keys = [jnp.concatenate([ref[slot] for ref in key_refs[k : k + 2]], axis=0) for k in (0, 2, 4)]
+        pairs = [
+            None if counts[k] is None else jnp.concatenate(counts[k : k + 2], axis=1) for k in (0, 2, 4)
+        ]
+        scores = [scores_of(q_ref[slot], key[:, :DH]) for key in keys]
+        top, total, mixed = join(state, scores, pairs, [key[:, DH:] for key in keys])
         done_ref[slot] = mixed[DEEP:] / total[DEEP:]
         for part, value in enumerate((top, total, mixed)):
             state_ref[slot, part] = jnp.broadcast_to(value[:DEEP], (DEEP, DH))
 
 
-def middle(deep_q, state, own, other, core):
+def middle(deep_q, state, keys):
     whole = pl.BlockSpec(memory_space=pltpu.VMEM)
     return pl.pallas_call(
         middle_body,
@@ -266,7 +273,7 @@
             jax.ShapeDtypeStruct((SLOTS, DROWS - DEEP, DH), F32),
             jax.ShapeDtypeStruct((SLOTS, 3, DEEP, DH), F32),
         ),
-        in_specs=[whole] * 5,
+        in_specs=[whole] * (2 + len(keys)),
         out_specs=[whole] * 2,
         compiler_params=pltpu.CompilerParams(vmem_limit_bytes=VMEM_BYTES),
         cost_estimate=pl.CostEstimate(
@@ -275,7 +282,7 @@
             transcendentals=SLOTS * DROWS * 3 * DROWS,
         ),
         name="middle",
-    )(deep_q, state, own, other, core)
+    )(deep_q, state, *keys)
 
 
 def far_body(place_ref, q_ref, state_ref, done_ref, mine5, mine6, mine7, their5, their6, their7, *rest):
@@ -385,7 +392,7 @@
     slabs = [d_upper, d_lower]
     (qkv,) = project(place, offsets, slabs, [qkv_weight], [[(3, (0, 1))]], 0, qkv, False)
     slabs = [tokens, z_upper, z_lower, y_upper, y_lower, d_upper, d_lower]
-    qkv, deep_q, low, high, low_sent, high_sent = project(
+    qkv, deep_q, low, high, low_sent = project(
         place,
         offsets,
         slabs,
@@ -401,11 +408,11 @@
     low, low_other, found = lax.optimization_barrier((low, low_other, found))
     low_core = flipped(low, 1, 0)
     low_both = flipped(low_other, 1, 0)
-    other4 = jnp.concatenate([low_core, low_both], axis=1)
-    other4, found, high_sent = lax.optimization_barrier((other4, found, high_sent))
-    high_other = flipped(high_sent, 0, 6)
+    low_both, found, high = lax.optimization_barrier((low_both, found, high))
+    high_other = flipped(jnp.concatenate([high[2:], high[:2]], axis=0), 0, 6)
     kept = jnp.concatenate([half_slots(low, core), half_slots(low_other, core)], axis=1)
-    other, pieces = half_slots(other4, core), 2
+    other = jnp.concatenate([half_slots(low_core, core), half_slots(low_both, core)], axis=1)
+    pieces = 2
     mine, their = [], []
     for level in range(1, 4):
         kept = jnp.concatenate(halves(kept, pieces) + halves(other, pieces), axis=1)
@@ -415,9 +422,8 @@
             kept, bulk, state = lax.optimization_barrier((kept, bulk, state))
         if level == 3:
             bulk = [bulk[0]] + [flipped(bulk[m], 0, m) for m in range(1, SLABS)]
-            deep_kv = jnp.concatenate([low, high], axis=1)
-            other3 = jnp.concatenate([low_other, high_other], axis=1)
-            done, state = middle(deep_q, state, deep_kv, other3, other4)
+            keys = (low, low_other, high, high_other, low_core, low_both)
+            done, state = middle(deep_q, state, keys)
             kept, done, state = lax.optimization_barrier((kept, done, state))
         other = flipped(kept, 1 << level, 0)
         if level == 3:

time: 98.3 us -> 98.6 us (level)
    unnamed x38 -> x34, local copies, waits for them, and re-layouts: 3.84 us -> 3.19 us
  transfers between devices with their start and end apart: 26 -> 26, of which waited for: 15 -> 16; matrix products, arithmetic and copies ran while one was open for 3% -> 1% of each run, Pallas kernels for 19% -> 20%
where the time goes in v5:
time: 98.6 us; the launch traced here: 98.3 us
  waiting for transfers between devices  33.7 us (34%)
  Pallas kernels  29.4 us (30%)
  starting transfers between devices  26.9 us (27%)
  local copies, waits for them, and re-layouts  6.98 us (7%)
  other arithmetic  1.01 us (1%)
    ppermute x26, waiting for transfers between devices, flipped(): lax.ppermute(value, ('outer', 'inner'), [(f, f ^ mask) for f in range(cou...  33.7 us
    ppermute x26, starting transfers between devices, flipped(): lax.ppermute(value, ('outer', 'inner'), [(f, f ^ mask) for f in range(cou...  26.9 us
    pallas_call x4, Pallas kernels, project(): pl.pallas_call(body, out_shape=out_shape, in_specs=[scalars, scalars] + [...  15.7 us
    pallas_call x2, Pallas kernels, near(): pl.pallas_call(lambda *refs: near_body(base, heads, len(carried), *refs),...  6.95 us
    unnamed x34, local copies, waits for them, and re-layouts  3.19 us
    dynamic_slice x1, local copies, waits for them, and re-layouts, shards(): lax.dynamic_slice(qkv_weight, ((2 * core + k) * chunk, 0), (chunk, width))  2.7 us
    pallas_call x1, Pallas kernels, middle(): pl.pallas_call(middle_body, out_shape=(jax.ShapeDtypeStruct((SLOTS, DROWS...  2.53 us
    pallas_call x1, Pallas kernels, far(): pl.pallas_call(far_body, out_shape=tuple((jax.ShapeDtypeStruct((SLOTS, DE...  2.16 us
  transfers between devices with their start and end apart: 26, of which 16 were waited for; matrix products, arithmetic and copies ran while one was open for 1% of the time, Pallas kernels for 20%

profile of v5, /device:TPU:0, one launch (start us, length us, event | category | flops | bytes accessed | tf_op | source)
XLA Modules:
  0.0 98.3 jit_solution(6863778357459404632)
XLA Ops:
  0.0 2.7 %constant_dynamic-slice_fusion = (bf16[512,768]{1,0:T(8,128)(2,1)}, bf16[512,768]{1,0:T(8,128)(2,1)}) fusion(bf16[2048,768]{1,0:T(8,128)(2,1)} %refs_4_.1, s32[]{:T(128)S(6)} %select_n.28, s32[]{:T(128)S(6)} %select_n.27), kind=kLoop, calls=%fused_computation.31 | loop fusion | bytes 3145736 | tf_op jit(solution)/shard_map/dynamic_slice | solution.py:376
  2.7 3.1 %collective-permute-start.3 = (bf16[512,768]{1,0:T(8,128)(2,1)}, bf16[512,768]{1,0:T(8,128)(2,1)}, u32[]{:S(2)}, u32[]{:S(2)}) collective-permute-start(bf16[512,768]{1,0:T(8,128)(2,1)} %get-tuple-element.116), channel_id=1, source_target_pairs={{0,6},{1,7},{2,4},{3,5},{4,2},{5,3},{6,0},{7,1},{8,14},{9,15},{10,... | collective-permute-start | bytes 2359304 | tf_op jit(solution)/shard_map/ppermute | solution.py:29
  6.9 1.9 %collective-permute-start.2 = (bf16[128,2048]{1,0:T(8,128)(2,1)}, bf16[128,2048]{1,0:T(8,128)(2,1)S(1)}, u32[]{:S(2)}, u32[]{:S(2)}) collective-permute-start(bf16[128,2048]{1,0:T(8,128)(2,1)} %get-tuple-element.117), channel_id=1, source_target_pairs={{0,1},{1,0},{2,3},{3,2},{4,5},{5,4},{6,7},{7,6},{8,9},{9,8},{10,11... | collective-permute-start | bytes 1572872 | tf_op jit(solution)/shard_map/ppermute | solution.py:29
  10.8 9.8 %collective-permute-done.2.refs_3_.refs_4_ = bf16[128,2048]{1,0:T(8,128)(2,1)S(1)} collective-permute-done((bf16[128,2048]{1,0:T(8,128)(2,1)}, bf16[128,2048]{1,0:T(8,128)(2,1)S(1)}, u32[]{:S(2)}, u32[]{:S(2)}) %collective-permute-start.2) | collective-permute-done | bytes 524320 | tf_op jit(solution)/shard_map/ppermute | solution.py:29
  20.6 1.7 %collective-permute-start = (bf16[128,2048]{1,0:T(8,128)(2,1)}, bf16[128,2048]{1,0:T(8,128)(2,1)S(1)}, u32[]{:S(2)}, u32[]{:S(2)}) collective-permute-start(bf16[128,2048]{1,0:T(8,128)(2,1)} %get-tuple-element.118), channel_id=1, source_target_pairs={{0,1},{1,0},{2,3},{3,2},{4,5},{5,4},{6,7},{7,6},{8,9},{9,8},{10,11... | collective-permute-start | bytes 1572872 | tf_op jit(solution)/shard_map/ppermute | solution.py:29
  22.5 1.9 %copy-done = bf16[2048,768]{1,0:T(8,128)(2,1)S(1)} copy-done((bf16[2048,768]{1,0:T(8,128)(2,1)S(1)}, bf16[2048,768]{1,0:T(8,128)(2,1)}, u32[]{:S(2)}) %copy-start) | copy-done | bytes 3145752
  25.6 1.9 %project.4.refs_7_ = bf16[4,4,256,384]{3,2,1,0:T(8,128)(2,1)S(1)} custom-call(s32[2]{0:T(128)S(1)} %pad_add_fusion.refs_0_.place_ref, s32[16]{0:T(128)S(1)} %copy-done.5, bf16[256,2048]{1,0:T(8,128)(2,1)S(1)} %copy-done.2, bf16[2048,768]{1,0:T(8,128)(2,1)S(1)} %copy-done), custom_call_target="tpu_custom_call" | custom-call | flops 905969664 | bytes 4194304 | tf_op jit(solution)/shard_map/project/pallas_call | solution.py:122
  28.6 6.6 %collective-permute-done.4.refs_5_.refs_6_ = bf16[128,2048]{1,0:T(8,128)(2,1)} collective-permute-done((bf16[128,2048]{1,0:T(8,128)(2,1)}, bf16[128,2048]{1,0:T(8,128)(2,1)}, u32[]{:S(2)}, u32[]{:S(2)}) %collective-permute-start.4) | collective-permute-done | bytes 524320 | tf_op jit(solution)/shard_map/ppermute | solution.py:29
  35.7 3.8 %project.5.refs_5_ = bf16[4,4,256,384]{3,2,1,0:T(8,128)(2,1)S(1)} custom-call(s32[2]{0:T(128)S(1)} %pad_add_fusion.refs_0_.place_ref, s32[16]{0:T(128)S(1)} %copy-done.5, bf16[128,2048]{1,0:T(8,128)(2,1)S(1)} %collective-permute-done.refs_2_.refs_3_, bf16[128,2048]{1,0:T(8,128)(2,1)S(1)} %copy-done.4, ...), custom_call_target="tpu_custom_call", output_to_operand_aliasing={{}: (7, {})} | custom-call | flops 1811939328 | bytes 5242880 | tf_op jit(solution)/shard_map/project/pallas_call | solution.py:122
  40.5 4.0 %collective-permute-done.7.refs_3_.refs_8_ = bf16[128,2048]{1,0:T(8,128)(2,1)S(1)} collective-permute-done((bf16[128,2048]{1,0:T(8,128)(2,1)S(1)}, bf16[128,2048]{1,0:T(8,128)(2,1)S(1)}, u32[]{:S(2)}, u32[]{:S(2)}) %collective-permute-start.7) | collective-permute-done | bytes 524320 | tf_op jit(solution)/shard_map/ppermute | solution.py:29
  44.8 1.9 %project.6.refs_13_ = bf16[4,4,256,384]{3,2,1,0:T(8,128)(2,1)S(1)} custom-call(s32[2]{0:T(128)S(1)} %pad_add_fusion.refs_0_.place_ref, s32[16]{0:T(128)S(1)} %copy-done.5, bf16[128,2048]{1,0:T(8,128)(2,1)S(1)} %collective-permute-done.6.refs_2_.refs_7_, bf16[128,2048]{1,0:T(8,128)(2,1)S(1)} %collective-permute-done.7.refs_3_.refs_8_, ...), custom_call_target="tpu_custom_call", output_to_operand_aliasing={{}: (5, {})} | custom-call | flops 905969664 | bytes 4194304 | tf_op jit(solution)/shard_map/project/pallas_call | solution.py:122
  47.3 8.0 %project.7 = (bf16[4,4,256,384]{3,2,1,0:T(8,128)(2,1)S(1)}, bf16[4,128,128]{2,1,0:T(8,128)(2,1)S(1)}, bf16[4,64,256]{2,1,0:T(8,128)(2,1)S(1)}, bf16[4,64,256]{2,1,0:T(8,128)(2,1)S(1)}, bf16[4,64,256]{2,1,0:T(8,128)(2,1)}) custom-call(s32[2]{0:T(128)S(1)} %pad_add_fusion.refs_0_.place_ref, s32[16]{0:T(128)S(1)} %copy-done.5, ...), custom_call_target="tpu_custom_call", output_to_operand_aliasing={{0}: (13, {})} | custom-call | flops 3623878656 | bytes 7340032 | tf_op jit(solution)/shard_map/project/pallas_call | solution.py:122
  55.8 3.5 %near.2 = (bf16[4,256,128]{2,1,0:T(8,128)(2,1)S(1)}, bf16[4,256,128]{2,1,0:T(8,128)(2,1)S(1)}, bf16[4,256,128]{2,1,0:T(8,128)(2,1)S(1)}, bf16[4,256,128]{2,1,0:T(8,128)(2,1)S(1)}, f32[4,3,128,128]{3,2,1,0:T(8,128)S(1)}) custom-call(s32[2]{0:T(128)S(1)} %pad_add_fusion.refs_0_.place_ref, s32[16]{0:T(128)S(1)} %copy-done.5, ...), custom_call_target="tpu_custom_call" | custom-call | flops 469762048 | bytes 2097152 | tf_op jit(solution)/shard_map/near/pallas_call | solution.py:203
  59.3 3.1 %collective-permute-done.10.refs_1_ = bf16[4,64,256]{2,1,0:T(8,128)(2,1)} collective-permute-done((bf16[4,64,256]{2,1,0:T(8,128)(2,1)}, bf16[4,64,256]{2,1,0:T(8,128)(2,1)}, u32[]{:S(2)}, u32[]{:S(2)}) %collective-permute-start.10) | collective-permute-done | bytes 131104 | tf_op jit(solution)/shard_map/ppermute | solution.py:29
  65.2 3.6 %collective-permute-start.13 = (bf16[2,128,256]{2,1,0:T(8,128)(2,1)S(1)}, bf16[2,128,256]{2,1,0:T(8,128)(2,1)S(1)}, u32[]{:S(2)}, u32[]{:S(2)}) collective-permute-start(bf16[2,128,256]{2,1,0:T(8,128)(2,1)S(1)} %pad_maximum_fusion), channel_id=1, source_target_pairs={{0,16},{1,17},{2,18},{3,19},{4,20},{5,21},{6,22},{7,23},{8,24},{9,... | collective-permute-start | bytes 393224 | tf_op jit(solution)/shard_map/ppermute | solution.py:29
  69.2 3.5 %near.3 = (bf16[4,256,128]{2,1,0:T(8,128)(2,1)S(1)}, bf16[4,256,128]{2,1,0:T(8,128)(2,1)S(1)}, bf16[4,256,128]{2,1,0:T(8,128)(2,1)S(1)}, bf16[4,256,128]{2,1,0:T(8,128)(2,1)S(1)}, f32[4,3,128,128]{3,2,1,0:T(8,128)S(1)}) custom-call(s32[2]{0:T(128)S(1)} %pad_add_fusion.refs_0_.place_ref, ...), custom_call_target="tpu_custom_call", output_to_operand_aliasing={{0}: (3, {}), {1}: (4, {}), {2}: (5, {}), {3}: (6, {}), {4}... | custom-call | flops 469762048 | bytes 2097152 | tf_op jit(solution)/shard_map/near/pallas_call | solution.py:203
  72.8 1.6 %collective-permute-start.14 = (bf16[2,128,256]{2,1,0:T(8,128)(2,1)S(1)}, bf16[2,128,256]{2,1,0:T(8,128)(2,1)S(1)}, u32[]{:S(2)}, u32[]{:S(2)}) collective-permute-start(bf16[2,128,256]{2,1,0:T(8,128)(2,1)S(1)} %constant_dynamic-update-slice_fusion), channel_id=1, source_target_pairs={{0,32},{1,33},{2,34},{3,35},{4,36},{5,37},{6,38},{7,39},{8,40},{9,... | collective-permute-start | bytes 393224 | tf_op jit(solution)/shard_map/ppermute | solution.py:29
  75.8 2.5 %middle.1 = (f32[4,96,128]{2,1,0:T(8,128)S(1)}, f32[4,3,32,128]{3,2,1,0:T(8,128)S(1)}) custom-call(bf16[4,128,128]{2,1,0:T(8,128)(2,1)S(1)} %get-tuple-element.97.q_ref, f32[4,3,128,128]{3,2,1,0:T(8,128)S(1)} %get-tuple-element.98.near_ref, bf16[4,64,256]{2,1,0:T(8,128)(2,1)S(1)} %get-tuple-element.76.refs_0_, ...), custom_call_target="tpu_custom_call" | custom-call | flops 100663296 | bytes 1310720 | tf_op jit(solution)/shard_map/middle/pallas_call | solution.py:270
  78.4 2.9 %collective-permute-start.16 = (bf16[2,128,256]{2,1,0:T(8,128)(2,1)S(1)}, bf16[2,128,256]{2,1,0:T(8,128)(2,1)S(1)}, u32[]{:S(2)}, u32[]{:S(2)}) collective-permute-start(bf16[2,128,256]{2,1,0:T(8,128)(2,1)S(1)} %constant_dynamic-update-slice_fusion.8), channel_id=1, source_target_pairs={{0,64},{1,65},{2,66},{3,67},{4,68},{5,69},{6,70},{7,71},{8,72},{9,... | collective-permute-start | bytes 393224 | tf_op jit(solution)/shard_map/ppermute | solution.py:29
  81.3 2.1 %collective-permute-start.19 = (bf16[4,256,128]{2,1,0:T(8,128)(2,1)S(1)}, bf16[4,256,128]{2,1,0:T(8,128)(2,1)S(1)}, u32[]{:S(2)}, u32[]{:S(2)}) collective-permute-start(bf16[4,256,128]{2,1,0:T(8,128)(2,1)S(1)} %get-tuple-element.107), channel_id=1, source_target_pairs={{0,3},{1,2},{2,1},{3,0},{4,7},{5,6},{6,5},{7,4},{8,11},{9,10},{10,... | collective-permute-start | bytes 786440 | tf_op jit(solution)/shard_map/ppermute | solution.py:29
  86.3 2.2 %far.1 = (bf16[4,32,128]{2,1,0:T(8,128)(2,1)S(1)}, bf16[4,32,128]{2,1,0:T(8,128)(2,1)S(1)}, bf16[4,32,128]{2,1,0:T(8,128)(2,1)S(1)}, bf16[4,32,128]{2,1,0:T(8,128)(2,1)S(1)}) custom-call(s32[2]{0:T(128)S(1)} %pad_add_fusion.refs_0_.place_ref, bf16[4,128,128]{2,1,0:T(8,128)(2,1)S(1)} %get-tuple-element.97.q_ref, ...), custom_call_target="tpu_custom_call" | custom-call | flops 25165824 | bytes 1048576 | tf_op jit(solution)/shard_map/far/pallas_call | solution.py:310
  89.4 2.0 %collective-permute-start.24 = (bf16[4,32,128]{2,1,0:T(8,128)(2,1)S(1)}, bf16[4,32,128]{2,1,0:T(8,128)(2,1)S(1)}, u32[]{:S(2)}, u32[]{:S(2)}) collective-permute-start(bf16[4,32,128]{2,1,0:T(8,128)(2,1)S(1)} %get-tuple-element.113), channel_id=1, source_target_pairs={{0,2},{1,3},{2,0},{3,1},{4,6},{5,7},{6,4},{7,5},{8,10},{9,11},{10,... | collective-permute-start | bytes 98312 | tf_op jit(solution)/shard_map/ppermute | solution.py:29
  93.3 2.9 %collective-permute-done.25.refs_7_ = bf16[4,32,128]{2,1,0:T(8,128)(2,1)S(1)} collective-permute-done((bf16[4,32,128]{2,1,0:T(8,128)(2,1)S(1)}, bf16[4,32,128]{2,1,0:T(8,128)(2,1)S(1)}, u32[]{:S(2)}, u32[]{:S(2)}) %collective-permute-start.25) | collective-permute-done | bytes 32800 | tf_op jit(solution)/shard_map/ppermute | solution.py:29
  96.2 2.1 %place.1 = bf16[256,2048]{1,0:T(8,128)(2,1)} custom-call(s32[2]{0:T(128)S(1)} %pad_add_fusion.refs_0_.place_ref, s32[16]{0:T(128)S(1)} %copy-done.5, bf16[4,256,128]{2,1,0:T(8,128)(2,1)S(1)} %get-tuple-element.95.refs_0_, bf16[4,256,128]{2,1,0:T(8,128)(2,1)S(1)} %collective-permute-done.17.refs_1_, bf16[4,256,128]{2,1,0:T(8,128)(2,1)S(1)} %collective-permute-done.18.refs_2_, ...), custom_call_target="tpu_custom_call" | custom-call | flops 33554432 | bytes 2097152 | tf_op jit(solution)/shard_map/place/pallas_call | solution.py:341
  (86 shorter events, 18.6 us)
Async XLA Ops:
  2.7 24.8 %collective-permute-start.3 = (bf16[512,768]{1,0:T(8,128)(2,1)}, bf16[512,768]{1,0:T(8,128)(2,1)}, u32[]{:S(2)}, u32[]{:S(2)}) collective-permute-start(bf16[512,768]{1,0:T(8,128)(2,1)} %get-tuple-element.116), channel_id=1, source_target_pairs={{0,6},{1,7},{2,4},{3,5},{4,2},{5,3},{6,0},{7,1},{8,14},{9,15},{10,... | collective-permute-start | bytes 2359304 | tf_op jit(solution)/shard_map/ppermute | solution.py:29
  6.9 13.8 %collective-permute-start.2 = (bf16[128,2048]{1,0:T(8,128)(2,1)}, bf16[128,2048]{1,0:T(8,128)(2,1)S(1)}, u32[]{:S(2)}, u32[]{:S(2)}) collective-permute-start(bf16[128,2048]{1,0:T(8,128)(2,1)} %get-tuple-element.117), channel_id=1, source_target_pairs={{0,1},{1,0},{2,3},{3,2},{4,5},{5,4},{6,7},{7,6},{8,9},{9,8},{10,11... | collective-permute-start | bytes 1572872 | tf_op jit(solution)/shard_map/ppermute | solution.py:29
  8.8 18.8 %collective-permute-start.1 = (bf16[128,2048]{1,0:T(8,128)(2,1)}, bf16[128,2048]{1,0:T(8,128)(2,1)}, u32[]{:S(2)}, u32[]{:S(2)}) collective-permute-start(bf16[128,2048]{1,0:T(8,128)(2,1)} %get-tuple-element.118), channel_id=1, source_target_pairs={{0,2},{1,3},{2,0},{3,1},{4,6},{5,7},{6,4},{7,5},{8,10},{9,11},{10,... | collective-permute-start | bytes 1572872 | tf_op jit(solution)/shard_map/ppermute | solution.py:29
  8.9 31.6 %collective-permute-start.5 = (bf16[512,768]{1,0:T(8,128)(2,1)}, bf16[512,768]{1,0:T(8,128)(2,1)}, u32[]{:S(2)}, u32[]{:S(2)}) collective-permute-start(bf16[512,768]{1,0:T(8,128)(2,1)} %get-tuple-element.115), channel_id=1, source_target_pairs={{0,6},{1,7},{2,4},{3,5},{4,2},{5,3},{6,0},{7,1},{8,14},{9,15},{10,... | collective-permute-start | bytes 2359304 | tf_op jit(solution)/shard_map/ppermute | solution.py:29
  10.0 25.2 %collective-permute-start.4 = (bf16[128,2048]{1,0:T(8,128)(2,1)}, bf16[128,2048]{1,0:T(8,128)(2,1)}, u32[]{:S(2)}, u32[]{:S(2)}) collective-permute-start(bf16[128,2048]{1,0:T(8,128)(2,1)} %get-tuple-element.117), channel_id=1, source_target_pairs={{0,2},{1,3},{2,0},{3,1},{4,6},{5,7},{6,4},{7,5},{8,10},{9,11},{10,... | collective-permute-start | bytes 1572872 | tf_op jit(solution)/shard_map/ppermute | solution.py:29
  20.6 15.1 %collective-permute-start = (bf16[128,2048]{1,0:T(8,128)(2,1)}, bf16[128,2048]{1,0:T(8,128)(2,1)S(1)}, u32[]{:S(2)}, u32[]{:S(2)}) collective-permute-start(bf16[128,2048]{1,0:T(8,128)(2,1)} %get-tuple-element.118), channel_id=1, source_target_pairs={{0,1},{1,0},{2,3},{3,2},{4,5},{5,4},{6,7},{7,6},{8,9},{9,8},{10,11... | collective-permute-start | bytes 1572872 | tf_op jit(solution)/shard_map/ppermute | solution.py:29
  27.6 17.0 %collective-permute-start.7 = (bf16[128,2048]{1,0:T(8,128)(2,1)S(1)}, bf16[128,2048]{1,0:T(8,128)(2,1)S(1)}, u32[]{:S(2)}, u32[]{:S(2)}) collective-permute-start(bf16[128,2048]{1,0:T(8,128)(2,1)S(1)} %copy-done.4), channel_id=1, source_target_pairs={{0,2},{1,3},{2,0},{3,1},{4,6},{5,7},{6,4},{7,5},{8,10},{9,11},{10,... | collective-permute-start | bytes 1572872 | tf_op jit(solution)/shard_map/ppermute | solution.py:29
  27.8 17.1 %collective-permute-start.6 = (bf16[128,2048]{1,0:T(8,128)(2,1)}, bf16[128,2048]{1,0:T(8,128)(2,1)S(1)}, u32[]{:S(2)}, u32[]{:S(2)}) collective-permute-start(bf16[128,2048]{1,0:T(8,128)(2,1)} %collective-permute-done.1.refs_4_.refs_5_), channel_id=1, source_target_pairs={{0,1},{1,0},{2,3},{3,2},{4,5},{5,4},{6,7},{7,6},{8,9},{9,8},{10,11... | collective-permute-start | bytes 1572872 | tf_op jit(solution)/shard_map/ppermute | solution.py:29
  35.2 11.6 %collective-permute-start.8 = (bf16[512,768]{1,0:T(8,128)(2,1)}, bf16[512,768]{1,0:T(8,128)(2,1)S(1)}, u32[]{:S(2)}, u32[]{:S(2)}) collective-permute-start(bf16[512,768]{1,0:T(8,128)(2,1)} %collective-permute-done.3.refs_9_), channel_id=1, source_target_pairs={{0,8},{1,9},{2,10},{3,11},{4,12},{5,13},{6,14},{7,15},{8,0},{9,1},... | collective-permute-start | bytes 2359304 | tf_op jit(solution)/shard_map/ppermute | solution.py:29
  44.8 2.5 %collective-permute-start.9 = (bf16[512,768]{1,0:T(8,128)(2,1)}, bf16[512,768]{1,0:T(8,128)(2,1)S(1)}, u32[]{:S(2)}, u32[]{:S(2)}) collective-permute-start(bf16[512,768]{1,0:T(8,128)(2,1)} %collective-permute-done.5.refs_10_), channel_id=1, source_target_pairs={{0,8},{1,9},{2,10},{3,11},{4,12},{5,13},{6,14},{7,15},{8,0},{9,1},... | collective-permute-start | bytes 2359304 | tf_op jit(solution)/shard_map/ppermute | solution.py:29
  55.3 7.1 %collective-permute-start.10 = (bf16[4,64,256]{2,1,0:T(8,128)(2,1)}, bf16[4,64,256]{2,1,0:T(8,128)(2,1)}, u32[]{:S(2)}, u32[]{:S(2)}) collective-permute-start(bf16[4,64,256]{2,1,0:T(8,128)(2,1)} %get-tuple-element.69), channel_id=1, source_target_pairs={{0,6},{1,7},{2,4},{3,5},{4,2},{5,3},{6,0},{7,1},{8,14},{9,15},{10,... | collective-permute-start | bytes 393224 | tf_op jit(solution)/shard_map/ppermute | solution.py:29
  63.4 1.7 %collective-permute-start.12 = (bf16[4,64,256]{2,1,0:T(8,128)(2,1)}, bf16[4,64,256]{2,1,0:T(8,128)(2,1)S(1)}, u32[]{:S(2)}, u32[]{:S(2)}) collective-permute-start(bf16[4,64,256]{2,1,0:T(8,128)(2,1)} %collective-permute-done.10.refs_1_), channel_id=1, source_target_pairs={{0,8},{1,9},{2,10},{3,11},{4,12},{5,13},{6,14},{7,15},{8,0},{9,1},... | collective-permute-start | bytes 393224 | tf_op jit(solution)/shard_map/ppermute | solution.py:29
  65.2 7.6 %collective-permute-start.13 = (bf16[2,128,256]{2,1,0:T(8,128)(2,1)S(1)}, bf16[2,128,256]{2,1,0:T(8,128)(2,1)S(1)}, u32[]{:S(2)}, u32[]{:S(2)}) collective-permute-start(bf16[2,128,256]{2,1,0:T(8,128)(2,1)S(1)} %pad_maximum_fusion), channel_id=1, source_target_pairs={{0,16},{1,17},{2,18},{3,19},{4,20},{5,21},{6,22},{7,23},{8,24},{9,... | collective-permute-start | bytes 393224 | tf_op jit(solution)/shard_map/ppermute | solution.py:29
  68.8 7.0 %collective-permute-start.15 = (bf16[4,64,256]{2,1,0:T(8,128)(2,1)S(1)}, bf16[4,64,256]{2,1,0:T(8,128)(2,1)S(1)}, u32[]{:S(2)}, u32[]{:S(2)}) collective-permute-start(bf16[4,64,256]{2,1,0:T(8,128)(2,1)S(1)} %pad_maximum_fusion.1), channel_id=1, source_target_pairs={{0,6},{1,7},{2,4},{3,5},{4,2},{5,3},{6,0},{7,1},{8,14},{9,15},{10,... | collective-permute-start | bytes 393224 | tf_op jit(solution)/shard_map/ppermute | solution.py:29
  72.8 5.5 %collective-permute-start.14 = (bf16[2,128,256]{2,1,0:T(8,128)(2,1)S(1)}, bf16[2,128,256]{2,1,0:T(8,128)(2,1)S(1)}, u32[]{:S(2)}, u32[]{:S(2)}) collective-permute-start(bf16[2,128,256]{2,1,0:T(8,128)(2,1)S(1)} %constant_dynamic-update-slice_fusion), channel_id=1, source_target_pairs={{0,32},{1,33},{2,34},{3,35},{4,36},{5,37},{6,38},{7,39},{8,40},{9,... | collective-permute-start | bytes 393224 | tf_op jit(solution)/shard_map/ppermute | solution.py:29
  74.4 9.0 %collective-permute-start.17 = (bf16[4,256,128]{2,1,0:T(8,128)(2,1)S(1)}, bf16[4,256,128]{2,1,0:T(8,128)(2,1)S(1)}, u32[]{:S(2)}, u32[]{:S(2)}) collective-permute-start(bf16[4,256,128]{2,1,0:T(8,128)(2,1)S(1)} %get-tuple-element.103), channel_id=1, source_target_pairs={{0,1},{1,0},{2,3},{3,2},{4,5},{5,4},{6,7},{7,6},{8,9},{9,8},{10,11... | collective-permute-start | bytes 786440 | tf_op jit(solution)/shard_map/ppermute | solution.py:29
  75.8 8.2 %collective-permute-start.18 = (bf16[4,256,128]{2,1,0:T(8,128)(2,1)S(1)}, bf16[4,256,128]{2,1,0:T(8,128)(2,1)S(1)}, u32[]{:S(2)}, u32[]{:S(2)}) collective-permute-start(bf16[4,256,128]{2,1,0:T(8,128)(2,1)S(1)} %get-tuple-element.104), channel_id=1, source_target_pairs={{0,2},{1,3},{2,0},{3,1},{4,6},{5,7},{6,4},{7,5},{8,10},{9,11},{10,... | collective-permute-start | bytes 786440 | tf_op jit(solution)/shard_map/ppermute | solution.py:29
  78.4 6.6 %collective-permute-start.16 = (bf16[2,128,256]{2,1,0:T(8,128)(2,1)S(1)}, bf16[2,128,256]{2,1,0:T(8,128)(2,1)S(1)}, u32[]{:S(2)}, u32[]{:S(2)}) collective-permute-start(bf16[2,128,256]{2,1,0:T(8,128)(2,1)S(1)} %constant_dynamic-update-slice_fusion.8), channel_id=1, source_target_pairs={{0,64},{1,65},{2,66},{3,67},{4,68},{5,69},{6,70},{7,71},{8,72},{9,... | collective-permute-start | bytes 393224 | tf_op jit(solution)/shard_map/ppermute | solution.py:29
  81.3 10.8 %collective-permute-start.19 = (bf16[4,256,128]{2,1,0:T(8,128)(2,1)S(1)}, bf16[4,256,128]{2,1,0:T(8,128)(2,1)S(1)}, u32[]{:S(2)}, u32[]{:S(2)}) collective-permute-start(bf16[4,256,128]{2,1,0:T(8,128)(2,1)S(1)} %get-tuple-element.107), channel_id=1, source_target_pairs={{0,3},{1,2},{2,1},{3,0},{4,7},{5,6},{6,5},{7,4},{8,11},{9,10},{10,... | collective-permute-start | bytes 786440 | tf_op jit(solution)/shard_map/ppermute | solution.py:29
  83.5 1.6 %collective-permute-start.20 = (bf16[2,128,256]{2,1,0:T(8,128)(2,1)S(1)}, bf16[2,128,256]{2,1,0:T(8,128)(2,1)S(1)}, u32[]{:S(2)}, u32[]{:S(2)}) collective-permute-start(bf16[2,128,256]{2,1,0:T(8,128)(2,1)S(1)} %collective-permute-done.13.mine5), channel_id=1, source_target_pairs={{0,8},{1,9},{2,10},{3,11},{4,12},{5,13},{6,14},{7,15},{8,0},{9,1},... | collective-permute-start | bytes 393224 | tf_op jit(solution)/shard_map/ppermute | solution.py:29
  83.5 1.5 %collective-permute-start.21 = (bf16[2,128,256]{2,1,0:T(8,128)(2,1)S(1)}, bf16[2,128,256]{2,1,0:T(8,128)(2,1)S(1)}, u32[]{:S(2)}, u32[]{:S(2)}) collective-permute-start(bf16[2,128,256]{2,1,0:T(8,128)(2,1)S(1)} %collective-permute-done.14.mine6), channel_id=1, source_target_pairs={{0,8},{1,9},{2,10},{3,11},{4,12},{5,13},{6,14},{7,15},{8,0},{9,1},... | collective-permute-start | bytes 393224 | tf_op jit(solution)/shard_map/ppermute | solution.py:29
  88.5 4.0 %collective-permute-start.23 = (bf16[4,32,128]{2,1,0:T(8,128)(2,1)S(1)}, bf16[4,32,128]{2,1,0:T(8,128)(2,1)S(1)}, u32[]{:S(2)}, u32[]{:S(2)}) collective-permute-start(bf16[4,32,128]{2,1,0:T(8,128)(2,1)S(1)} %get-tuple-element.112), channel_id=1, source_target_pairs={{0,1},{1,0},{2,3},{3,2},{4,5},{5,4},{6,7},{7,6},{8,9},{9,8},{10,11... | collective-permute-start | bytes 98312 | tf_op jit(solution)/shard_map/ppermute | solution.py:29
  89.4 3.9 %collective-permute-start.24 = (bf16[4,32,128]{2,1,0:T(8,128)(2,1)S(1)}, bf16[4,32,128]{2,1,0:T(8,128)(2,1)S(1)}, u32[]{:S(2)}, u32[]{:S(2)}) collective-permute-start(bf16[4,32,128]{2,1,0:T(8,128)(2,1)S(1)} %get-tuple-element.113), channel_id=1, source_target_pairs={{0,2},{1,3},{2,0},{3,1},{4,6},{5,7},{6,4},{7,5},{8,10},{9,11},{10,... | collective-permute-start | bytes 98312 | tf_op jit(solution)/shard_map/ppermute | solution.py:29
  91.3 4.8 %collective-permute-start.25 = (bf16[4,32,128]{2,1,0:T(8,128)(2,1)S(1)}, bf16[4,32,128]{2,1,0:T(8,128)(2,1)S(1)}, u32[]{:S(2)}, u32[]{:S(2)}) collective-permute-start(bf16[4,32,128]{2,1,0:T(8,128)(2,1)S(1)} %get-tuple-element.114), channel_id=1, source_target_pairs={{0,3},{1,2},{2,1},{3,0},{4,7},{5,6},{6,5},{7,4},{8,11},{9,10},{10,... | collective-permute-start | bytes 98312 | tf_op jit(solution)/shard_map/ppermute | solution.py:29
  (8 other events, 37.9 us)
